TPU v7x, 32 devices: a whole 2x2x4 slice. The times are simulated.
32 devices in a mesh: groups: 2 (over y), row: 8 (over z, x), col: 2 (over core).
Axes of the slice: x: 2, y: 2, z: 4, core: 2. Of those that a mesh axis runs over, the one named last changes fastest.
Arguments:
- features: bfloat16 [2048, 2048], P(('groups', 'row'), 'col'), parts along dimension 0, may hold values from -6 to 6
- tiles: bfloat16 [16, 8, 128, 128], P(('groups', 'row')), parts along dimension 0, may hold values from -6 to 6
- pattern: int32 [16, 8], P(('groups', 'row')), parts along dimension 0, may hold values from 0 to 7, as said below
- degrees: int32 [2048], P(('groups', 'row')), parts along dimension 0, may hold values from 16 to 63
- segments: int32 [2048], P(('groups', 'row')), parts along dimension 0, may hold values from 0 to 7, never falling along the last dimension, each value on 1 to 192 neighbouring positions
- pairs: int32 [128, 3], P('groups'), parts along dimension 0, may hold values from 0 to 15, as said below
- w_self: bfloat16 [128, 128], replicated, may hold values from -0.5 to 0.5
- w_neigh: bfloat16 [128, 128], replicated, may hold values from -0.5 to 0.5
- bias: float32 [128], replicated, may hold values from -3 to 3
- w_out: float32 [128], replicated, may hold values from -0.5 to 0.5
Outputs:
- loss: float32 [2], P('groups'), parts along dimension 0
- grad_self: float32 [256, 128], P('groups'), parts along dimension 0
- grad_neigh: float32 [256, 128], P('groups'), parts along dimension 0
- grad_bias: float32 [256], P('groups'), parts along dimension 0
- grad_out: float32 [256], P('groups'), parts along dimension 0
- node_grad: bfloat16 [2048, 2048], P(('groups', 'row'), 'col'), parts along dimension 0
There are 2 independent parts, one for each index of `groups`. A program takes and returns all parts, laid end to end along the dimension named above; an argument that names none is the same for every part. Nothing has to cross between parts.
Inputs may be any that keep to these rules, and one draw needn't show every extreme that they name: `pattern`: block row i names only block columns held by the device that holds block row i or by the 2 devices before it along row, and its slot 0 names i itself. `pairs`: A pair's first entry is a segment, the other two are different configurations.
All inputs are finite; a program needn't handle non-finite values.
Results may differ from a plain program's by a relative error of at most 0.0059.
Values may be sent and summed in bfloat16 or wider, within the bound.
No kernel may reach another device: no remote copies, remote signals or barrier semaphores. Data moves between devices by JAX's collectives and lax.ppermute only.
A program may use at most 64 MiB of HBM per device.

v0:
```python
import math

import jax
import jax.numpy as jnp
from jax import lax
from jax.sharding import PartitionSpec as P

REACH = 2
SEGS = 8


def shifted(value, axis, steps):
    count = lax.axis_size(axis)
    initial, last = (max(0, -steps), min(count, count - steps))
    return lax.ppermute(value, axis, [(source, source + steps) for source in range(initial, last)])


def silu_slope(value):
    sigm = jax.nn.sigmoid(value)
    return sigm * (1.0 + value * (1.0 - sigm))


def spread_blocks(grad_blocks, tile_set, column_ids, first_block, target_count):
    width = grad_blocks.shape[2]
    edge = tile_set.shape[2]
    total = jnp.zeros((target_count, edge, width), jnp.float32)
    for slot_index in range(tile_set.shape[1]):
        contrib = jnp.einsum(
            "brs,brc->bsc", tile_set[:, slot_index], grad_blocks, preferred_element_type=jnp.float32
        )
        offset = column_ids[:, slot_index] - first_block
        inside = jnp.logical_and(offset >= 0, offset < target_count)
        target = jnp.where(inside, offset, target_count)
        total = total.at[target].add(contrib, mode="drop")
    return total


def body(features, tiles, pattern, degrees, segments, pairs, w_self, w_neigh, bias, w_out):
    highest = lax.Precision.HIGHEST
    node_count, width = features.shape
    hidden_width = w_self.shape[0]
    local_confs = width // hidden_width
    edge = tiles.shape[2]
    block_count = node_count // edge
    position = lax.axis_index("row")
    lowest = (position - REACH) * block_count
    earlier = [shifted(features, "row", step_back) for step_back in range(REACH, 0, -1)]
    window = jnp.concatenate(earlier + [features], axis=0).reshape(
        (REACH + 1) * block_count, edge, width
    )
    local_ids = pattern - lowest
    summed = jnp.zeros((block_count, edge, width), jnp.float32)
    for slot_index in range(tiles.shape[1]):
        panels = jnp.take(window, local_ids[:, slot_index], axis=0)
        summed = summed + jnp.einsum(
            "brs,bsc->brc", tiles[:, slot_index], panels, preferred_element_type=jnp.float32
        )
    degree = degrees.astype(jnp.float32)[:, None]
    mean_agg = (summed.reshape(node_count, width) / degree).astype(jnp.bfloat16)
    rows_x = features.reshape(node_count * local_confs, hidden_width)
    rows_a = mean_agg.reshape(node_count * local_confs, hidden_width)
    pre = (
        jnp.dot(rows_x, w_self, preferred_element_type=jnp.float32)
        + jnp.dot(rows_a, w_neigh, preferred_element_type=jnp.float32)
        + bias
    )
    hidden = jax.nn.silu(pre)
    node_score = jnp.einsum(
        "ncd,d->nc", hidden.reshape(node_count, local_confs, hidden_width), w_out, precision=highest
    )
    member = (segments[:, None] == jnp.arange(SEGS, dtype=jnp.int32)[None, :]).astype(jnp.float32)
    seg_part = jnp.dot(member.T, node_score, precision=highest, preferred_element_type=jnp.float32)
    count_part = jnp.sum(member, axis=0)
    columns = lax.axis_size("col")
    col_index = lax.axis_index("col")
    seg_sums, counts = lax.psum((seg_part, count_part), "row")
    root = jnp.sqrt(counts)
    scores = lax.all_gather(seg_sums / root[:, None], "col", axis=1, tiled=True)
    total_confs = local_confs * columns
    seg_hot = (pairs[:, 0:1] == jnp.arange(SEGS, dtype=jnp.int32)[None, :]).astype(jnp.float32)
    first_hot = (pairs[:, 1:2] == jnp.arange(total_confs, dtype=jnp.int32)[None, :]).astype(
        jnp.float32
    )
    second_hot = (pairs[:, 2:3] == jnp.arange(total_confs, dtype=jnp.int32)[None, :]).astype(
        jnp.float32
    )
    signed = first_hot - second_hot
    picked = jnp.dot(seg_hot, scores, precision=highest, preferred_element_type=jnp.float32)
    margin = jnp.maximum(0.0, 1.0 - jnp.sum(picked * signed, axis=1))
    loss = jnp.sum(margin * margin).reshape(1)
    d_scores = jnp.dot(
        seg_hot.T,
        (-2.0 * margin)[:, None] * signed,
        precision=highest,
        preferred_element_type=jnp.float32,
    )
    d_local = lax.dynamic_slice_in_dim(
        d_scores / root[:, None], col_index * local_confs, local_confs, 1
    )
    d_node = jnp.dot(member, d_local, precision=highest, preferred_element_type=jnp.float32)
    d_pre = (
        d_node[:, :, None] * w_out * silu_slope(pre.reshape(node_count, local_confs, hidden_width))
    )
    d_pre_b = d_pre.reshape(node_count * local_confs, hidden_width).astype(jnp.bfloat16)
    grad_self = jnp.einsum("nd,ne->de", rows_x, d_pre_b, preferred_element_type=jnp.float32)
    grad_neigh = jnp.einsum("nd,ne->de", rows_a, d_pre_b, preferred_element_type=jnp.float32)
    grad_bias = jnp.sum(d_pre, axis=(0, 1))
    grad_out = jnp.einsum(
        "ncd,nc->d",
        hidden.reshape(node_count, local_confs, hidden_width),
        d_node,
        precision=highest,
    )
    grad_self, grad_neigh, grad_bias, grad_out = lax.psum(
        (grad_self, grad_neigh, grad_bias, grad_out), ("row", "col")
    )
    direct_term = jnp.dot(d_pre_b, w_self.T, preferred_element_type=jnp.float32).reshape(
        node_count, width
    )
    back = (
        jnp.dot(d_pre_b, w_neigh.T, preferred_element_type=jnp.float32).reshape(node_count, width)
        / degree
    ).astype(jnp.bfloat16)
    back_blocks = back.reshape(block_count, edge, width)
    pieces = spread_blocks(back_blocks, tiles, pattern, lowest, (REACH + 1) * block_count).reshape(
        REACH + 1, block_count, edge, width
    )
    gathered = pieces[REACH]
    for step_back in range(1, REACH + 1):
        gathered = gathered + shifted(pieces[REACH - step_back], "row", -step_back)
    scale = math.sqrt(node_count * lax.axis_size("row") / SEGS)
    node_grad = ((direct_term + gathered.reshape(node_count, width)) * scale).astype(jnp.bfloat16)
    return (loss, grad_self, grad_neigh, grad_bias, grad_out, node_grad)


def solution(mesh):
    in_specs = (
        P(("groups", "row"), "col"),
        P(("groups", "row"), None, None, None),
        P(("groups", "row"), None),
        P(("groups", "row")),
        P(("groups", "row")),
        P("groups", None),
        P(),
        P(),
        P(),
        P(),
    )
    out_specs = (
        P("groups"),
        P("groups", None),
        P("groups", None),
        P("groups"),
        P("groups"),
        P(("groups", "row"), "col"),
    )
    return jax.shard_map(body, mesh=mesh, in_specs=in_specs, out_specs=out_specs, check_vma=False)
```

profile of v0, /device:TPU:0, one launch (start us, length us, event | category | flops | bytes accessed | tf_op | source)
XLA Modules:
  0.0 193.9 jit_solution(8198178705377375716)
XLA Ops:
  7.2 4.9 %collective-permute-start = (bf16[128,1024]{1,0:T(8,128)(2,1)}, bf16[128,1024]{1,0:T(8,128)(2,1)S(1)}, u32[]{:S(2)}, u32[]{:S(2)}) collective-permute-start(bf16[128,1024]{1,0:T(8,128)(2,1)} %param.28), channel_id=1, source_target_pairs={{0,4},{2,6},{4,8},{6,10},{8,12},{10,14},{1,5},{3,7},{5,9},{7,11},{... | collective-permute-start | bytes 786440 | tf_op jit(solution)/shard_map/ppermute | solution.py:15
  12.2 3.4 %collective-permute-start.1 = (bf16[128,1024]{1,0:T(8,128)(2,1)}, bf16[128,1024]{1,0:T(8,128)(2,1)S(1)}, u32[]{:S(2)}, u32[]{:S(2)}) collective-permute-start(bf16[128,1024]{1,0:T(8,128)(2,1)} %param.28), channel_id=1, source_target_pairs={{0,2},{2,4},{4,6},{6,8},{8,10},{10,12},{12,14},{1,3},{3,5},{5,7},{... | collective-permute-start | bytes 786440 | tf_op jit(solution)/shard_map/ppermute | solution.py:15
  15.6 1.6 fusion.145
  17.2 0.7 broadcast_subtract_fusion
  23.1 0.8 slice_bitcast_fusion.4
  23.9 0.7 fusion.146
  24.6 1.4 and_reduce_fusion
  26.0 1.5 and_reduce_fusion.2
  27.5 0.8 convert_reduce_fusion
  43.8 1.1 reshape.489
  44.8 0.7 convert_element_type.45
  45.7 0.1 div.72
  45.8 0.9 div.73
  46.7 0.2 fusion.147
  47.0 0.3 fusion.45
  47.2 0.3 convolution_add_fusion.7
  47.5 0.3 convolution_add_fusion.6
  47.8 0.3 convolution_add_fusion.5
  48.1 0.3 convolution_add_fusion.4
  48.3 0.3 convolution_add_fusion.3
  48.6 0.3 convolution_add_fusion.2
  48.9 0.3 fusion
  49.1 0.2 copy.39
  49.5 0.2 divide_convert_fusion
  49.7 0.1 copy-done.6
  49.8 0.2 fusion.3
  50.0 7.0 %fusion.35 = f32[1,128,8]{2,0,1:T(1,128)S(1)} fusion(f32[1024,128]{1,0:T(8,128)S(1)} %fusion.3, f32[128]{0:T(128)S(1)} %copy-done.8), kind=kOutput, calls=%fused_computation.60 | convolution fusion | flops 2097152 | bytes 528896 | tf_op jit(solution)/shard_map/ncd,d->nc/dot_general | solution.py:68
  57.0 0.1 fusion.130
  57.2 18.9 %all-reduce.2 = (f32[8,8]{1,0:T(8,128)S(1)}, f32[8]{0:T(128)S(1)}) all-reduce(f32[8,8]{1,0:T(8,128)S(1)} %fusion.130, f32[8]{0:T(128)S(1)} %convert_reduce_fusion), channel_id=1, replica_groups=mesh['groups'=2,'row'=8,'col'=2] {'row'}, use_global_device_ids=true, to_apply=%region_0.0 | all-reduce | flops 72 | bytes 576 | tf_op jit(solution)/shard_map/psum | solution.py:76
  76.2 1.8 all_gather.3
  78.0 0.2 fusion.27
  78.3 0.6 broadcast_multiply_fusion
  78.9 0.2 convolution_divide_fusion.1
  79.1 0.3 fusion.126
  79.4 0.1 copy.41
  79.6 0.3 fusion.144
  79.8 0.9 fusion.148
  80.8 0.2 fusion.26
  81.0 0.1 convert_element_type.52
  81.1 0.1 broadcast_in_dim.19
  81.2 0.8 fusion.2
  82.0 0.9 fusion.6
  83.0 0.8 fusion.9
  83.8 0.9 fusion.12
  84.7 0.9 fusion.15
  85.6 0.9 fusion.18
  86.5 0.9 fusion.21
  87.4 0.1 copy.59
  87.5 0.9 fusion.25
  88.4 0.8 slice_bitcast_fusion
  89.2 0.9 slice_bitcast_fusion.1
  90.1 1.3 collective-permute-start.3
  91.4 1.3 collective-permute-start.2
  92.7 0.9 convolution_bitcast_fusion.7
  93.6 0.1 copy.49
  93.7 0.2 fusion.149
  93.9 1.0 convolution_bitcast_fusion.8
  95.0 0.2 copy.45
  95.2 42.6 %all-reduce = (f32[128]{0:T(128)}, f32[128]{0:T(128)}) all-reduce(f32[128]{0:T(128)S(1)} %get-tuple-element.152, f32[128]{0:T(128)S(1)} %convolution_bitcast_fusion.8), channel_id=1, replica_groups=mesh['groups'=2,'row'=8,'col'=2] {'row','col'}, use_global_device_ids=true, to_apply=%region_8.10 | all-reduce | flops 256 | bytes 2048 | tf_op jit(solution)/shard_map/psum | solution.py:114
  137.8 44.9 %all-reduce.5.cloned.1.call-done = (f32[128,128]{0,1:T(8,128)}, f32[128,128]{1,0:T(8,128)}) async-done(((f32[128,128]{0,1:T(8,128)}, f32[128,128]{1,0:T(8,128)}), (f32[128,128]{0,1:T(8,128)}, f32[128,128]{1,0:T(8,128)})) %all-reduce.5.cloned.1.call-update) | async-done | bytes 131088 | tf_op jit(solution)/shard_map/psum | solution.py:114
  182.7 1.6 copy.46
  184.3 1.3 fusion.33
  185.6 0.9 copy.47
  186.4 0.6 copy.60
  (32 shorter events, 0.8 us)
Async XLA Ops:
  7.2 42.5 %copy-start = (bf16[128,128]{1,0:T(8,128)(2,1)S(1)}, bf16[128,128]{1,0:T(8,128)(2,1)}, u32[]{:S(2)}) copy-start(bf16[128,128]{1,0:T(8,128)(2,1)} %param.35) | copy-start | bytes 98308
  7.2 39.5 %copy-start.4 = (bf16[128,128]{1,0:T(8,128)(2,1)S(1)}, bf16[128,128]{1,0:T(8,128)(2,1)}, u32[]{:S(2)}) copy-start(bf16[128,128]{1,0:T(8,128)(2,1)} %param.34) | copy-start | bytes 98308
  7.2 175.5 %all-reduce.5.cloned.1.call-start = ((), (), s32[]{:S(2)}) async-start(), calls=%async_computation | async-start | bytes 262144 | tf_op jit(solution)/shard_map/psum | solution.py:114
  7.2 39.6 %collective-permute-start = (bf16[128,1024]{1,0:T(8,128)(2,1)}, bf16[128,1024]{1,0:T(8,128)(2,1)S(1)}, u32[]{:S(2)}, u32[]{:S(2)}) collective-permute-start(bf16[128,1024]{1,0:T(8,128)(2,1)} %param.28), channel_id=1, source_target_pairs={{0,4},{2,6},{4,8},{6,10},{8,12},{10,14},{1,5},{3,7},{5,9},{7,11},{... | collective-permute-start | bytes 786440 | tf_op jit(solution)/shard_map/ppermute | solution.py:15
  12.2 34.7 %collective-permute-start.1 = (bf16[128,1024]{1,0:T(8,128)(2,1)}, bf16[128,1024]{1,0:T(8,128)(2,1)S(1)}, u32[]{:S(2)}, u32[]{:S(2)}) collective-permute-start(bf16[128,1024]{1,0:T(8,128)(2,1)} %param.28), channel_id=1, source_target_pairs={{0,2},{2,4},{4,6},{6,8},{8,10},{10,12},{12,14},{1,3},{3,5},{5,7},{... | collective-permute-start | bytes 786440 | tf_op jit(solution)/shard_map/ppermute | solution.py:15
  34.0 12.9 %copy-start.2 = (bf16[128,1024]{1,0:T(8,128)(2,1)S(1)}, bf16[128,1024]{1,0:T(8,128)(2,1)}, u32[]{:S(2)}) copy-start(bf16[128,1024]{1,0:T(8,128)(2,1)} %param.28) | copy-start | bytes 786436
  45.8 1.2 copy-start.1
  49.1 0.7 copy-start.6
  49.3 0.7 copy-start.8
  49.8 7.2 %copy-start.7 = (s32[128]{0:T(128)S(1)}, s32[128]{0:T(128)}, u32[]{:S(2)}) copy-start(s32[128]{0:T(128)} %param.32) | copy-start | bytes 1540
  50.0 30.7 %copy-start.3 = (f32[1024,128]{1,0:T(8,128)S(1)}, f32[1024,128]{1,0:T(8,128)}, u32[]{:S(2)}) copy-start(f32[1024,128]{1,0:T(8,128)} %div.73) | copy-start | bytes 1572868
  90.1 94.2 %collective-permute-start.3 = (f32[1,128,1024]{1,2,0:T(8,128)}, f32[1,128,1024]{1,2,0:T(8,128)}, u32[]{:S(2)}, u32[]{:S(2)}) collective-permute-start(f32[1,128,1024]{1,2,0:T(8,128)} %slice_bitcast_fusion), channel_id=1, source_target_pairs={{4,0},{6,2},{8,4},{10,6},{12,8},{14,10},{5,1},{7,3},{9,5},{11,7},{... | collective-permute-start | bytes 1572872 | tf_op jit(solution)/shard_map/ppermute | solution.py:15
  91.4 92.9 %collective-permute-start.2 = (f32[1,128,1024]{1,2,0:T(8,128)}, f32[1,128,1024]{1,2,0:T(8,128)}, u32[]{:S(2)}, u32[]{:S(2)}) collective-permute-start(f32[1,128,1024]{1,2,0:T(8,128)} %slice_bitcast_fusion.1), channel_id=1, source_target_pairs={{2,0},{4,2},{6,4},{8,6},{10,8},{12,10},{14,12},{3,1},{5,3},{7,5},{... | collective-permute-start | bytes 1572872 | tf_op jit(solution)/shard_map/ppermute | solution.py:15
  182.7 3.8 %copy-start.5 = (f32[128,128]{1,0:T(8,128)S(1)}, f32[128,128]{1,0:T(8,128)}, u32[]{:S(2)}) copy-start(f32[128,128]{1,0:T(8,128)} %get-tuple-element.183) | copy-start | bytes 196612
Sparse Core Ops, SparseCore 0:
  93.8 88.8 all-reduce.4
where the time goes:
time: 196 us; the launch traced here: 194 us
  blocking collectives  63.3 us (32%)
  waiting for transfers between devices  44.9 us (23%)
  between operations  35.1 us (18%)
  matrix products  20.7 us (11%)
  local copies, waits for them, and re-layouts  11.5 us (6%)
  starting transfers between devices  11 us (6%)
  other arithmetic  7.5 us (4%)
    psum x1, waiting for transfers between devices, body(): lax.psum((grad_self, grad_neigh, grad_bias, grad_out), ('row', 'col'))  44.9 us
    psum x1, blocking collectives, body(): lax.psum((grad_self, grad_neigh, grad_bias, grad_out), ('row', 'col'))  42.6 us
    psum x1, blocking collectives, body(): seg_sums, counts = lax.psum((seg_part, count_part), 'row')  18.9 us
    ppermute x4, starting transfers between devices, shifted(): lax.ppermute(value, axis, [(source, source + steps) for source in range(i...  10.9 us
    dot_general x8, matrix products, spread_blocks(): jnp.einsum('brs,brc->bsc', tile_set[:, slot_index], grad_blocks, preferre...  7.03 us
    dot_general x1, matrix products, body(): jnp.einsum('ncd,d->nc', hidden.reshape(node_count, local_confs, hidden_wi...  7 us
  transfers between devices with their start and end apart: 5, of which 1 were waited for; matrix products, arithmetic and copies ran while one was open for 8% of the time, Pallas kernels for 0%

commit v1 on v0

v1 whole, which is shorter than its diff:
```python
import functools
import math

import jax
import jax.numpy as jnp
from jax import lax
from jax.experimental import pallas as pl
from jax.experimental.pallas import tpu as pltpu
from jax.sharding import PartitionSpec as P

REACH = 2
SEGS = 8
WINDOW = REACH + 1
F32 = jnp.float32
BF16 = jnp.bfloat16
HIGHEST = lax.Precision.HIGHEST
VMEM = pl.BlockSpec(memory_space=pltpu.VMEM)
SMEM = pl.BlockSpec(memory_space=pltpu.SMEM)
LIMIT = 24 << 20


def shifted(value, axis, steps):
    count = lax.axis_size(axis)
    initial, last = (max(0, -steps), min(count, count - steps))
    return lax.ppermute(value, axis, [(source, source + steps) for source in range(initial, last)])


def exchanged(value, axis, bit):
    count = lax.axis_size(axis)
    return lax.ppermute(value, axis, [(source, source ^ bit) for source in range(count)])


def mm(left, right, contract=((1,), (0,))):
    return lax.dot_general(left, right, (contract, ((), ())), preferred_element_type=F32)


def mm_exact(left, right, contract):
    return lax.dot_general(
        left, right, (contract, ((), ())), precision=HIGHEST, preferred_element_type=F32
    )


def split_two(value):
    high = value.astype(BF16)
    return high, (value - high.astype(F32)).astype(BF16)


def forward_kernel(
    local_confs,
    place_ref,
    ids_ref,
    own_ref,
    near_ref,
    far_ref,
    tiles_ref,
    degree_ref,
    segments_ref,
    w_self_ref,
    w_neigh_ref,
    bias_ref,
    w_out_ref,
    mean_ref,
    slope_ref,
    hidden_sum_ref,
    message_ref,
    tile_high_ref,
    tile_low_ref,
):
    hid = w_self_ref.shape[0]
    window = (far_ref, near_ref, own_ref)
    summed = None
    for reach in range(WINDOW):
        total = None
        for slot in range(tiles_ref.shape[1]):
            keep = (ids_ref[0, slot] == reach).astype(F32)
            term = tiles_ref[0, slot].astype(F32) * keep
            total = term if total is None else total + term
        high, low = split_two(total)
        tile_high_ref[reach] = high
        tile_low_ref[reach] = low
        panel = window[reach][...]
        term = mm(high, panel) + mm(low, panel)
        summed = term if summed is None else summed + term
    inverse = 1.0 / degree_ref[...]
    w_out = w_out_ref[...]
    seg_iota = lax.broadcasted_iota(jnp.int32, (SEGS, segments_ref.shape[1]), 0)
    member = (segments_ref[...] == seg_iota).astype(F32)
    member_b = member.astype(BF16)
    lane = lax.broadcasted_iota(jnp.int32, (SEGS, 128), 1)
    total_confs = place_ref[1]
    first_conf = place_ref[0] * local_confs
    counts = jnp.sum(member, axis=1, keepdims=True)
    message = jnp.where((lane == total_confs) & (place_ref[0] == 0), counts, 0.0)
    for conf in range(local_confs):
        cols = slice(conf * hid, (conf + 1) * hid)
        mean = (summed[:, cols] * inverse).astype(BF16)
        mean_ref[:, cols] = mean
        pre = mm(own_ref[:, cols], w_self_ref[...]) + mm(mean, w_neigh_ref[...]) + bias_ref[...]
        sigm = 1.0 / (1.0 + jnp.exp(-pre))
        hidden = pre * sigm
        slope_ref[:, cols] = w_out * (sigm * (1.0 + pre * (1.0 - sigm)))
        high, low = split_two(hidden)
        hidden_sum = mm(member_b, high) + mm(member_b, low)
        hidden_sum_ref[:, cols] = hidden_sum
        score = jnp.sum(hidden_sum * w_out, axis=1, keepdims=True)
        message = message + jnp.where(lane == first_conf + conf, score, 0.0)
    for peer in range(message_ref.shape[0]):
        message_ref[peer] = message


def gradient_kernel(
    local_confs,
    place_ref,
    received_ref,
    pairs_ref,
    segments_ref,
    own_ref,
    mean_ref,
    slope_ref,
    hidden_sum_ref,
    grads_ref,
    loss_ref,
    d_pre_ref,
):
    hid = grads_ref.shape[1]
    nodes = own_ref.shape[0]
    pair_count = pairs_ref.shape[1]
    total = jnp.sum(received_ref[...], axis=0)
    lane = lax.broadcasted_iota(jnp.int32, (SEGS, 128), 1)
    counts = jnp.sum(jnp.where(lane == place_ref[1], total, 0.0), axis=1, keepdims=True)
    root = jnp.sqrt(counts)
    scores = total / root
    seg_hot = (
        pairs_ref[0:1, :] == lax.broadcasted_iota(jnp.int32, (SEGS, pair_count), 0)
    ).astype(F32)
    conf_iota = lax.broadcasted_iota(jnp.int32, (128, pair_count), 0)
    signed = (pairs_ref[1:2, :] == conf_iota).astype(F32) - (
        pairs_ref[2:3, :] == conf_iota
    ).astype(F32)
    picked = mm_exact(scores, seg_hot, ((0,), (0,)))
    margin = jnp.maximum(0.0, 1.0 - jnp.sum(picked * signed, axis=0, keepdims=True))
    loss_ref[...] = jnp.sum(margin * margin, axis=1, keepdims=True)
    d_scores = mm_exact(seg_hot, (-2.0 * margin) * signed, ((1,), (1,))) / root
    seg_iota = lax.broadcasted_iota(jnp.int32, (SEGS, nodes), 0)
    member = (segments_ref[...] == seg_iota).astype(BF16)
    member = jnp.concatenate([member, member], axis=0)
    first_conf = place_ref[0] * local_confs
    grads = None
    d_bias = None
    d_out = None
    for conf in range(local_confs):
        cols = slice(conf * hid, (conf + 1) * hid)
        column = jnp.sum(
            jnp.where(lane == first_conf + conf, d_scores, 0.0), axis=1, keepdims=True
        )
        spread = jnp.broadcast_to(column, (SEGS, hid))
        high, low = split_two(spread)
        low, last = split_two(spread - high.astype(F32))
        d_node = mm(
            jnp.concatenate([member, member[:SEGS]], axis=0),
            jnp.concatenate([high, low, last], axis=0),
            ((0,), (0,)),
        )
        d_pre = d_node * slope_ref[:, cols]
        d_pre_b = d_pre.astype(BF16)
        d_pre_ref[:, cols] = d_pre_b
        rows = jnp.concatenate([own_ref[:, cols], mean_ref[:, cols]], axis=1)
        term = mm(rows, d_pre_b, ((0,), (0,)))
        bias_term = jnp.sum(d_pre, axis=0, keepdims=True)
        out_term = jnp.sum(spread * hidden_sum_ref[:, cols], axis=0, keepdims=True)
        grads = term if grads is None else grads + term
        d_bias = bias_term if d_bias is None else d_bias + bias_term
        d_out = out_term if d_out is None else d_out + out_term
    grads_ref[: 2 * hid] = grads
    sub = lax.broadcasted_iota(jnp.int32, (8, hid), 0)
    grads_ref[2 * hid :] = jnp.where(sub == 0, d_bias, 0.0) + jnp.where(sub == 1, d_out, 0.0)


def spread_kernel(
    local_confs,
    d_pre_ref,
    w_self_ref,
    w_neigh_ref,
    degree_ref,
    tile_high_ref,
    tile_low_ref,
    far_ref,
    near_ref,
    own_ref,
):
    hid = w_self_ref.shape[0]
    inverse = 1.0 / degree_ref[...]
    for conf in range(local_confs):
        cols = slice(conf * hid, (conf + 1) * hid)
        d_pre = d_pre_ref[:, cols]
        back = (mm(d_pre, w_neigh_ref[...], ((1,), (1,))) * inverse).astype(BF16)
        own = mm(d_pre, w_self_ref[...], ((1,), (1,)))
        pieces = [
            mm(tile_high_ref[reach], back, ((0,), (0,)))
            + mm(tile_low_ref[reach], back, ((0,), (0,)))
            for reach in range(WINDOW)
        ]
        far_ref[:, cols] = pieces[0].astype(BF16)
        near_ref[:, cols] = pieces[1].astype(BF16)
        own_ref[:, cols] = own + pieces[2]


def rounded(value):
    return lax.reduce_precision(value, 8, 7)


def packed(total, main):
    vectors = total[main:]
    high = rounded(vectors)
    middle = rounded(vectors - high)
    last = rounded(vectors - high - middle)
    return jnp.concatenate([rounded(total[:main]), high, middle, last], axis=0).astype(BF16)


def unpacked(message, main):
    message = message.astype(F32)
    extra = (message.shape[0] - main) // 3
    parts = [message[main + i * extra : main + (i + 1) * extra] for i in range(3)]
    return jnp.concatenate([message[:main], parts[0] + parts[1] + parts[2]], axis=0)


def summed_over_devices(total, main):
    for axis in ("col", "row"):
        count = lax.axis_size(axis)
        if count & (count - 1):
            total = lax.psum(total, axis)
            continue
        for step in range(count.bit_length() - 1):
            if axis == "col":
                total = total + exchanged(total, axis, 1 << step)
            else:
                message = packed(total, main)
                total = unpacked(message, main) + unpacked(
                    exchanged(message, axis, 1 << step), main
                )
    return total


def body(features, tiles, pattern, degrees, segments, pairs, w_self, w_neigh, bias, w_out):
    nodes, width = features.shape
    hid = w_self.shape[0]
    local_confs = width // hid
    rows, columns = lax.axis_size("row"), lax.axis_size("col")
    position, column = lax.axis_index("row"), lax.axis_index("col")
    far = shifted(features, "row", 2)
    near = shifted(features, "row", 1)
    ids = pattern - (position - REACH)
    place = jnp.stack([column, jnp.int32(local_confs * columns)]).astype(jnp.int32)
    degree = jnp.broadcast_to(degrees.astype(F32)[:, None], (nodes, hid))
    segment_row = segments.reshape(1, nodes)
    params = pltpu.CompilerParams(vmem_limit_bytes=LIMIT)
    mean, slope, hidden_sum, message, tile_high, tile_low = pl.pallas_call(
        functools.partial(forward_kernel, local_confs),
        out_shape=(
            jax.ShapeDtypeStruct((nodes, width), BF16),
            jax.ShapeDtypeStruct((nodes, width), F32),
            jax.ShapeDtypeStruct((SEGS, width), F32),
            jax.ShapeDtypeStruct((rows * columns, SEGS, 128), F32),
            jax.ShapeDtypeStruct((WINDOW, nodes, nodes), BF16),
            jax.ShapeDtypeStruct((WINDOW, nodes, nodes), BF16),
        ),
        in_specs=[SMEM] * 2 + [VMEM] * 10,
        out_specs=(VMEM,) * 6,
        compiler_params=params,
        name="forward",
    )(
        place,
        ids,
        features,
        near,
        far,
        tiles,
        degree,
        segment_row,
        w_self,
        w_neigh,
        bias.reshape(1, hid),
        w_out.reshape(1, hid),
    )
    received = lax.all_to_all(message, ("row", "col"), 0, 0, tiled=True)
    main = 2 * hid
    grads, loss, d_pre = pl.pallas_call(
        functools.partial(gradient_kernel, local_confs),
        out_shape=(
            jax.ShapeDtypeStruct((main + 8, hid), F32),
            jax.ShapeDtypeStruct((1, 1), F32),
            jax.ShapeDtypeStruct((nodes, width), BF16),
        ),
        in_specs=[SMEM] + [VMEM] * 7,
        out_specs=(VMEM,) * 3,
        compiler_params=params,
        name="gradient",
    )(place, received, pairs.T, segment_row, features, mean, slope, hidden_sum)
    far_piece, near_piece, own_piece = pl.pallas_call(
        functools.partial(spread_kernel, local_confs),
        out_shape=(
            jax.ShapeDtypeStruct((nodes, width), BF16),
            jax.ShapeDtypeStruct((nodes, width), BF16),
            jax.ShapeDtypeStruct((nodes, width), F32),
        ),
        in_specs=[VMEM] * 6,
        out_specs=(VMEM,) * 3,
        compiler_params=params,
        name="spread",
    )(d_pre, w_self, w_neigh, degree, tile_high, tile_low)
    gathered = (
        own_piece
        + shifted(far_piece, "row", -2).astype(F32)
        + shifted(near_piece, "row", -1).astype(F32)
    )
    scale = math.sqrt(nodes * rows / SEGS)
    node_grad = (gathered * scale).astype(BF16)
    total = summed_over_devices(grads, main)
    return (
        loss.reshape(1),
        total[:hid],
        total[hid:main],
        total[main],
        total[main + 1],
        node_grad,
    )


def solution(mesh):
    in_specs = (
        P(("groups", "row"), "col"),
        P(("groups", "row"), None, None, None),
        P(("groups", "row"), None),
        P(("groups", "row")),
        P(("groups", "row")),
        P("groups", None),
        P(),
        P(),
        P(),
        P(),
    )
    out_specs = (
        P("groups"),
        P("groups", None),
        P("groups", None),
        P("groups"),
        P("groups"),
        P(("groups", "row"), "col"),
    )
    return jax.shard_map(body, mesh=mesh, in_specs=in_specs, out_specs=out_specs, check_vma=False)
```

time: 196 us -> 65 us (0.33)
  blocking collectives: 63.3 us -> 15.9 us
  between operations: 35.1 us -> 0.88 us
  waiting for transfers between devices: 44.9 us -> 17.3 us
  matrix products: 20.7 us -> 0 us
  starting transfers between devices: 11 us -> 17.8 us
  local copies, waits for them, and re-layouts: 11.5 us -> 5.41 us
  other arithmetic: 7.5 us -> 1.69 us
  Pallas kernels: 0 us -> 5.64 us
    psum x2 -> x0, blocking collectives: 61.5 us -> none  [the longest x1 42.6 us: body(): lax.psum((grad_self, grad_neigh, grad_bias, grad_out), ('row', 'col'))]
    psum x1 -> x0, waiting for transfers between devices: 44.9 us -> none  [body(): lax.psum((grad_self, grad_neigh, grad_bias, grad_out), ('row', 'col'))]
    dot_general x28 -> x0, matrix products: 20.7 us -> none  [the longest x8 7.03 us: spread_blocks(): jnp.einsum('brs,brc->bsc', tile_set[:, slot_index], grad_blocks, preferre...]
    all_to_all x0 -> x1, blocking collectives: none -> 15.9 us  [body(): received = lax.all_to_all(message, ('row', 'col'), 0, 0, tiled=True)]
    ppermute x0 -> x4, waiting for transfers between devices: none -> 13.1 us  [exchanged(): lax.ppermute(value, axis, [(source, source ^ bit) for source in range(cou...]
    ppermute x0 -> x4, starting transfers between devices: none -> 6.84 us  [exchanged(): lax.ppermute(value, axis, [(source, source ^ bit) for source in range(cou...]
    pallas_call x0 -> x3, Pallas kernels: none -> 5.64 us  [the longest x1 2.06 us: body(): pl.pallas_call(functools.partial(gradient_kernel, local_confs), out_shape...]
    ppermute x4, waiting for transfers between devices: 0.01 us -> 4.17 us  [shifted(): lax.ppermute(value, axis, [(source, source + steps) for source in range(i...]
  transfers between devices with their start and end apart: 5 -> 8, of which waited for: 1 -> 5; matrix products, arithmetic and copies ran while one was open for 8% -> 2% of each run, Pallas kernels for 0% -> 3%
where the time goes in v1:
time: 65 us; the launch traced here: 64.6 us
  starting transfers between devices  17.8 us (27%)
  waiting for transfers between devices  17.3 us (27%)
  blocking collectives  15.9 us (24%)
  Pallas kernels  5.64 us (9%)
  local copies, waits for them, and re-layouts  5.41 us (8%)
  other arithmetic  1.69 us (3%)
  between operations  0.88 us (1%)
    all_to_all x1, blocking collectives, body(): received = lax.all_to_all(message, ('row', 'col'), 0, 0, tiled=True)  15.9 us
    ppermute x4, waiting for transfers between devices, exchanged(): lax.ppermute(value, axis, [(source, source ^ bit) for source in range(cou...  13.1 us
    ppermute x4, starting transfers between devices, shifted(): lax.ppermute(value, axis, [(source, source + steps) for source in range(i...  10.9 us
    ppermute x4, starting transfers between devices, exchanged(): lax.ppermute(value, axis, [(source, source ^ bit) for source in range(cou...  6.84 us
    unnamed x22, local copies, waits for them, and re-layouts  4.62 us
    ppermute x4, waiting for transfers between devices, shifted(): lax.ppermute(value, axis, [(source, source + steps) for source in range(i...  4.17 us
    pallas_call x1, Pallas kernels, body(): pl.pallas_call(functools.partial(gradient_kernel, local_confs), out_shape...  2.06 us
    pallas_call x1, Pallas kernels, body(): pl.pallas_call(functools.partial(spread_kernel, local_confs), out_shape=(...  1.85 us
  transfers between devices with their start and end apart: 8, of which 5 were waited for; matrix products, arithmetic and copies ran while one was open for 2% of the time, Pallas kernels for 3%

profile of v1, /device:TPU:0, one launch (start us, length us, event | category | flops | bytes accessed | tf_op | source)
XLA Modules:
  0.0 64.6 jit_solution(5280285541727566367)
XLA Ops:
  0.6 4.9 %collective-permute-start.1 = (bf16[128,1024]{1,0:T(8,128)(2,1)}, bf16[128,1024]{1,0:T(8,128)(2,1)S(1)}, u32[]{:S(2)}, u32[]{:S(2)}) collective-permute-start(bf16[128,1024]{1,0:T(8,128)(2,1)} %own_ref.3), channel_id=1, source_target_pairs={{0,4},{2,6},{4,8},{6,10},{8,12},{10,14},{1,5},{3,7},{5,9},{7,11},{... | collective-permute-start | bytes 786440 | tf_op jit(solution)/shard_map/ppermute | solution.py:25
  5.6 3.4 %collective-permute-start = (bf16[128,1024]{1,0:T(8,128)(2,1)}, bf16[128,1024]{1,0:T(8,128)(2,1)S(1)}, u32[]{:S(2)}, u32[]{:S(2)}) collective-permute-start(bf16[128,1024]{1,0:T(8,128)(2,1)} %own_ref.3), channel_id=1, source_target_pairs={{0,2},{2,4},{4,6},{6,8},{8,10},{10,12},{12,14},{1,3},{3,5},{5,7},{... | collective-permute-start | bytes 786440 | tf_op jit(solution)/shard_map/ppermute | solution.py:25
  9.0 0.1 pad_add_fusion.place_ref
  9.1 0.0 copy-start.9
  9.1 0.7 %copy-done.9 = s32[128]{0:T(128)S(1)} copy-done((s32[128]{0:T(128)S(1)}, s32[128]{0:T(128)}, u32[]{:S(2)}) %copy-start.9) | copy-done | bytes 536
  9.7 0.0 copy-start.10
  9.7 0.7 %copy-done.10 = s32[1,8]{1,0:T(1,128)S(1)} copy-done((s32[1,8]{1,0:T(1,128)S(1)}, s32[1,8]{1,0:T(1,128)}, u32[]{:S(2)}) %copy-start.10) | copy-done | bytes 56
  10.4 1.0 %collective-permute-done.1.far_ref = bf16[128,1024]{1,0:T(8,128)(2,1)S(1)} collective-permute-done((bf16[128,1024]{1,0:T(8,128)(2,1)}, bf16[128,1024]{1,0:T(8,128)(2,1)S(1)}, u32[]{:S(2)}, u32[]{:S(2)}) %collective-permute-start.1) | collective-permute-done | bytes 262176 | tf_op jit(solution)/shard_map/ppermute | solution.py:25
  11.4 3.1 %collective-permute-done.near_ref = bf16[128,1024]{1,0:T(8,128)(2,1)S(1)} collective-permute-done((bf16[128,1024]{1,0:T(8,128)(2,1)}, bf16[128,1024]{1,0:T(8,128)(2,1)S(1)}, u32[]{:S(2)}, u32[]{:S(2)}) %collective-permute-start) | collective-permute-done | bytes 262176 | tf_op jit(solution)/shard_map/ppermute | solution.py:25
  14.6 0.0 copy-start.7
  14.6 0.0 copy-start.8
  14.6 0.0 copy-start.3
  14.6 0.0 copy-start.4
  14.6 0.0 copy-start.6
  14.6 0.1 broadcast_in_dim.2.degree_ref
  14.7 0.6 copy-done.7
  15.2 0.0 copy-done.8
  15.2 0.1 copy-done.3
  15.4 0.0 copy-done.4
  15.4 0.0 copy-done.6
  15.4 0.0 copy-start
  15.4 0.9 %copy-done = bf16[128,1024]{1,0:T(8,128)(2,1)S(1)} copy-done((bf16[128,1024]{1,0:T(8,128)(2,1)S(1)}, bf16[128,1024]{1,0:T(8,128)(2,1)}, u32[]{:S(2)}) %copy-start) | copy-done | bytes 262168
  16.3 0.0 copy-start.2
  16.3 0.9 %copy-done.2 = bf16[1,8,128,128]{3,2,1,0:T(8,128)(2,1)S(1)} copy-done((bf16[1,8,128,128]{3,2,1,0:T(8,128)(2,1)S(1)}, bf16[1,8,128,128]{3,2,1,0:T(8,128)(2,1)}, u32[]{:S(2)}) %copy-start.2) | copy-done | bytes 262168
  17.3 0.0 copy-start.1
  17.3 1.7 %forward.1 = (bf16[128,1024]{1,0:T(8,128)(2,1)S(1)}, f32[128,1024]{1,0:T(8,128)S(1)}, f32[8,1024]{1,0:T(8,128)S(1)}, f32[16,8,128]{2,1,0:T(8,128)S(1)}, bf16[3,1...) custom-call(s32[2]{0:T(128)S(1)} %pad_add_fusion.place_ref, s32[1,8]{1,0:T(1,128)S(1)} %broadcast_subtract_fusion.ids_ref, ...), custom_call_target="tpu_custom_call" | custom-call | tf_op jit(solution)/shard_map/forward/pallas_call | solution.py:257
  19.0 15.9 %all_to_all.5.received_ref = f32[16,8,128]{2,1,0:T(8,128)S(1)} all-to-all(f32[16,8,128]{2,1,0:T(8,128)S(1)} %get-tuple-element.18), channel_id=1, replica_groups=mesh['groups'=2,'row'=8,'col'=2] {'row','col'}, dimensions={0} | all-to-all | bytes 131072 | tf_op jit(solution)/shard_map/all_to_all | solution.py:285
  34.9 0.0 copy-start.5
  34.9 0.0 copy-done.1
  34.9 0.7 %copy-done.5 = s32[64,3]{0,1:T(4,128)S(1)} copy-done((s32[64,3]{0,1:T(4,128)S(1)}, s32[64,3]{0,1:T(4,128)}, u32[]{:S(2)}) %copy-start.5) | copy-done | bytes 792
  35.6 2.1 %gradient.1 = (f32[264,128]{1,0:T(8,128)S(1)}, f32[1,1]{1,0:T(1,128)}, bf16[128,1024]{1,0:T(8,128)(2,1)S(1)}) custom-call(s32[2]{0:T(128)S(1)} %pad_add_fusion.place_ref, f32[16,8,128]{2,1,0:T(8,128)S(1)} %all_to_all.5.received_ref, s32[3,64]{1,0:T(4,128)S(1)} %bitcast.10, s32[1,128]{1,0:T(1,128)S(1)} %bitcast.12, bf16[128,1024]{1,0:T(8,128)(2,1)S(1)} %copy-done.1, ...), custom_call_target="tpu_custom_call" | custom-call | tf_op jit(solution)/shard_map/gradient/pallas_call | solution.py:287
  37.7 0.0 collective-permute-start.2
  37.7 1.8 %spread.1 = (bf16[128,1024]{1,0:T(8,128)(2,1)S(1)}, bf16[128,1024]{1,0:T(8,128)(2,1)S(1)}, f32[128,1024]{1,0:T(8,128)S(1)}) custom-call(bf16[128,1024]{1,0:T(8,128)(2,1)S(1)} %get-tuple-element.24.d_pre_ref, bf16[128,128]{1,0:T(8,128)(2,1)S(1)} %copy-done.3, bf16[128,128]{1,0:T(8,128)(2,1)S(1)} %copy-done.4, f32[128,128]{1,0:T(8,128)S(1)} %broadcast_in_dim.2.degree_ref, ...), custom_call_target="tpu_custom_call" | custom-call | tf_op jit(solution)/shard_map/spread/pallas_call | solution.py:299
  39.5 1.3 %collective-permute-start.6 = (bf16[128,1024]{1,0:T(8,128)(2,1)S(1)}, bf16[128,1024]{1,0:T(8,128)(2,1)S(1)}, u32[]{:S(2)}, u32[]{:S(2)}) collective-permute-start(bf16[128,1024]{1,0:T(8,128)(2,1)S(1)} %get-tuple-element.28), channel_id=1, source_target_pairs={{4,0},{6,2},{8,4},{10,6},{12,8},{14,10},{5,1},{7,3},{9,5},{11,7},{... | collective-permute-start | bytes 786440 | tf_op jit(solution)/shard_map/ppermute | solution.py:25
  40.8 1.3 %collective-permute-start.7 = (bf16[128,1024]{1,0:T(8,128)(2,1)S(1)}, bf16[128,1024]{1,0:T(8,128)(2,1)S(1)}, u32[]{:S(2)}, u32[]{:S(2)}) collective-permute-start(bf16[128,1024]{1,0:T(8,128)(2,1)S(1)} %get-tuple-element.29), channel_id=1, source_target_pairs={{2,0},{4,2},{6,4},{8,6},{10,8},{12,10},{14,12},{3,1},{5,3},{7,5},{... | collective-permute-start | bytes 786440 | tf_op jit(solution)/shard_map/ppermute | solution.py:25
  42.1 0.0 collective-permute-done.2
  42.2 2.7 %collective-permute-start.3 = (bf16[280,128]{1,0:T(8,128)(2,1)S(1)}, bf16[280,128]{1,0:T(8,128)(2,1)S(1)}, u32[]{:S(2)}, u32[]{:S(2)}) collective-permute-start(bf16[280,128]{1,0:T(8,128)(2,1)S(1)} %get-tuple-element.46), channel_id=1, source_target_pairs={{0,2},{2,0},{4,6},{6,4},{8,10},{10,8},{12,14},{14,12},{1,3},{3,1},... | collective-permute-start | bytes 215048 | tf_op jit(solution)/shard_map/ppermute | solution.py:30
  45.0 8.0 %collective-permute-done.3 = bf16[280,128]{1,0:T(8,128)(2,1)S(1)} collective-permute-done((bf16[280,128]{1,0:T(8,128)(2,1)S(1)}, bf16[280,128]{1,0:T(8,128)(2,1)S(1)}, u32[]{:S(2)}, u32[]{:S(2)}) %collective-permute-start.3) | collective-permute-done | bytes 71712 | tf_op jit(solution)/shard_map/ppermute | solution.py:30
  53.1 2.4 %collective-permute-start.4 = (bf16[280,128]{1,0:T(8,128)(2,1)S(1)}, bf16[280,128]{1,0:T(8,128)(2,1)S(1)}, u32[]{:S(2)}, u32[]{:S(2)}) collective-permute-start(bf16[280,128]{1,0:T(8,128)(2,1)S(1)} %get-tuple-element.44), channel_id=1, source_target_pairs={{0,4},{2,6},{4,0},{6,2},{8,12},{10,14},{12,8},{14,10},{1,5},{3,7},... | collective-permute-start | bytes 215048 | tf_op jit(solution)/shard_map/ppermute | solution.py:30
  55.6 0.0 collective-permute-done.6
  55.6 0.0 collective-permute-done.7
  55.6 0.8 %multiply_convert_fusion = bf16[128,1024]{1,0:T(8,128)(2,1)} fusion(bf16[128,1024]{1,0:T(8,128)(2,1)S(1)} %collective-permute-done.7, f32[128,1024]{1,0:T(8,128)S(1)} %get-tuple-element.27, bf16[128,1024]{1,0:T(8,128)(2,1)S(1)} %collective-permute-done.6), kind=kLoop, calls=%fused_computation | loop fusion | flops 786432 | bytes 1310720 | tf_op jit(solution)/shard_map/convert_element_type | solution.py:317
  56.4 1.5 %collective-permute-done.4 = bf16[280,128]{1,0:T(8,128)(2,1)S(1)} collective-permute-done((bf16[280,128]{1,0:T(8,128)(2,1)S(1)}, bf16[280,128]{1,0:T(8,128)(2,1)S(1)}, u32[]{:S(2)}, u32[]{:S(2)}) %collective-permute-start.4) | collective-permute-done | bytes 71712 | tf_op jit(solution)/shard_map/ppermute | solution.py:30
  58.0 1.7 %collective-permute-start.5 = (bf16[280,128]{1,0:T(8,128)(2,1)S(1)}, bf16[280,128]{1,0:T(8,128)(2,1)S(1)}, u32[]{:S(2)}, u32[]{:S(2)}) collective-permute-start(bf16[280,128]{1,0:T(8,128)(2,1)S(1)} %get-tuple-element.41), channel_id=1, source_target_pairs={{0,8},{2,10},{4,12},{6,14},{8,0},{10,2},{12,4},{14,6},{1,9},{3,11}... | collective-permute-start | bytes 215048 | tf_op jit(solution)/shard_map/ppermute | solution.py:30
  59.7 3.6 %collective-permute-done.5 = bf16[280,128]{1,0:T(8,128)(2,1)S(1)} collective-permute-done((bf16[280,128]{1,0:T(8,128)(2,1)S(1)}, bf16[280,128]{1,0:T(8,128)(2,1)S(1)}, u32[]{:S(2)}, u32[]{:S(2)}) %collective-permute-start.5) | collective-permute-done | bytes 71712 | tf_op jit(solution)/shard_map/ppermute | solution.py:30
  63.4 0.5 add_bitcast_fusion
  63.9 0.7 %fusion.12 = (f32[128,128]{1,0:T(8,128)}, f32[128,128]{1,0:T(8,128)}) fusion(f32[264,128]{1,0:T(8,128)S(1)} %maximum_add_fusion.2), kind=kLoop, calls=%fused_computation.52 | loop fusion | bytes 262144 | tf_op jit(solution)/shard_map/slice | solution.py:322
  (32 shorter events, 0.3 us)
Async XLA Ops:
  0.6 10.8 %collective-permute-start.1 = (bf16[128,1024]{1,0:T(8,128)(2,1)}, bf16[128,1024]{1,0:T(8,128)(2,1)S(1)}, u32[]{:S(2)}, u32[]{:S(2)}) collective-permute-start(bf16[128,1024]{1,0:T(8,128)(2,1)} %own_ref.3), channel_id=1, source_target_pairs={{0,4},{2,6},{4,8},{6,10},{8,12},{10,14},{1,5},{3,7},{5,9},{7,11},{... | collective-permute-start | bytes 786440 | tf_op jit(solution)/shard_map/ppermute | solution.py:25
  5.6 9.0 %collective-permute-start = (bf16[128,1024]{1,0:T(8,128)(2,1)}, bf16[128,1024]{1,0:T(8,128)(2,1)S(1)}, u32[]{:S(2)}, u32[]{:S(2)}) collective-permute-start(bf16[128,1024]{1,0:T(8,128)(2,1)} %own_ref.3), channel_id=1, source_target_pairs={{0,2},{2,4},{4,6},{6,8},{8,10},{10,12},{12,14},{1,3},{3,5},{5,7},{... | collective-permute-start | bytes 786440 | tf_op jit(solution)/shard_map/ppermute | solution.py:25
  9.1 0.7 %copy-start.9 = (s32[128]{0:T(128)S(1)}, s32[128]{0:T(128)}, u32[]{:S(2)}) copy-start(s32[128]{0:T(128)} %param.13) | copy-start | bytes 1540
  9.7 0.7 %copy-start.10 = (s32[1,8]{1,0:T(1,128)S(1)}, s32[1,8]{1,0:T(1,128)}, u32[]{:S(2)}) copy-start(s32[1,8]{1,0:T(1,128)} %param.12) | copy-start | bytes 100
  14.6 0.7 %copy-start.7 = (f32[128]{0:T(128)S(1)}, f32[128]{0:T(128)}, u32[]{:S(2)}) copy-start(f32[128]{0:T(128)} %param.18) | copy-start | bytes 1540
  14.6 0.7 %copy-start.8 = (f32[128]{0:T(128)S(1)}, f32[128]{0:T(128)}, u32[]{:S(2)}) copy-start(f32[128]{0:T(128)} %param.19) | copy-start | bytes 1540
  14.6 0.8 %copy-start.3 = (bf16[128,128]{1,0:T(8,128)(2,1)S(1)}, bf16[128,128]{1,0:T(8,128)(2,1)}, u32[]{:S(2)}) copy-start(bf16[128,128]{1,0:T(8,128)(2,1)} %w_self_ref.3) | copy-start | bytes 98308
  14.6 0.8 %copy-start.4 = (bf16[128,128]{1,0:T(8,128)(2,1)S(1)}, bf16[128,128]{1,0:T(8,128)(2,1)}, u32[]{:S(2)}) copy-start(bf16[128,128]{1,0:T(8,128)(2,1)} %w_neigh_ref.3) | copy-start | bytes 98308
  14.6 0.8 %copy-start.6 = (s32[128]{0:T(128)S(1)}, s32[128]{0:T(128)}, u32[]{:S(2)}) copy-start(s32[128]{0:T(128)} %param.14) | copy-start | bytes 1540
  15.4 1.0 %copy-start = (bf16[128,1024]{1,0:T(8,128)(2,1)S(1)}, bf16[128,1024]{1,0:T(8,128)(2,1)}, u32[]{:S(2)}) copy-start(bf16[128,1024]{1,0:T(8,128)(2,1)} %own_ref.3) | copy-start | bytes 786436
  16.3 0.9 %copy-start.2 = (bf16[1,8,128,128]{3,2,1,0:T(8,128)(2,1)S(1)}, bf16[1,8,128,128]{3,2,1,0:T(8,128)(2,1)}, u32[]{:S(2)}) copy-start(bf16[1,8,128,128]{3,2,1,0:T(8,128)(2,1)} %tiles_ref.1) | copy-start | bytes 786436
  17.3 17.6 %copy-start.1 = (bf16[128,1024]{1,0:T(8,128)(2,1)S(1)}, bf16[128,1024]{1,0:T(8,128)(2,1)}, u32[]{:S(2)}) copy-start(bf16[128,1024]{1,0:T(8,128)(2,1)} %own_ref.3) | copy-start | bytes 786436
  34.9 0.7 %copy-start.5 = (s32[64,3]{0,1:T(4,128)S(1)}, s32[64,3]{0,1:T(4,128)}, u32[]{:S(2)}) copy-start(s32[64,3]{0,1:T(4,128)} %param.15) | copy-start | bytes 2308
  37.7 4.5 %collective-permute-start.2 = (f32[264,128]{1,0:T(8,128)S(1)}, f32[264,128]{1,0:T(8,128)S(1)}, u32[]{:S(2)}, u32[]{:S(2)}) collective-permute-start(f32[264,128]{1,0:T(8,128)S(1)} %get-tuple-element.23), channel_id=1, source_target_pairs={{0,1},{1,0},{2,3},{3,2},{4,5},{5,4},{6,7},{7,6},{8,9},{9,8},{10,11... | collective-permute-start | bytes 405512 | tf_op jit(solution)/shard_map/ppermute | solution.py:30
  39.5 16.0 %collective-permute-start.6 = (bf16[128,1024]{1,0:T(8,128)(2,1)S(1)}, bf16[128,1024]{1,0:T(8,128)(2,1)S(1)}, u32[]{:S(2)}, u32[]{:S(2)}) collective-permute-start(bf16[128,1024]{1,0:T(8,128)(2,1)S(1)} %get-tuple-element.28), channel_id=1, source_target_pairs={{4,0},{6,2},{8,4},{10,6},{12,8},{14,10},{5,1},{7,3},{9,5},{11,7},{... | collective-permute-start | bytes 786440 | tf_op jit(solution)/shard_map/ppermute | solution.py:25
  40.8 14.7 %collective-permute-start.7 = (bf16[128,1024]{1,0:T(8,128)(2,1)S(1)}, bf16[128,1024]{1,0:T(8,128)(2,1)S(1)}, u32[]{:S(2)}, u32[]{:S(2)}) collective-permute-start(bf16[128,1024]{1,0:T(8,128)(2,1)S(1)} %get-tuple-element.29), channel_id=1, source_target_pairs={{2,0},{4,2},{6,4},{8,6},{10,8},{12,10},{14,12},{3,1},{5,3},{7,5},{... | collective-permute-start | bytes 786440 | tf_op jit(solution)/shard_map/ppermute | solution.py:25
  42.2 10.7 %collective-permute-start.3 = (bf16[280,128]{1,0:T(8,128)(2,1)S(1)}, bf16[280,128]{1,0:T(8,128)(2,1)S(1)}, u32[]{:S(2)}, u32[]{:S(2)}) collective-permute-start(bf16[280,128]{1,0:T(8,128)(2,1)S(1)} %get-tuple-element.46), channel_id=1, source_target_pairs={{0,2},{2,0},{4,6},{6,4},{8,10},{10,8},{12,14},{14,12},{1,3},{3,1},... | collective-permute-start | bytes 215048 | tf_op jit(solution)/shard_map/ppermute | solution.py:30
  53.1 4.7 %collective-permute-start.4 = (bf16[280,128]{1,0:T(8,128)(2,1)S(1)}, bf16[280,128]{1,0:T(8,128)(2,1)S(1)}, u32[]{:S(2)}, u32[]{:S(2)}) collective-permute-start(bf16[280,128]{1,0:T(8,128)(2,1)S(1)} %get-tuple-element.44), channel_id=1, source_target_pairs={{0,4},{2,6},{4,0},{6,2},{8,12},{10,14},{12,8},{14,10},{1,5},{3,7},... | collective-permute-start | bytes 215048 | tf_op jit(solution)/shard_map/ppermute | solution.py:30
  58.0 5.3 %collective-permute-start.5 = (bf16[280,128]{1,0:T(8,128)(2,1)S(1)}, bf16[280,128]{1,0:T(8,128)(2,1)S(1)}, u32[]{:S(2)}, u32[]{:S(2)}) collective-permute-start(bf16[280,128]{1,0:T(8,128)(2,1)S(1)} %get-tuple-element.41), channel_id=1, source_target_pairs={{0,8},{2,10},{4,12},{6,14},{8,0},{10,2},{12,4},{14,6},{1,9},{3,11}... | collective-permute-start | bytes 215048 | tf_op jit(solution)/shard_map/ppermute | solution.py:30

commit v2 on v1

--- a/solution.py
+++ b/solution.py
@@ -45,30 +45,27 @@
     return high, (value - high.astype(F32)).astype(BF16)
 
 
-def forward_kernel(
+def prepare_kernel(
     local_confs,
-    place_ref,
     ids_ref,
     own_ref,
-    near_ref,
-    far_ref,
     tiles_ref,
     degree_ref,
     segments_ref,
     w_self_ref,
-    w_neigh_ref,
     bias_ref,
-    w_out_ref,
-    mean_ref,
-    slope_ref,
-    hidden_sum_ref,
-    message_ref,
     tile_high_ref,
     tile_low_ref,
+    far_tile_ref,
+    near_tile_ref,
+    base_ref,
+    summed_ref,
+    inverse_ref,
 ):
     hid = w_self_ref.shape[0]
-    window = (far_ref, near_ref, own_ref)
-    summed = None
+    nodes = own_ref.shape[0]
+    inverse_ref[...] = 1.0 / jnp.broadcast_to(degree_ref[...], (nodes, nodes)).astype(F32).T
+    segment_rows = jnp.broadcast_to(segments_ref[...], (16, nodes)).astype(F32).astype(BF16)
     for reach in range(WINDOW):
         total = None
         for slot in range(tiles_ref.shape[1]):
@@ -78,10 +75,43 @@
         high, low = split_two(total)
         tile_high_ref[reach] = high
         tile_low_ref[reach] = low
-        panel = window[reach][...]
-        term = mm(high, panel) + mm(low, panel)
-        summed = term if summed is None else summed + term
-    inverse = 1.0 / degree_ref[...]
+        if reach < REACH:
+            message = (far_tile_ref, near_tile_ref)[reach]
+            message[:nodes] = high
+            message[nodes : 2 * nodes] = low
+            message[2 * nodes :] = segment_rows
+    own = own_ref[...]
+    summed_ref[...] = mm(tile_high_ref[REACH], own) + mm(tile_low_ref[REACH], own)
+    for conf in range(local_confs):
+        cols = slice(conf * hid, (conf + 1) * hid)
+        base_ref[:, cols] = mm(own_ref[:, cols], w_self_ref[...]) + bias_ref[...]
+
+
+def forward_kernel(
+    local_confs,
+    place_ref,
+    near_ref,
+    far_ref,
+    tile_high_ref,
+    tile_low_ref,
+    base_ref,
+    summed_ref,
+    inverse_ref,
+    segments_ref,
+    w_neigh_ref,
+    w_out_ref,
+    mean_ref,
+    slope_ref,
+    hidden_sum_ref,
+    message_ref,
+    back_ref,
+):
+    hid = w_neigh_ref.shape[0]
+    summed = summed_ref[...]
+    for reach, panel_ref in enumerate((far_ref, near_ref)):
+        panel = panel_ref[...]
+        summed = summed + (mm(tile_high_ref[reach], panel) + mm(tile_low_ref[reach], panel))
+    inverse = inverse_ref[...]
     w_out = w_out_ref[...]
     seg_iota = lax.broadcasted_iota(jnp.int32, (SEGS, segments_ref.shape[1]), 0)
     member = (segments_ref[...] == seg_iota).astype(F32)
@@ -95,10 +125,13 @@
         cols = slice(conf * hid, (conf + 1) * hid)
         mean = (summed[:, cols] * inverse).astype(BF16)
         mean_ref[:, cols] = mean
-        pre = mm(own_ref[:, cols], w_self_ref[...]) + mm(mean, w_neigh_ref[...]) + bias_ref[...]
+        pre = base_ref[:, cols] + mm(mean, w_neigh_ref[...])
         sigm = 1.0 / (1.0 + jnp.exp(-pre))
         hidden = pre * sigm
-        slope_ref[:, cols] = w_out * (sigm * (1.0 + pre * (1.0 - sigm)))
+        slope = w_out * (sigm * (1.0 + pre * (1.0 - sigm)))
+        slope_ref[:, cols] = slope
+        back = mm(slope.astype(BF16), w_neigh_ref[...], ((1,), (1,))) * inverse
+        back_ref[:, cols] = back.astype(BF16)
         high, low = split_two(hidden)
         hidden_sum = mm(member_b, high) + mm(member_b, low)
         hidden_sum_ref[:, cols] = hidden_sum
@@ -121,6 +154,7 @@
     grads_ref,
     loss_ref,
     d_pre_ref,
+    parts_ref,
 ):
     hid = grads_ref.shape[1]
     nodes = own_ref.shape[0]
@@ -141,9 +175,7 @@
     margin = jnp.maximum(0.0, 1.0 - jnp.sum(picked * signed, axis=0, keepdims=True))
     loss_ref[...] = jnp.sum(margin * margin, axis=1, keepdims=True)
     d_scores = mm_exact(seg_hot, (-2.0 * margin) * signed, ((1,), (1,))) / root
-    seg_iota = lax.broadcasted_iota(jnp.int32, (SEGS, nodes), 0)
-    member = (segments_ref[...] == seg_iota).astype(BF16)
-    member = jnp.concatenate([member, member], axis=0)
+    member = members(segments_ref[...])
     first_conf = place_ref[0] * local_confs
     grads = None
     d_bias = None
@@ -156,12 +188,9 @@
         spread = jnp.broadcast_to(column, (SEGS, hid))
         high, low = split_two(spread)
         low, last = split_two(spread - high.astype(F32))
-        d_node = mm(
-            jnp.concatenate([member, member[:SEGS]], axis=0),
-            jnp.concatenate([high, low, last], axis=0),
-            ((0,), (0,)),
-        )
-        d_pre = d_node * slope_ref[:, cols]
+        parts = jnp.concatenate([high, low, last], axis=0)
+        parts_ref[:, cols] = parts
+        d_pre = mm(member, parts, ((0,), (0,))) * slope_ref[:, cols]
         d_pre_b = d_pre.astype(BF16)
         d_pre_ref[:, cols] = d_pre_b
         rows = jnp.concatenate([own_ref[:, cols], mean_ref[:, cols]], axis=1)
@@ -176,33 +205,48 @@
     grads_ref[2 * hid :] = jnp.where(sub == 0, d_bias, 0.0) + jnp.where(sub == 1, d_out, 0.0)
 
 
+def members(segment_row):
+    seg_iota = lax.broadcasted_iota(jnp.int32, (SEGS, segment_row.shape[1]), 0)
+    member = (segment_row.astype(jnp.int32) == seg_iota).astype(F32)
+    return jnp.concatenate([member, member, member], axis=0).astype(BF16)
+
+
 def spread_kernel(
     local_confs,
+    scale,
     d_pre_ref,
+    parts_ref,
     w_self_ref,
     w_neigh_ref,
-    degree_ref,
+    inverse_ref,
     tile_high_ref,
     tile_low_ref,
-    far_ref,
-    near_ref,
-    own_ref,
+    far_back_ref,
+    near_back_ref,
+    far_tile_ref,
+    near_tile_ref,
+    node_grad_ref,
 ):
     hid = w_self_ref.shape[0]
-    inverse = 1.0 / degree_ref[...]
+    nodes = d_pre_ref.shape[0]
+    inverse = inverse_ref[...]
+    others = []
+    for back_ref, message_ref in ((far_back_ref, far_tile_ref), (near_back_ref, near_tile_ref)):
+        segment_row = message_ref[2 * nodes : 2 * nodes + 16].astype(F32)[0:1]
+        others.append((back_ref, message_ref, members(segment_row)))
     for conf in range(local_confs):
         cols = slice(conf * hid, (conf + 1) * hid)
         d_pre = d_pre_ref[:, cols]
         back = (mm(d_pre, w_neigh_ref[...], ((1,), (1,))) * inverse).astype(BF16)
-        own = mm(d_pre, w_self_ref[...], ((1,), (1,)))
-        pieces = [
-            mm(tile_high_ref[reach], back, ((0,), (0,)))
-            + mm(tile_low_ref[reach], back, ((0,), (0,)))
-            for reach in range(WINDOW)
-        ]
-        far_ref[:, cols] = pieces[0].astype(BF16)
-        near_ref[:, cols] = pieces[1].astype(BF16)
-        own_ref[:, cols] = own + pieces[2]
+        total = mm(d_pre, w_self_ref[...], ((1,), (1,)))
+        total = total + mm(tile_high_ref[REACH], back, ((0,), (0,)))
+        total = total + mm(tile_low_ref[REACH], back, ((0,), (0,)))
+        for back_ref, message_ref, member in others:
+            d_node = mm(member, parts_ref[:, cols], ((0,), (0,)))
+            back = (d_node * back_ref[:, cols].astype(F32)).astype(BF16)
+            total = total + mm(message_ref[:nodes], back, ((0,), (0,)))
+            total = total + mm(message_ref[nodes : 2 * nodes], back, ((0,), (0,)))
+        node_grad_ref[:, cols] = (total * scale).astype(BF16)
 
 
 def rounded(value):
@@ -241,80 +285,122 @@
     return total
 
 
+def shape(dims, dtype):
+    return jax.ShapeDtypeStruct(dims, dtype)
+
+
+def kernel_call(kernel, outs, scalars, name, flops, *operands):
+    moved = sum(math.prod(leaf.shape) * leaf.dtype.itemsize for leaf in operands + tuple(outs))
+    return pl.pallas_call(
+        kernel,
+        out_shape=outs,
+        in_specs=[SMEM] * scalars + [VMEM] * (len(operands) - scalars),
+        out_specs=(VMEM,) * len(outs),
+        compiler_params=pltpu.CompilerParams(vmem_limit_bytes=LIMIT),
+        cost_estimate=pl.CostEstimate(flops=flops, bytes_accessed=moved, transcendentals=0),
+        name=name,
+    )(*operands)
+
+
 def body(features, tiles, pattern, degrees, segments, pairs, w_self, w_neigh, bias, w_out):
     nodes, width = features.shape
     hid = w_self.shape[0]
     local_confs = width // hid
     rows, columns = lax.axis_size("row"), lax.axis_size("col")
     position, column = lax.axis_index("row"), lax.axis_index("col")
+    product = 2 * nodes * nodes * width
     far = shifted(features, "row", 2)
     near = shifted(features, "row", 1)
     ids = pattern - (position - REACH)
     place = jnp.stack([column, jnp.int32(local_confs * columns)]).astype(jnp.int32)
-    degree = jnp.broadcast_to(degrees.astype(F32)[:, None], (nodes, hid))
     segment_row = segments.reshape(1, nodes)
-    params = pltpu.CompilerParams(vmem_limit_bytes=LIMIT)
-    mean, slope, hidden_sum, message, tile_high, tile_low = pl.pallas_call(
-        functools.partial(forward_kernel, local_confs),
-        out_shape=(
-            jax.ShapeDtypeStruct((nodes, width), BF16),
-            jax.ShapeDtypeStruct((nodes, width), F32),
-            jax.ShapeDtypeStruct((SEGS, width), F32),
-            jax.ShapeDtypeStruct((rows * columns, SEGS, 128), F32),
-            jax.ShapeDtypeStruct((WINDOW, nodes, nodes), BF16),
-            jax.ShapeDtypeStruct((WINDOW, nodes, nodes), BF16),
-        ),
-        in_specs=[SMEM] * 2 + [VMEM] * 10,
-        out_specs=(VMEM,) * 6,
-        compiler_params=params,
-        name="forward",
-    )(
-        place,
+    wide = shape((nodes, width), F32)
+    narrow = shape((nodes, width), BF16)
+    tile_set = shape((WINDOW, nodes, nodes), BF16)
+    tile_message = shape((2 * nodes + 16, nodes), BF16)
+    tile_high, tile_low, far_tile, near_tile, base, summed, inverse = kernel_call(
+        functools.partial(prepare_kernel, local_confs),
+        (tile_set, tile_set, tile_message, tile_message, wide, wide, shape((nodes, nodes), F32)),
+        1,
+        "prepare",
+        3 * product,
         ids,
         features,
+        tiles,
+        degrees.reshape(1, nodes),
+        segment_row,
+        w_self,
+        bias.reshape(1, hid),
+    )
+    far_tile = shifted(far_tile, "row", -2)
+    near_tile = shifted(near_tile, "row", -1)
+    mean, slope, hidden_sum, message, back = kernel_call(
+        functools.partial(forward_kernel, local_confs),
+        (
+            narrow,
+            wide,
+            shape((SEGS, width), F32),
+            shape((rows * columns, SEGS, 128), F32),
+            narrow,
+        ),
+        1,
+        "forward",
+        6 * product,
+        place,
         near,
         far,
-        tiles,
-        degree,
+        tile_high,
+        tile_low,
+        base,
+        summed,
+        inverse,
         segment_row,
+        w_neigh,
+        w_out.reshape(1, hid),
+    )
+    far_back = shifted(back, "row", -2)
+    near_back = shifted(back, "row", -1)
+    received = lax.all_to_all(message, ("row", "col"), 0, 0, tiled=True)
+    main = 2 * hid
+    grads, loss, d_pre, parts = kernel_call(
+        functools.partial(gradient_kernel, local_confs),
+        (
+            shape((main + 8, hid), F32),
+            shape((1, 1), F32),
+            narrow,
+            shape((3 * SEGS, width), BF16),
+        ),
+        1,
+        "gradient",
+        3 * product,
+        place,
+        received,
+        pairs.T,
+        segment_row,
+        features,
+        mean,
+        slope,
+        hidden_sum,
+    )
+    scale = math.sqrt(nodes * rows / SEGS)
+    (node_grad,) = kernel_call(
+        functools.partial(spread_kernel, local_confs, scale),
+        (narrow,),
+        0,
+        "spread",
+        10 * product,
+        d_pre,
+        parts,
         w_self,
         w_neigh,
-        bias.reshape(1, hid),
-        w_out.reshape(1, hid),
-    )
-    received = lax.all_to_all(message, ("row", "col"), 0, 0, tiled=True)
-    main = 2 * hid
-    grads, loss, d_pre = pl.pallas_call(
-        functools.partial(gradient_kernel, local_confs),
-        out_shape=(
-            jax.ShapeDtypeStruct((main + 8, hid), F32),
-            jax.ShapeDtypeStruct((1, 1), F32),
-            jax.ShapeDtypeStruct((nodes, width), BF16),
-        ),
-        in_specs=[SMEM] + [VMEM] * 7,
-        out_specs=(VMEM,) * 3,
-        compiler_params=params,
-        name="gradient",
-    )(place, received, pairs.T, segment_row, features, mean, slope, hidden_sum)
-    far_piece, near_piece, own_piece = pl.pallas_call(
-        functools.partial(spread_kernel, local_confs),
-        out_shape=(
-            jax.ShapeDtypeStruct((nodes, width), BF16),
-            jax.ShapeDtypeStruct((nodes, width), BF16),
-            jax.ShapeDtypeStruct((nodes, width), F32),
-        ),
-        in_specs=[VMEM] * 6,
-        out_specs=(VMEM,) * 3,
-        compiler_params=params,
-        name="spread",
-    )(d_pre, w_self, w_neigh, degree, tile_high, tile_low)
-    gathered = (
-        own_piece
-        + shifted(far_piece, "row", -2).astype(F32)
-        + shifted(near_piece, "row", -1).astype(F32)
-    )
-    scale = math.sqrt(nodes * rows / SEGS)
-    node_grad = (gathered * scale).astype(BF16)
+        inverse,
+        tile_high,
+        tile_low,
+        far_back,
+        near_back,
+        far_tile,
+        near_tile,
+    )
     total = summed_over_devices(grads, main)
     return (
         loss.reshape(1),

time: 65 us -> 71.6 us (1.10)
  starting transfers between devices: 17.8 us -> 21 us
  Pallas kernels: 5.64 us -> 8.12 us
  waiting for transfers between devices: 17.3 us -> 18.4 us
  other arithmetic: 1.69 us -> 0.86 us
    ppermute x4 -> x6, waiting for transfers between devices: 4.17 us -> 12.4 us  [shifted(): lax.ppermute(value, axis, [(source, source + steps) for source in range(i...]
    ppermute x4, waiting for transfers between devices: 13.1 us -> 5.97 us  [exchanged(): lax.ppermute(value, axis, [(source, source ^ bit) for source in range(cou...]
    ppermute x4 -> x6, starting transfers between devices: 10.9 us -> 13.5 us  [shifted(): lax.ppermute(value, axis, [(source, source + steps) for source in range(i...]
    pallas_call x3 -> x4, Pallas kernels: 5.64 us -> 8.12 us  [kernel_call(): pl.pallas_call(kernel, out_shape=outs, in_specs=[SMEM] * scalars + [VMEM]...]
    convert_element_type x2 -> x0, other arithmetic: 0.83 us -> none  [the longest x1 0.83 us: body(): node_grad = (gathered * scale).astype(BF16)]
    unnamed x22 -> x24, local copies, waits for them, and re-layouts: 4.62 us -> 5.33 us
  transfers between devices with their start and end apart: 8 -> 10, of which waited for: 5 -> 5; matrix products, arithmetic and copies ran while one was open for 2% -> 0% of each run, Pallas kernels for 3% -> 5%
where the time goes in v2:
time: 71.6 us; the launch traced here: 71.1 us
  starting transfers between devices  21 us (29%)
  waiting for transfers between devices  18.4 us (26%)
  blocking collectives  15.9 us (22%)
  Pallas kernels  8.12 us (11%)
  local copies, waits for them, and re-layouts  6.05 us (8%)
  between operations  0.92 us (1%)
  other arithmetic  0.86 us (1%)
    all_to_all x1, blocking collectives, body(): received = lax.all_to_all(message, ('row', 'col'), 0, 0, tiled=True)  15.9 us
    ppermute x6, starting transfers between devices, shifted(): lax.ppermute(value, axis, [(source, source + steps) for source in range(i...  13.5 us
    ppermute x6, waiting for transfers between devices, shifted(): lax.ppermute(value, axis, [(source, source + steps) for source in range(i...  12.4 us
    pallas_call x4, Pallas kernels, kernel_call(): pl.pallas_call(kernel, out_shape=outs, in_specs=[SMEM] * scalars + [VMEM]...  8.12 us
    ppermute x4, starting transfers between devices, exchanged(): lax.ppermute(value, axis, [(source, source ^ bit) for source in range(cou...  7.43 us
    ppermute x4, waiting for transfers between devices, exchanged(): lax.ppermute(value, axis, [(source, source ^ bit) for source in range(cou...  5.97 us
    unnamed x24, local copies, waits for them, and re-layouts  5.33 us
  transfers between devices with their start and end apart: 10, of which 5 were waited for; matrix products, arithmetic and copies ran while one was open for 0% of the time, Pallas kernels for 5%

profile of v2, /device:TPU:0, one launch (start us, length us, event | category | flops | bytes accessed | tf_op | source)
XLA Modules:
  0.0 71.1 jit_solution(15939464787508225938)
XLA Ops:
  0.6 4.9 %collective-permute-start.1 = (bf16[128,1024]{1,0:T(8,128)(2,1)}, bf16[128,1024]{1,0:T(8,128)(2,1)S(1)}, u32[]{:S(2)}, u32[]{:S(2)}) collective-permute-start(bf16[128,1024]{1,0:T(8,128)(2,1)} %own_ref.3), channel_id=1, source_target_pairs={{0,4},{2,6},{4,8},{6,10},{8,12},{10,14},{1,5},{3,7},{5,9},{7,11},{... | collective-permute-start | bytes 786440 | tf_op jit(solution)/shard_map/ppermute | solution.py:25
  5.6 3.4 %collective-permute-start = (bf16[128,1024]{1,0:T(8,128)(2,1)}, bf16[128,1024]{1,0:T(8,128)(2,1)S(1)}, u32[]{:S(2)}, u32[]{:S(2)}) collective-permute-start(bf16[128,1024]{1,0:T(8,128)(2,1)} %own_ref.3), channel_id=1, source_target_pairs={{0,2},{2,4},{4,6},{6,8},{8,10},{10,12},{12,14},{1,3},{3,5},{5,7},{... | collective-permute-start | bytes 786440 | tf_op jit(solution)/shard_map/ppermute | solution.py:25
  9.0 0.0 copy-start.11
  9.0 0.6 copy-done.11
  9.7 0.0 copy-start.6
  9.7 0.0 copy-start.8
  9.7 0.0 copy-start.9
  9.7 0.6 copy-done.6
  10.3 0.0 copy-done.8
  10.3 0.0 copy-done.9
  10.4 0.0 copy-start
  10.4 0.9 %copy-done = bf16[128,1024]{1,0:T(8,128)(2,1)S(1)} copy-done((bf16[128,1024]{1,0:T(8,128)(2,1)S(1)}, bf16[128,1024]{1,0:T(8,128)(2,1)}, u32[]{:S(2)}) %copy-start) | copy-done | bytes 262168
  11.3 0.0 copy-start.2
  11.3 0.9 %copy-done.2 = bf16[1,8,128,128]{3,2,1,0:T(8,128)(2,1)S(1)} copy-done((bf16[1,8,128,128]{3,2,1,0:T(8,128)(2,1)S(1)}, bf16[1,8,128,128]{3,2,1,0:T(8,128)(2,1)}, u32[]{:S(2)}) %copy-start.2) | copy-done | bytes 262168
  12.3 0.0 copy-start.4
  12.3 0.8 %copy-done.4 = bf16[128,128]{1,0:T(8,128)(2,1)S(1)} copy-done((bf16[128,128]{1,0:T(8,128)(2,1)S(1)}, bf16[128,128]{1,0:T(8,128)(2,1)}, u32[]{:S(2)}) %copy-start.4) | copy-done | bytes 32792
  13.0 0.0 copy-start.3
  13.0 1.1 %prepare.1 = (bf16[3,128,128]{2,1,0:T(8,128)(2,1)S(1)}, bf16[3,128,128]{2,1,0:T(8,128)(2,1)S(1)}, bf16[272,128]{1,0:T(8,128)(2,1)S(1)}, bf16[272,128]{1,0:T(8,12...) custom-call(s32[1,8]{1,0:T(1,128)S(1)} %broadcast_subtract_fusion.ids_ref, ...), custom_call_target="tpu_custom_call" | custom-call | flops 100663296 | bytes 2008608 | tf_op jit(solution)/shard_map/prepare/pallas_call | solution.py:294
  14.1 0.1 pad_add_fusion.place_ref
  14.2 0.0 collective-permute-done.1.far_ref
  14.2 0.4 collective-permute-done.near_ref
  14.6 0.0 copy-start.10
  14.6 0.0 copy-done.3
  14.6 0.7 copy-done.10
  15.2 0.0 copy-start.1
  15.2 2.4 %forward.1 = (bf16[128,1024]{1,0:T(8,128)(2,1)S(1)}, f32[128,1024]{1,0:T(8,128)S(1)}, f32[8,1024]{1,0:T(8,128)S(1)}, f32[16,8,128]{2,1,0:T(8,128)S(1)}, bf16[128,1024]{1,0:T(8,128)(2,1)S(1)}) custom-call(s32[2]{0:T(128)S(1)} %pad_add_fusion.place_ref, bf16[128,1024]{1,0:T(8,128)(2,1)S(1)} %collective-permute-done.near_ref, ...), custom_call_target="tpu_custom_call" | custom-call | flops 201326592 | bytes 3015688 | tf_op jit(solution)/shard_map/forward/pallas_call | solution.py:294
  17.7 15.9 %all_to_all.5.received_ref = f32[16,8,128]{2,1,0:T(8,128)S(1)} all-to-all(f32[16,8,128]{2,1,0:T(8,128)S(1)} %get-tuple-element.27), channel_id=1, replica_groups=mesh['groups'=2,'row'=8,'col'=2] {'row','col'}, dimensions={0} | all-to-all | bytes 131072 | tf_op jit(solution)/shard_map/all_to_all | solution.py:363
  33.5 0.0 copy-start.7
  33.5 0.0 copy-done.1
  33.5 0.7 copy-done.7
  34.2 2.0 %gradient.1 = (f32[264,128]{1,0:T(8,128)S(1)}, f32[1,1]{1,0:T(1,128)}, bf16[128,1024]{1,0:T(8,128)(2,1)S(1)}, bf16[24,1024]{1,0:T(8,128)(2,1)S(1)}) custom-call(s32[2]{0:T(128)S(1)} %pad_add_fusion.place_ref, f32[16,8,128]{2,1,0:T(8,128)S(1)} %all_to_all.5.received_ref, s32[3,64]{1,0:T(4,128)S(1)} %bitcast.14, s32[1,128]{1,0:T(1,128)S(1)} %bitcast.13, ...), custom_call_target="tpu_custom_call" | custom-call | flops 100663296 | bytes 1594636 | tf_op jit(solution)/shard_map/gradient/pallas_call | solution.py:294
  36.3 0.0 collective-permute-start.2
  36.3 1.3 %collective-permute-start.8 = (bf16[272,128]{1,0:T(8,128)(2,1)S(1)}, bf16[272,128]{1,0:T(8,128)(2,1)S(1)}, u32[]{:S(2)}, u32[]{:S(2)}) collective-permute-start(bf16[272,128]{1,0:T(8,128)(2,1)S(1)} %get-tuple-element.36), channel_id=1, source_target_pairs={{4,0},{6,2},{8,4},{10,6},{12,8},{14,10},{5,1},{7,3},{9,5},{11,7},{... | collective-permute-start | bytes 208904 | tf_op jit(solution)/shard_map/ppermute | solution.py:25
  37.6 1.3 %collective-permute-start.9 = (bf16[272,128]{1,0:T(8,128)(2,1)S(1)}, bf16[272,128]{1,0:T(8,128)(2,1)S(1)}, u32[]{:S(2)}, u32[]{:S(2)}) collective-permute-start(bf16[272,128]{1,0:T(8,128)(2,1)S(1)} %get-tuple-element.37), channel_id=1, source_target_pairs={{2,0},{4,2},{6,4},{8,6},{10,8},{12,10},{14,12},{3,1},{5,3},{7,5},{... | collective-permute-start | bytes 208904 | tf_op jit(solution)/shard_map/ppermute | solution.py:25
  38.9 1.3 %collective-permute-start.7 = (bf16[128,1024]{1,0:T(8,128)(2,1)S(1)}, bf16[128,1024]{1,0:T(8,128)(2,1)S(1)}, u32[]{:S(2)}, u32[]{:S(2)}) collective-permute-start(bf16[128,1024]{1,0:T(8,128)(2,1)S(1)} %get-tuple-element.35), channel_id=1, source_target_pairs={{2,0},{4,2},{6,4},{8,6},{10,8},{12,10},{14,12},{3,1},{5,3},{7,5},{... | collective-permute-start | bytes 786440 | tf_op jit(solution)/shard_map/ppermute | solution.py:25
  40.2 1.3 %collective-permute-start.6 = (bf16[128,1024]{1,0:T(8,128)(2,1)S(1)}, bf16[128,1024]{1,0:T(8,128)(2,1)S(1)}, u32[]{:S(2)}, u32[]{:S(2)}) collective-permute-start(bf16[128,1024]{1,0:T(8,128)(2,1)S(1)} %get-tuple-element.35), channel_id=1, source_target_pairs={{4,0},{6,2},{8,4},{10,6},{12,8},{14,10},{5,1},{7,3},{9,5},{11,7},{... | collective-permute-start | bytes 786440 | tf_op jit(solution)/shard_map/ppermute | solution.py:25
  41.5 0.0 collective-permute-done.2
  41.6 3.3 %collective-permute-start.3 = (bf16[280,128]{1,0:T(8,128)(2,1)S(1)}, bf16[280,128]{1,0:T(8,128)(2,1)S(1)}, u32[]{:S(2)}, u32[]{:S(2)}) collective-permute-start(bf16[280,128]{1,0:T(8,128)(2,1)S(1)} %get-tuple-element.54), channel_id=1, source_target_pairs={{0,2},{2,0},{4,6},{6,4},{8,10},{10,8},{12,14},{14,12},{1,3},{3,1},... | collective-permute-start | bytes 215048 | tf_op jit(solution)/shard_map/ppermute | solution.py:30
  44.9 0.0 copy-start.5
  45.0 0.0 collective-permute-done.8.far_tile_ref
  45.0 0.0 collective-permute-done.9.near_tile_ref
  45.0 5.6 %collective-permute-done.7.near_back_ref = bf16[128,1024]{1,0:T(8,128)(2,1)S(1)} collective-permute-done((bf16[128,1024]{1,0:T(8,128)(2,1)S(1)}, bf16[128,1024]{1,0:T(8,128)(2,1)S(1)}, u32[]{:S(2)}, u32[]{:S(2)}) %collective-permute-start.7) | collective-permute-done | bytes 262176 | tf_op jit(solution)/shard_map/ppermute | solution.py:25
  50.5 6.4 %collective-permute-done.6.far_back_ref = bf16[128,1024]{1,0:T(8,128)(2,1)S(1)} collective-permute-done((bf16[128,1024]{1,0:T(8,128)(2,1)S(1)}, bf16[128,1024]{1,0:T(8,128)(2,1)S(1)}, u32[]{:S(2)}, u32[]{:S(2)}) %collective-permute-start.6) | collective-permute-done | bytes 262176 | tf_op jit(solution)/shard_map/ppermute | solution.py:25
  57.0 0.0 copy-done.5
  57.0 2.6 %spread.1 = bf16[128,1024]{1,0:T(8,128)(2,1)} custom-call(bf16[128,1024]{1,0:T(8,128)(2,1)S(1)} %get-tuple-element.33.d_pre_ref, bf16[24,1024]{1,0:T(8,128)(2,1)S(1)} %get-tuple-element.34.parts_ref, bf16[128,128]{1,0:T(8,128)(2,1)S(1)} %copy-done.5, bf16[128,128]{1,0:T(8,128)(2,1)S(1)} %copy-done.3, f32[128,128]{1,0:T(8,128)S(1)} %get-tuple-element.26.inverse_ref, ...), custom_call_target="tpu_custom_call" | custom-call | flops 335544320 | bytes 1564672 | tf_op jit(solution)/shard_map/spread/pallas_call | solution.py:294
  59.6 0.0 collective-permute-done.3
  59.7 2.4 %collective-permute-start.4 = (bf16[280,128]{1,0:T(8,128)(2,1)S(1)}, bf16[280,128]{1,0:T(8,128)(2,1)S(1)}, u32[]{:S(2)}, u32[]{:S(2)}) collective-permute-start(bf16[280,128]{1,0:T(8,128)(2,1)S(1)} %get-tuple-element.52), channel_id=1, source_target_pairs={{0,4},{2,6},{4,0},{6,2},{8,12},{10,14},{12,8},{14,10},{1,5},{3,7},... | collective-permute-start | bytes 215048 | tf_op jit(solution)/shard_map/ppermute | solution.py:30
  62.2 2.3 %collective-permute-done.4 = bf16[280,128]{1,0:T(8,128)(2,1)S(1)} collective-permute-done((bf16[280,128]{1,0:T(8,128)(2,1)S(1)}, bf16[280,128]{1,0:T(8,128)(2,1)S(1)}, u32[]{:S(2)}, u32[]{:S(2)}) %collective-permute-start.4) | collective-permute-done | bytes 71712 | tf_op jit(solution)/shard_map/ppermute | solution.py:30
  64.6 1.6 %collective-permute-start.5 = (bf16[280,128]{1,0:T(8,128)(2,1)S(1)}, bf16[280,128]{1,0:T(8,128)(2,1)S(1)}, u32[]{:S(2)}, u32[]{:S(2)}) collective-permute-start(bf16[280,128]{1,0:T(8,128)(2,1)S(1)} %get-tuple-element.49), channel_id=1, source_target_pairs={{0,8},{2,10},{4,12},{6,14},{8,0},{10,2},{12,4},{14,6},{1,9},{3,11}... | collective-permute-start | bytes 215048 | tf_op jit(solution)/shard_map/ppermute | solution.py:30
  66.2 3.7 %collective-permute-done.5 = bf16[280,128]{1,0:T(8,128)(2,1)S(1)} collective-permute-done((bf16[280,128]{1,0:T(8,128)(2,1)S(1)}, bf16[280,128]{1,0:T(8,128)(2,1)S(1)}, u32[]{:S(2)}, u32[]{:S(2)}) %collective-permute-start.5) | collective-permute-done | bytes 71712 | tf_op jit(solution)/shard_map/ppermute | solution.py:30
  69.9 0.5 add_bitcast_fusion
  70.5 0.7 fusion.12
  (31 shorter events, 0.3 us)
Async XLA Ops:
  0.6 13.5 %collective-permute-start.1 = (bf16[128,1024]{1,0:T(8,128)(2,1)}, bf16[128,1024]{1,0:T(8,128)(2,1)S(1)}, u32[]{:S(2)}, u32[]{:S(2)}) collective-permute-start(bf16[128,1024]{1,0:T(8,128)(2,1)} %own_ref.3), channel_id=1, source_target_pairs={{0,4},{2,6},{4,8},{6,10},{8,12},{10,14},{1,5},{3,7},{5,9},{7,11},{... | collective-permute-start | bytes 786440 | tf_op jit(solution)/shard_map/ppermute | solution.py:25
  5.6 9.0 %collective-permute-start = (bf16[128,1024]{1,0:T(8,128)(2,1)}, bf16[128,1024]{1,0:T(8,128)(2,1)S(1)}, u32[]{:S(2)}, u32[]{:S(2)}) collective-permute-start(bf16[128,1024]{1,0:T(8,128)(2,1)} %own_ref.3), channel_id=1, source_target_pairs={{0,2},{2,4},{4,6},{6,8},{8,10},{10,12},{12,14},{1,3},{3,5},{5,7},{... | collective-permute-start | bytes 786440 | tf_op jit(solution)/shard_map/ppermute | solution.py:25
  9.0 0.7 copy-start.11
  9.7 0.7 copy-start.6
  9.7 0.7 copy-start.8
  9.7 0.7 copy-start.9
  10.4 0.9 %copy-start = (bf16[128,1024]{1,0:T(8,128)(2,1)S(1)}, bf16[128,1024]{1,0:T(8,128)(2,1)}, u32[]{:S(2)}) copy-start(bf16[128,1024]{1,0:T(8,128)(2,1)} %own_ref.3) | copy-start | bytes 786436
  11.3 0.9 %copy-start.2 = (bf16[1,8,128,128]{3,2,1,0:T(8,128)(2,1)S(1)}, bf16[1,8,128,128]{3,2,1,0:T(8,128)(2,1)}, u32[]{:S(2)}) copy-start(bf16[1,8,128,128]{3,2,1,0:T(8,128)(2,1)} %tiles_ref.1) | copy-start | bytes 786436
  12.3 0.8 %copy-start.4 = (bf16[128,128]{1,0:T(8,128)(2,1)S(1)}, bf16[128,128]{1,0:T(8,128)(2,1)}, u32[]{:S(2)}) copy-start(bf16[128,128]{1,0:T(8,128)(2,1)} %w_self_ref.3) | copy-start | bytes 98308
  13.0 1.6 %copy-start.3 = (bf16[128,128]{1,0:T(8,128)(2,1)S(1)}, bf16[128,128]{1,0:T(8,128)(2,1)}, u32[]{:S(2)}) copy-start(bf16[128,128]{1,0:T(8,128)(2,1)} %w_neigh_ref.3) | copy-start | bytes 98308
  14.6 0.7 copy-start.10
  15.2 18.3 %copy-start.1 = (bf16[128,1024]{1,0:T(8,128)(2,1)S(1)}, bf16[128,1024]{1,0:T(8,128)(2,1)}, u32[]{:S(2)}) copy-start(bf16[128,1024]{1,0:T(8,128)(2,1)} %own_ref.3) | copy-start | bytes 786436
  33.5 0.7 copy-start.7
  36.3 5.3 %collective-permute-start.2 = (f32[264,128]{1,0:T(8,128)S(1)}, f32[264,128]{1,0:T(8,128)S(1)}, u32[]{:S(2)}, u32[]{:S(2)}) collective-permute-start(f32[264,128]{1,0:T(8,128)S(1)} %get-tuple-element.32), channel_id=1, source_target_pairs={{0,1},{1,0},{2,3},{3,2},{4,5},{5,4},{6,7},{7,6},{8,9},{9,8},{10,11... | collective-permute-start | bytes 405512 | tf_op jit(solution)/shard_map/ppermute | solution.py:30
  36.3 8.7 %collective-permute-start.8 = (bf16[272,128]{1,0:T(8,128)(2,1)S(1)}, bf16[272,128]{1,0:T(8,128)(2,1)S(1)}, u32[]{:S(2)}, u32[]{:S(2)}) collective-permute-start(bf16[272,128]{1,0:T(8,128)(2,1)S(1)} %get-tuple-element.36), channel_id=1, source_target_pairs={{4,0},{6,2},{8,4},{10,6},{12,8},{14,10},{5,1},{7,3},{9,5},{11,7},{... | collective-permute-start | bytes 208904 | tf_op jit(solution)/shard_map/ppermute | solution.py:25
  37.6 7.4 %collective-permute-start.9 = (bf16[272,128]{1,0:T(8,128)(2,1)S(1)}, bf16[272,128]{1,0:T(8,128)(2,1)S(1)}, u32[]{:S(2)}, u32[]{:S(2)}) collective-permute-start(bf16[272,128]{1,0:T(8,128)(2,1)S(1)} %get-tuple-element.37), channel_id=1, source_target_pairs={{2,0},{4,2},{6,4},{8,6},{10,8},{12,10},{14,12},{3,1},{5,3},{7,5},{... | collective-permute-start | bytes 208904 | tf_op jit(solution)/shard_map/ppermute | solution.py:25
  38.9 11.6 %collective-permute-start.7 = (bf16[128,1024]{1,0:T(8,128)(2,1)S(1)}, bf16[128,1024]{1,0:T(8,128)(2,1)S(1)}, u32[]{:S(2)}, u32[]{:S(2)}) collective-permute-start(bf16[128,1024]{1,0:T(8,128)(2,1)S(1)} %get-tuple-element.35), channel_id=1, source_target_pairs={{2,0},{4,2},{6,4},{8,6},{10,8},{12,10},{14,12},{3,1},{5,3},{7,5},{... | collective-permute-start | bytes 786440 | tf_op jit(solution)/shard_map/ppermute | solution.py:25
  40.2 16.7 %collective-permute-start.6 = (bf16[128,1024]{1,0:T(8,128)(2,1)S(1)}, bf16[128,1024]{1,0:T(8,128)(2,1)S(1)}, u32[]{:S(2)}, u32[]{:S(2)}) collective-permute-start(bf16[128,1024]{1,0:T(8,128)(2,1)S(1)} %get-tuple-element.35), channel_id=1, source_target_pairs={{4,0},{6,2},{8,4},{10,6},{12,8},{14,10},{5,1},{7,3},{9,5},{11,7},{... | collective-permute-start | bytes 786440 | tf_op jit(solution)/shard_map/ppermute | solution.py:25
  41.6 18.0 %collective-permute-start.3 = (bf16[280,128]{1,0:T(8,128)(2,1)S(1)}, bf16[280,128]{1,0:T(8,128)(2,1)S(1)}, u32[]{:S(2)}, u32[]{:S(2)}) collective-permute-start(bf16[280,128]{1,0:T(8,128)(2,1)S(1)} %get-tuple-element.54), channel_id=1, source_target_pairs={{0,2},{2,0},{4,6},{6,4},{8,10},{10,8},{12,14},{14,12},{1,3},{3,1},... | collective-permute-start | bytes 215048 | tf_op jit(solution)/shard_map/ppermute | solution.py:30
  44.9 12.0 %copy-start.5 = (bf16[128,128]{1,0:T(8,128)(2,1)S(1)}, bf16[128,128]{1,0:T(8,128)(2,1)}, u32[]{:S(2)}) copy-start(bf16[128,128]{1,0:T(8,128)(2,1)} %w_self_ref.3) | copy-start | bytes 98308
  59.7 4.7 %collective-permute-start.4 = (bf16[280,128]{1,0:T(8,128)(2,1)S(1)}, bf16[280,128]{1,0:T(8,128)(2,1)S(1)}, u32[]{:S(2)}, u32[]{:S(2)}) collective-permute-start(bf16[280,128]{1,0:T(8,128)(2,1)S(1)} %get-tuple-element.52), channel_id=1, source_target_pairs={{0,4},{2,6},{4,0},{6,2},{8,12},{10,14},{12,8},{14,10},{1,5},{3,7},... | collective-permute-start | bytes 215048 | tf_op jit(solution)/shard_map/ppermute | solution.py:30
  64.6 5.3 %collective-permute-start.5 = (bf16[280,128]{1,0:T(8,128)(2,1)S(1)}, bf16[280,128]{1,0:T(8,128)(2,1)S(1)}, u32[]{:S(2)}, u32[]{:S(2)}) collective-permute-start(bf16[280,128]{1,0:T(8,128)(2,1)S(1)} %get-tuple-element.49), channel_id=1, source_target_pairs={{0,8},{2,10},{4,12},{6,14},{8,0},{10,2},{12,4},{14,6},{1,9},{3,11}... | collective-permute-start | bytes 215048 | tf_op jit(solution)/shard_map/ppermute | solution.py:30

commit v3 on v2

v3 whole, which is shorter than its diff:
```python
import functools
import math

import jax
import jax.numpy as jnp
from jax import lax
from jax.experimental import pallas as pl
from jax.experimental.pallas import tpu as pltpu
from jax.sharding import PartitionSpec as P

REACH = 2
SEGS = 8
WINDOW = REACH + 1
F32 = jnp.float32
BF16 = jnp.bfloat16
HIGHEST = lax.Precision.HIGHEST
VMEM = pl.BlockSpec(memory_space=pltpu.VMEM)
SMEM = pl.BlockSpec(memory_space=pltpu.SMEM)
LIMIT = 24 << 20


def shifted(value, axis, steps):
    count = lax.axis_size(axis)
    initial, last = (max(0, -steps), min(count, count - steps))
    return lax.ppermute(value, axis, [(source, source + steps) for source in range(initial, last)])


def exchanged(value, axis, bit):
    count = lax.axis_size(axis)
    return lax.ppermute(value, axis, [(source, source ^ bit) for source in range(count)])


def mm(left, right, contract=((1,), (0,))):
    return lax.dot_general(left, right, (contract, ((), ())), preferred_element_type=F32)


def mm_exact(left, right, contract):
    return lax.dot_general(
        left, right, (contract, ((), ())), precision=HIGHEST, preferred_element_type=F32
    )


def split_two(value):
    high = value.astype(BF16)
    return high, (value - high.astype(F32)).astype(BF16)


def split_three(value):
    high, rest = value.astype(BF16), value
    rest = rest - high.astype(F32)
    middle = rest.astype(BF16)
    return high, middle, (rest - middle.astype(F32)).astype(BF16)


def iota(dims, dim):
    return lax.broadcasted_iota(jnp.int32, dims, dim)


def column_of(row, count):
    return jnp.broadcast_to(row.astype(F32), (count, row.shape[1])).T


def prepare_kernel(
    local_confs,
    pattern_ref,
    features_ref,
    tiles_ref,
    w_self_ref,
    w_neigh_ref,
    degree_ref,
    segments_ref,
    pairs_ref,
    bias_ref,
    w_out_ref,
    own_ref,
    self_ref,
    neigh_ref,
    out_ref,
    high_ref,
    low_ref,
    base_ref,
    summed_ref,
    inverse_ref,
    expand_ref,
    mask_ref,
    chosen_ref,
    stub_ref,
    tiles_buffer,
    sems,
):
    copies = [
        pltpu.make_async_copy(source, target, sems.at[i])
        for i, (source, target) in enumerate(
            (
                (tiles_ref, tiles_buffer),
                (features_ref, own_ref),
                (w_self_ref, self_ref),
                (w_neigh_ref, neigh_ref),
            )
        )
    ]
    for copy in copies:
        copy.start()
    nodes, hid = own_ref.shape[0], self_ref.shape[0]
    first_conf = lax.axis_index("col") * local_confs
    lowest = lax.axis_index("row") - REACH
    out_ref[...] = w_out_ref[...]
    inverse_ref[...] = 1.0 / column_of(degree_ref[...], nodes)
    slots = expand_ref.shape[0]
    for conf in range(local_confs):
        cols = slice(conf * hid, (conf + 1) * hid)
        chosen = iota((slots, hid), 0) // SEGS == first_conf + conf
        expand_ref[:, cols] = chosen.astype(F32).astype(BF16)
    segment_row = segments_ref[...]
    mask = (column_of(segment_row, slots).astype(jnp.int32) == iota((nodes, slots), 1) % SEGS).astype(
        F32
    )
    mask_ref[...] = mask
    slot = iota((slots, pairs_ref.shape[1]), 0)
    segment = pairs_ref[0:1, :]
    first = (pairs_ref[1:2, :] * SEGS + segment == slot).astype(F32)
    second = (pairs_ref[2:3, :] * SEGS + segment == slot).astype(F32)
    chosen_ref[...] = (first - second).astype(BF16)
    counts = jnp.sum(mask, axis=0, keepdims=True) * (first_conf == 0).astype(F32)
    sub = iota((8, slots), 0)
    stub_ref[...] = jnp.where(sub == 1, counts, 0.0) + jnp.where(
        sub == 2, segment_row.astype(F32), 0.0
    )
    copies[0].wait()
    for reach in range(WINDOW):
        total = None
        for index in range(tiles_buffer.shape[1]):
            keep = (pattern_ref[0, index] - lowest == reach).astype(F32)
            term = tiles_buffer[0, index].astype(F32) * keep
            total = term if total is None else total + term
        high, low = split_two(total)
        high_ref[reach] = high
        low_ref[reach] = low
    copies[1].wait()
    own = own_ref[...]
    summed_ref[...] = mm(high_ref[REACH], own) + mm(low_ref[REACH], own)
    copies[2].wait()
    for conf in range(local_confs):
        cols = slice(conf * hid, (conf + 1) * hid)
        base_ref[:, cols] = mm(own_ref[:, cols], self_ref[...]) + bias_ref[...]
    copies[3].wait()


def forward_kernel(
    local_confs,
    near_ref,
    far_ref,
    neigh_ref,
    out_ref,
    high_ref,
    low_ref,
    base_ref,
    summed_ref,
    inverse_ref,
    stub_ref,
    mean_ref,
    slope_ref,
    hidden_ref,
    message_ref,
    far_back_ref,
    near_back_ref,
):
    nodes, hid = base_ref.shape[0], neigh_ref.shape[0]
    summed = summed_ref[...]
    for reach, panel_ref in enumerate((far_ref, near_ref)):
        panel = panel_ref[...]
        summed = summed + (mm(high_ref[reach], panel) + mm(low_ref[reach], panel))
    inverse = inverse_ref[...]
    w_out = out_ref[...]
    segment_row = stub_ref[2:3, :].astype(jnp.int32)
    member = (segment_row == iota((SEGS, nodes), 0)).astype(F32).astype(BF16)
    first_conf = lax.axis_index("col") * local_confs
    hidden_ref[...] = jnp.zeros_like(hidden_ref)
    for conf in range(local_confs):
        cols = slice(conf * hid, (conf + 1) * hid)
        mean = (summed[:, cols] * inverse).astype(BF16)
        mean_ref[:, cols] = mean
        pre = base_ref[:, cols] + mm(mean, neigh_ref[...])
        sigm = 1.0 / (1.0 + jnp.exp(-pre))
        hidden = pre * sigm
        slope = w_out * (sigm * (1.0 + pre * (1.0 - sigm)))
        slope_ref[:, cols] = slope
        back = (mm(slope.astype(BF16), neigh_ref[...], ((1,), (1,))) * inverse).astype(BF16)
        far_back_ref[:nodes, cols] = back
        near_back_ref[:nodes, cols] = back
        high, low = split_two(hidden)
        start = pl.multiple_of((first_conf + conf) * SEGS, SEGS)
        hidden_ref[pl.ds(start, SEGS), :] = mm(member, high) + mm(member, low)
    step = nodes // local_confs
    for part in range(local_confs):
        rows = slice(part * step, (part + 1) * step)
        cols = slice(part * nodes, (part + 1) * nodes)
        far_back_ref[nodes:, cols] = high_ref[0, rows]
        near_back_ref[nodes:, cols] = high_ref[1, rows]
    scores = mm_exact(jnp.broadcast_to(w_out, (8, hid)), hidden_ref[...], ((1,), (1,)))
    message = stub_ref[...] + jnp.where(iota(scores.shape, 0) == 0, scores, 0.0)
    for peer in range(message_ref.shape[0]):
        message_ref[peer] = message


def gradient_kernel(
    local_confs,
    received_ref,
    chosen_ref,
    mask_ref,
    expand_ref,
    own_ref,
    mean_ref,
    slope_ref,
    hidden_ref,
    grads_ref,
    loss_ref,
    d_pre_ref,
    d_row_ref,
):
    hid = grads_ref.shape[1]
    total = jnp.sum(received_ref[...], axis=0)
    root = jnp.sqrt(total[1:2])
    scores = total[0:1] / root
    chosen = chosen_ref[...]

    def one_row(row, contract):
        parts = jnp.concatenate([part.astype(F32) for part in split_three(row)], axis=0)
        parts = jnp.concatenate([parts, jnp.zeros((5, row.shape[1]), F32)], axis=0).astype(BF16)
        return jnp.sum(mm(parts, chosen, contract), axis=0, keepdims=True)

    margin = jnp.maximum(0.0, 1.0 - one_row(scores, ((1,), (0,))))
    loss_ref[...] = jnp.sum(margin * margin, axis=1, keepdims=True)
    d_row = one_row(-2.0 * margin, ((1,), (1,))) / root
    d_rows = jnp.broadcast_to(d_row, d_row_ref.shape)
    d_row_ref[...] = d_rows
    factors = split_three(mask_ref[...] * d_row)
    grads = None
    d_bias = None
    for conf in range(local_confs):
        cols = slice(conf * hid, (conf + 1) * hid)
        expand = expand_ref[:, cols]
        d_node = mm(factors[0], expand) + mm(factors[1], expand) + mm(factors[2], expand)
        d_pre = d_node * slope_ref[:, cols]
        d_pre_b = d_pre.astype(BF16)
        d_pre_ref[:, cols] = d_pre_b
        rows = jnp.concatenate([own_ref[:, cols], mean_ref[:, cols]], axis=1)
        term = mm(d_pre_b, rows, ((0,), (0,)))
        grads = term if grads is None else grads + term
        d_bias = d_pre if d_bias is None else d_bias + d_pre
    grads_ref[: 2 * hid] = grads.T
    d_out = mm_exact(d_rows, hidden_ref[...], ((1,), (0,)))
    d_bias = jnp.sum(d_bias, axis=0, keepdims=True)
    sub = iota((8, hid), 0)
    grads_ref[2 * hid :] = jnp.where(sub == 0, d_bias, 0.0) + jnp.where(sub == 1, d_out, 0.0)


def spread_kernel(
    local_confs,
    columns,
    scale,
    d_pre_ref,
    d_row_ref,
    expand_ref,
    self_ref,
    neigh_ref,
    inverse_ref,
    high_ref,
    low_ref,
    far_back_ref,
    near_back_ref,
    received_ref,
    node_grad_ref,
):
    hid = self_ref.shape[0]
    nodes = d_pre_ref.shape[0]
    slots = expand_ref.shape[0]
    inverse = inverse_ref[...]
    d_row = d_row_ref[0:1, :]
    row, column = lax.axis_index("row"), lax.axis_index("col")
    step = nodes // local_confs
    others = []
    for distance, back_ref in ((2, far_back_ref), (1, near_back_ref)):
        source = jnp.minimum(row + distance, lax.axis_size("row") - 1)
        segment_row = received_ref[source * columns + column][2:3, :]
        segment = column_of(segment_row, slots).astype(jnp.int32)
        mask = (segment == iota((nodes, slots), 1) % SEGS).astype(F32)
        tile = jnp.concatenate(
            [back_ref[nodes:, part * nodes : (part + 1) * nodes] for part in range(local_confs)],
            axis=0,
        )
        others.append((back_ref, tile, split_two(mask * d_row)))
    for conf in range(local_confs):
        cols = slice(conf * hid, (conf + 1) * hid)
        d_pre = d_pre_ref[:, cols]
        back = (mm(d_pre, neigh_ref[...], ((1,), (1,))) * inverse).astype(BF16)
        total = mm(d_pre, self_ref[...], ((1,), (1,)))
        total = total + mm(high_ref[REACH], back, ((0,), (0,)))
        total = total + mm(low_ref[REACH], back, ((0,), (0,)))
        expand = expand_ref[:, cols]
        for back_ref, tile, (high, low) in others:
            d_node = mm(high, expand) + mm(low, expand)
            back = (d_node * back_ref[:nodes, cols].astype(F32)).astype(BF16)
            total = total + mm(tile, back, ((0,), (0,)))
        node_grad_ref[:, cols] = (total * scale).astype(BF16)


def rounded(value):
    return lax.reduce_precision(value, 8, 7)


def packed(total, main):
    vectors = total[main:]
    high = rounded(vectors)
    middle = rounded(vectors - high)
    last = rounded(vectors - high - middle)
    return jnp.concatenate([rounded(total[:main]), high, middle, last], axis=0).astype(BF16)


def unpacked(message, main):
    message = message.astype(F32)
    extra = (message.shape[0] - main) // 3
    parts = [message[main + i * extra : main + (i + 1) * extra] for i in range(3)]
    return jnp.concatenate([message[:main], parts[0] + parts[1] + parts[2]], axis=0)


def summed_over_devices(total, main):
    for axis in ("col", "row"):
        count = lax.axis_size(axis)
        if count & (count - 1):
            total = lax.psum(total, axis)
            continue
        if axis == "col":
            for step in range(count.bit_length() - 1):
                total = total + exchanged(total, axis, 1 << step)
            continue
        stride = 1
        while stride < count:
            message = packed(total, main)
            others = [
                exchanged(message, axis, stride * k) for k in (1, 2, 3) if stride * k < count
            ]
            if len(others) == 1:
                total = unpacked(message, main) + unpacked(others[0], main)
            else:
                total = four_summed([unpacked(m, main) for m in [message] + others])
            stride *= 4
    return total


def four_summed(parts):
    return (parts[0] + parts[1]) + (parts[2] + parts[3])


def shape(dims, dtype):
    return jax.ShapeDtypeStruct(dims, dtype)


def kernel_call(kernel, outs, spaces, name, flops, operands, scratch=()):
    moved = sum(math.prod(leaf.shape) * leaf.dtype.itemsize for leaf in tuple(operands) + tuple(outs))
    spaces = list(spaces) + [pltpu.VMEM] * (len(operands) - len(spaces))
    return pl.pallas_call(
        kernel,
        out_shape=outs,
        in_specs=[pl.BlockSpec(memory_space=space) for space in spaces],
        out_specs=(pl.BlockSpec(memory_space=pltpu.VMEM),) * len(outs),
        scratch_shapes=scratch,
        compiler_params=pltpu.CompilerParams(vmem_limit_bytes=LIMIT),
        cost_estimate=pl.CostEstimate(flops=flops, bytes_accessed=moved, transcendentals=0),
        name=name,
    )(*operands)


def body(features, tiles, pattern, degrees, segments, pairs, w_self, w_neigh, bias, w_out):
    nodes, width = features.shape
    hid = w_self.shape[0]
    local_confs = width // hid
    rows, columns = lax.axis_size("row"), lax.axis_size("col")
    product = 2 * nodes * nodes * width
    slots = local_confs * columns * SEGS
    far = shifted(features, "row", 2)
    near = shifted(features, "row", 1)
    wide = shape((nodes, width), F32)
    narrow = shape((nodes, width), BF16)
    square = shape((nodes, nodes), F32)
    weight = shape((hid, hid), BF16)
    tile_set = shape((WINDOW, nodes, nodes), BF16)
    own, self_w, neigh_w, out_w, high, low, base, summed, inverse, expand, mask, chosen, stub = (
        kernel_call(
            functools.partial(prepare_kernel, local_confs),
            (
                narrow,
                weight,
                weight,
                shape((1, hid), F32),
                tile_set,
                tile_set,
                wide,
                wide,
                square,
                shape((slots, width), BF16),
                shape((nodes, slots), F32),
                shape((slots, pairs.shape[0]), BF16),
                shape((8, slots), F32),
            ),
            [pltpu.SMEM] + [pltpu.HBM] * 4,
            "prepare",
            3 * product,
            (
                pattern,
                features,
                tiles,
                w_self,
                w_neigh,
                degrees.reshape(1, nodes),
                segments.reshape(1, nodes),
                pairs.T,
                bias.reshape(1, hid),
                w_out.reshape(1, hid),
            ),
            (pltpu.VMEM(tiles.shape, tiles.dtype), pltpu.SemaphoreType.DMA((4,))),
        )
    )
    back_message = shape((nodes + nodes // local_confs, width), BF16)
    mean, slope, hidden, message, far_back, near_back = kernel_call(
        functools.partial(forward_kernel, local_confs),
        (
            narrow,
            wide,
            shape((slots, hid), F32),
            shape((rows * columns, 8, slots), F32),
            back_message,
            back_message,
        ),
        [],
        "forward",
        6 * product,
        (near, far, neigh_w, out_w, high, low, base, summed, inverse, stub),
    )
    far_back = shifted(far_back, "row", -2)
    near_back = shifted(near_back, "row", -1)
    received = lax.all_to_all(message, ("row", "col"), 0, 0, tiled=True)
    received, far_back, near_back = lax.optimization_barrier((received, far_back, near_back))
    main = 2 * hid
    grads, loss, d_pre, d_row = kernel_call(
        functools.partial(gradient_kernel, local_confs),
        (
            shape((main + 8, hid), F32),
            shape((1, 1), F32),
            narrow,
            shape((8, slots), F32),
        ),
        [],
        "gradient",
        3 * product,
        (received, chosen, mask, expand, own, mean, slope, hidden),
    )
    scale = math.sqrt(nodes * rows / SEGS)
    (node_grad,) = kernel_call(
        functools.partial(spread_kernel, local_confs, columns, scale),
        (narrow,),
        [],
        "spread",
        10 * product,
        (
            d_pre,
            d_row,
            expand,
            self_w,
            neigh_w,
            inverse,
            high,
            low,
            far_back,
            near_back,
            received,
        ),
    )
    total = summed_over_devices(grads, main)
    return (
        loss.reshape(1),
        total[:hid],
        total[hid:main],
        total[main],
        total[main + 1],
        node_grad,
    )


def solution(mesh):
    in_specs = (
        P(("groups", "row"), "col"),
        P(("groups", "row"), None, None, None),
        P(("groups", "row"), None),
        P(("groups", "row")),
        P(("groups", "row")),
        P("groups", None),
        P(),
        P(),
        P(),
        P(),
    )
    out_specs = (
        P("groups"),
        P("groups", None),
        P("groups", None),
        P("groups"),
        P("groups"),
        P(("groups", "row"), "col"),
    )
    return jax.shard_map(body, mesh=mesh, in_specs=in_specs, out_specs=out_specs, check_vma=False)
```

time: 71.6 us -> 55.9 us (0.78)
  waiting for transfers between devices: 18.4 us -> 9.08 us
  starting transfers between devices: 21 us -> 14.9 us
  blocking collectives: 15.9 us -> 17.8 us
  local copies, waits for them, and re-layouts: 6.05 us -> 4.82 us
  Pallas kernels: 8.12 us -> 7.24 us
    ppermute x6 -> x4, waiting for transfers between devices: 12.4 us -> 0.01 us  [shifted(): lax.ppermute(value, axis, [(source, source + steps) for source in range(i...]
    ppermute x4 -> x5, starting transfers between devices: 7.43 us -> 3.93 us  [exchanged(): lax.ppermute(value, axis, [(source, source ^ bit) for source in range(cou...]
    ppermute x4 -> x5, waiting for transfers between devices: 5.97 us -> 9.07 us  [exchanged(): lax.ppermute(value, axis, [(source, source ^ bit) for source in range(cou...]
    ppermute x6 -> x4, starting transfers between devices: 13.5 us -> 10.9 us  [shifted(): lax.ppermute(value, axis, [(source, source + steps) for source in range(i...]
    all_to_all x1, blocking collectives: 15.9 us -> 17.8 us  [body(): received = lax.all_to_all(message, ('row', 'col'), 0, 0, tiled=True)]
    unnamed x24 -> x20, local copies, waits for them, and re-layouts: 5.33 us -> 4.1 us
    pallas_call x4, Pallas kernels: 8.12 us -> 7.24 us  [kernel_call(): pl.pallas_call(kernel, out_shape=outs, in_specs=[pl.BlockSpec(memory_spac...]
  transfers between devices with their start and end apart: 10 -> 9, of which waited for: 5 -> 3; matrix products, arithmetic and copies ran while one was open for 0% -> 0% of each run, Pallas kernels for 5% -> 6%
where the time goes in v3:
time: 55.9 us; the launch traced here: 55.5 us
  blocking collectives  17.8 us (32%)
  starting transfers between devices  14.9 us (27%)
  waiting for transfers between devices  9.08 us (16%)
  Pallas kernels  7.24 us (13%)
  local copies, waits for them, and re-layouts  4.82 us (9%)
  between operations  0.9 us (2%)
  other arithmetic  0.74 us (1%)
    all_to_all x1, blocking collectives, body(): received = lax.all_to_all(message, ('row', 'col'), 0, 0, tiled=True)  17.8 us
    ppermute x4, starting transfers between devices, shifted(): lax.ppermute(value, axis, [(source, source + steps) for source in range(i...  10.9 us
    ppermute x5, waiting for transfers between devices, exchanged(): lax.ppermute(value, axis, [(source, source ^ bit) for source in range(cou...  9.07 us
    pallas_call x4, Pallas kernels, kernel_call(): pl.pallas_call(kernel, out_shape=outs, in_specs=[pl.BlockSpec(memory_spac...  7.24 us
    unnamed x20, local copies, waits for them, and re-layouts  4.1 us
    ppermute x5, starting transfers between devices, exchanged(): lax.ppermute(value, axis, [(source, source ^ bit) for source in range(cou...  3.93 us
  transfers between devices with their start and end apart: 9, of which 3 were waited for; matrix products, arithmetic and copies ran while one was open for 0% of the time, Pallas kernels for 6%

profile of v3, /device:TPU:0, one launch (start us, length us, event | category | flops | bytes accessed | tf_op | source)
XLA Modules:
  0.0 55.5 jit_solution(13841112615950152477)
XLA Ops:
  0.6 4.9 %collective-permute-start = (bf16[128,1024]{1,0:T(8,128)(2,1)}, bf16[128,1024]{1,0:T(8,128)(2,1)S(1)}, u32[]{:S(2)}, u32[]{:S(2)}) collective-permute-start(bf16[128,1024]{1,0:T(8,128)(2,1)} %features_ref.1), channel_id=1, source_target_pairs={{0,2},{2,4},{4,6},{6,8},{8,10},{10,12},{12,14},{1,3},{3,5},{5,7},{... | collective-permute-start | bytes 786440 | tf_op jit(solution)/shard_map/ppermute | solution.py:25
  5.5 3.5 %collective-permute-start.1 = (bf16[128,1024]{1,0:T(8,128)(2,1)}, bf16[128,1024]{1,0:T(8,128)(2,1)S(1)}, u32[]{:S(2)}, u32[]{:S(2)}) collective-permute-start(bf16[128,1024]{1,0:T(8,128)(2,1)} %features_ref.1), channel_id=1, source_target_pairs={{0,4},{2,6},{4,8},{6,10},{8,12},{10,14},{1,5},{3,7},{5,9},{7,11},{... | collective-permute-start | bytes 786440 | tf_op jit(solution)/shard_map/ppermute | solution.py:25
  9.0 0.0 copy-start.8
  9.0 0.0 copy-start.9
  9.0 0.0 copy-start.4
  9.0 0.0 copy-start.5
  9.0 0.0 copy-start.6
  9.0 0.0 copy-start.7
  9.1 0.6 %copy-done.8 = f32[128]{0:T(128)S(1)} copy-done((f32[128]{0:T(128)S(1)}, f32[128]{0:T(128)}, u32[]{:S(2)}) %copy-start.8) | copy-done | bytes 536
  9.6 0.0 copy-done.9
  9.7 0.0 copy-done.4
  9.7 0.0 copy-done.5
  9.7 0.0 copy-done.6
  9.7 0.0 copy-done.7
  9.7 0.0 copy-start
  9.7 0.9 %copy-done = bf16[1,8,128,128]{3,2,1,0:T(8,128)(2,1)S(1)} copy-done((bf16[1,8,128,128]{3,2,1,0:T(8,128)(2,1)S(1)}, bf16[1,8,128,128]{3,2,1,0:T(8,128)(2,1)}, u32[]{:S(2)}) %copy-start) | copy-done | bytes 262168
  10.7 0.0 copy-start.1
  10.7 0.9 %copy-done.1 = bf16[128,1024]{1,0:T(8,128)(2,1)S(1)} copy-done((bf16[128,1024]{1,0:T(8,128)(2,1)S(1)}, bf16[128,1024]{1,0:T(8,128)(2,1)}, u32[]{:S(2)}) %copy-start.1) | copy-done | bytes 262168
  11.6 0.0 copy-start.2
  11.6 0.8 %copy-done.2 = bf16[128,128]{1,0:T(8,128)(2,1)S(1)} copy-done((bf16[128,128]{1,0:T(8,128)(2,1)S(1)}, bf16[128,128]{1,0:T(8,128)(2,1)}, u32[]{:S(2)}) %copy-start.2) | copy-done | bytes 32792
  12.4 0.0 copy-start.3
  12.4 0.8 %copy-done.3 = bf16[128,128]{1,0:T(8,128)(2,1)S(1)} copy-done((bf16[128,128]{1,0:T(8,128)(2,1)S(1)}, bf16[128,128]{1,0:T(8,128)(2,1)}, u32[]{:S(2)}) %copy-start.3) | copy-done | bytes 32792
  13.1 1.6 %prepare.1 = (bf16[128,1024]{1,0:T(8,128)(2,1)S(1)}, bf16[128,128]{1,0:T(8,128)(2,1)S(1)}, bf16[128,128]{1,0:T(8,128)(2,1)S(1)}, f32[1,128]{1,0:T(1,128)S(1)}, b...) custom-call(s32[1,8]{1,0:T(1,128)S(1)} %copy-done.5, ...), custom_call_target="tpu_custom_call" | custom-call | flops 100663296 | bytes 2579744 | tf_op jit(solution)/shard_map/prepare/pallas_call | solution.py:362
  14.7 0.0 collective-permute-done.near_ref
  14.7 0.0 collective-permute-done.1.far_ref
  14.7 2.2 %forward.1 = (bf16[128,1024]{1,0:T(8,128)(2,1)S(1)}, f32[128,1024]{1,0:T(8,128)S(1)}, f32[128,128]{1,0:T(8,128)S(1)}, f32[16,8,128]{2,1,0:T(8,128)S(1)}, bf16[14...) custom-call(bf16[128,1024]{1,0:T(8,128)(2,1)S(1)} %collective-permute-done.near_ref, ...), custom_call_target="tpu_custom_call" | custom-call | flops 201326592 | bytes 3379712 | tf_op jit(solution)/shard_map/forward/pallas_call | solution.py:362
  16.9 1.3 %collective-permute-start.2 = (bf16[144,1024]{1,0:T(8,128)(2,1)S(1)}, bf16[144,1024]{1,0:T(8,128)(2,1)S(1)}, u32[]{:S(2)}, u32[]{:S(2)}) collective-permute-start(bf16[144,1024]{1,0:T(8,128)(2,1)S(1)} %get-tuple-element.41), channel_id=1, source_target_pairs={{4,0},{6,2},{8,4},{10,6},{12,8},{14,10},{5,1},{7,3},{9,5},{11,7},{... | collective-permute-start | bytes 884744 | tf_op jit(solution)/shard_map/ppermute | solution.py:25
  18.3 1.3 %collective-permute-start.3 = (bf16[144,1024]{1,0:T(8,128)(2,1)S(1)}, bf16[144,1024]{1,0:T(8,128)(2,1)S(1)}, u32[]{:S(2)}, u32[]{:S(2)}) collective-permute-start(bf16[144,1024]{1,0:T(8,128)(2,1)S(1)} %get-tuple-element.42), channel_id=1, source_target_pairs={{2,0},{4,2},{6,4},{8,6},{10,8},{12,10},{14,12},{3,1},{5,3},{7,5},{... | collective-permute-start | bytes 884744 | tf_op jit(solution)/shard_map/ppermute | solution.py:25
  19.6 17.8 %all_to_all.5.received_ref = f32[16,8,128]{2,1,0:T(8,128)S(1)} all-to-all(f32[16,8,128]{2,1,0:T(8,128)S(1)} %get-tuple-element.40), channel_id=1, replica_groups=mesh['groups'=2,'row'=8,'col'=2] {'row','col'}, dimensions={0} | all-to-all | bytes 131072 | tf_op jit(solution)/shard_map/all_to_all | solution.py:442
  37.4 0.0 collective-permute-done.2.far_back_ref
  37.4 0.0 collective-permute-done.3.near_back_ref
  37.4 1.5 %gradient.1 = (f32[264,128]{1,0:T(8,128)S(1)}, f32[1,1]{1,0:T(1,128)}, bf16[128,1024]{1,0:T(8,128)(2,1)S(1)}, f32[8,128]{1,0:T(8,128)S(1)}) custom-call(f32[16,8,128]{2,1,0:T(8,128)S(1)} %all_to_all.5.received_ref, bf16[128,64]{1,0:T(8,128)(2,1)S(1)} %get-tuple-element.44.chosen_ref, f32[128,128]{1,0:T(8,128)S(1)} %get-tuple-element.45.mask_ref, ...), custom_call_target="tpu_custom_call" | custom-call | flops 100663296 | bytes 1925124 | tf_op jit(solution)/shard_map/gradient/pallas_call | solution.py:362
  38.9 0.0 collective-permute-start.4
  38.9 2.0 %spread.1 = bf16[128,1024]{1,0:T(8,128)(2,1)} custom-call(bf16[128,1024]{1,0:T(8,128)(2,1)S(1)} %get-tuple-element.53.d_pre_ref, f32[8,128]{1,0:T(8,128)S(1)} %get-tuple-element.54.d_row_ref, bf16[128,1024]{1,0:T(8,128)(2,1)S(1)} %get-tuple-element.46.expand_ref, bf16[128,128]{1,0:T(8,128)(2,1)S(1)} %get-tuple-element.55.self_ref, ...), custom_call_target="tpu_custom_call" | custom-call | flops 335544320 | bytes 1773568 | tf_op jit(solution)/shard_map/spread/pallas_call | solution.py:362
  40.9 0.0 collective-permute-done.4
  41.0 0.4 collective-permute-start.7
  41.4 1.4 %collective-permute-start.6 = (bf16[280,128]{1,0:T(8,128)(2,1)S(1)}, bf16[280,128]{1,0:T(8,128)(2,1)S(1)}, u32[]{:S(2)}, u32[]{:S(2)}) collective-permute-start(bf16[280,128]{1,0:T(8,128)(2,1)S(1)} %get-tuple-element.70), channel_id=1, source_target_pairs={{0,4},{2,6},{4,0},{6,2},{8,12},{10,14},{12,8},{14,10},{1,5},{3,7},... | collective-permute-start | bytes 215048 | tf_op jit(solution)/shard_map/ppermute | solution.py:30
  42.8 1.8 %collective-permute-start.5 = (bf16[280,128]{1,0:T(8,128)(2,1)S(1)}, bf16[280,128]{1,0:T(8,128)(2,1)S(1)}, u32[]{:S(2)}, u32[]{:S(2)}) collective-permute-start(bf16[280,128]{1,0:T(8,128)(2,1)S(1)} %get-tuple-element.70), channel_id=1, source_target_pairs={{0,2},{2,0},{4,6},{6,4},{8,10},{10,8},{12,14},{14,12},{1,3},{3,1},... | collective-permute-start | bytes 215048 | tf_op jit(solution)/shard_map/ppermute | solution.py:30
  44.6 2.3 %collective-permute-done.7 = bf16[280,128]{1,0:T(8,128)(2,1)S(1)} collective-permute-done((bf16[280,128]{1,0:T(8,128)(2,1)S(1)}, bf16[280,128]{1,0:T(8,128)(2,1)S(1)}, u32[]{:S(2)}, u32[]{:S(2)}) %collective-permute-start.7) | collective-permute-done | bytes 71712 | tf_op jit(solution)/shard_map/ppermute | solution.py:30
  47.0 1.1 %collective-permute-done.5 = bf16[280,128]{1,0:T(8,128)(2,1)S(1)} collective-permute-done((bf16[280,128]{1,0:T(8,128)(2,1)S(1)}, bf16[280,128]{1,0:T(8,128)(2,1)S(1)}, u32[]{:S(2)}, u32[]{:S(2)}) %collective-permute-start.5) | collective-permute-done | bytes 71712 | tf_op jit(solution)/shard_map/ppermute | solution.py:30
  48.1 0.0 collective-permute-done.6
  48.3 0.3 collective-permute-start.8
  48.7 5.6 %collective-permute-done.8 = bf16[280,128]{1,0:T(8,128)(2,1)S(1)} collective-permute-done((bf16[280,128]{1,0:T(8,128)(2,1)S(1)}, bf16[280,128]{1,0:T(8,128)(2,1)S(1)}, u32[]{:S(2)}, u32[]{:S(2)}) %collective-permute-start.8) | collective-permute-done | bytes 71712 | tf_op jit(solution)/shard_map/ppermute | solution.py:30
  54.3 0.5 add_bitcast_fusion
  54.8 0.7 %fusion.9 = (f32[128,128]{1,0:T(8,128)}, f32[128,128]{1,0:T(8,128)}) fusion(f32[264,128]{1,0:T(8,128)S(1)} %maximum_add_fusion.2), kind=kLoop, calls=%fused_computation.39 | loop fusion | bytes 262144 | tf_op jit(solution)/shard_map/slice | solution.py:483
  (26 shorter events, 0.3 us)
Async XLA Ops:
  0.6 14.1 %collective-permute-start = (bf16[128,1024]{1,0:T(8,128)(2,1)}, bf16[128,1024]{1,0:T(8,128)(2,1)S(1)}, u32[]{:S(2)}, u32[]{:S(2)}) collective-permute-start(bf16[128,1024]{1,0:T(8,128)(2,1)} %features_ref.1), channel_id=1, source_target_pairs={{0,2},{2,4},{4,6},{6,8},{8,10},{10,12},{12,14},{1,3},{3,5},{5,7},{... | collective-permute-start | bytes 786440 | tf_op jit(solution)/shard_map/ppermute | solution.py:25
  5.5 9.2 %collective-permute-start.1 = (bf16[128,1024]{1,0:T(8,128)(2,1)}, bf16[128,1024]{1,0:T(8,128)(2,1)S(1)}, u32[]{:S(2)}, u32[]{:S(2)}) collective-permute-start(bf16[128,1024]{1,0:T(8,128)(2,1)} %features_ref.1), channel_id=1, source_target_pairs={{0,4},{2,6},{4,8},{6,10},{8,12},{10,14},{1,5},{3,7},{5,9},{7,11},{... | collective-permute-start | bytes 786440 | tf_op jit(solution)/shard_map/ppermute | solution.py:25
  9.0 0.7 %copy-start.8 = (f32[128]{0:T(128)S(1)}, f32[128]{0:T(128)}, u32[]{:S(2)}) copy-start(f32[128]{0:T(128)} %param.18) | copy-start | bytes 1540
  9.0 0.7 %copy-start.9 = (f32[128]{0:T(128)S(1)}, f32[128]{0:T(128)}, u32[]{:S(2)}) copy-start(f32[128]{0:T(128)} %param.19) | copy-start | bytes 1540
  9.0 0.7 %copy-start.4 = (s32[64,3]{0,1:T(4,128)S(1)}, s32[64,3]{0,1:T(4,128)}, u32[]{:S(2)}) copy-start(s32[64,3]{0,1:T(4,128)} %param.15) | copy-start | bytes 2308
  9.0 0.7 %copy-start.5 = (s32[1,8]{1,0:T(1,128)S(1)}, s32[1,8]{1,0:T(1,128)}, u32[]{:S(2)}) copy-start(s32[1,8]{1,0:T(1,128)} %pattern_ref.1) | copy-start | bytes 100
  9.0 0.7 %copy-start.6 = (s32[128]{0:T(128)S(1)}, s32[128]{0:T(128)}, u32[]{:S(2)}) copy-start(s32[128]{0:T(128)} %param.13) | copy-start | bytes 1540
  9.0 0.7 %copy-start.7 = (s32[128]{0:T(128)S(1)}, s32[128]{0:T(128)}, u32[]{:S(2)}) copy-start(s32[128]{0:T(128)} %param.14) | copy-start | bytes 1540
  9.7 0.9 %copy-start = (bf16[1,8,128,128]{3,2,1,0:T(8,128)(2,1)S(1)}, bf16[1,8,128,128]{3,2,1,0:T(8,128)(2,1)}, u32[]{:S(2)}) copy-start(bf16[1,8,128,128]{3,2,1,0:T(8,128)(2,1)} %tiles_ref.1) | copy-start | bytes 786436
  10.7 0.9 %copy-start.1 = (bf16[128,1024]{1,0:T(8,128)(2,1)S(1)}, bf16[128,1024]{1,0:T(8,128)(2,1)}, u32[]{:S(2)}) copy-start(bf16[128,1024]{1,0:T(8,128)(2,1)} %features_ref.1) | copy-start | bytes 786436
  11.6 0.8 %copy-start.2 = (bf16[128,128]{1,0:T(8,128)(2,1)S(1)}, bf16[128,128]{1,0:T(8,128)(2,1)}, u32[]{:S(2)}) copy-start(bf16[128,128]{1,0:T(8,128)(2,1)} %w_self_ref.1) | copy-start | bytes 98308
  12.4 0.8 %copy-start.3 = (bf16[128,128]{1,0:T(8,128)(2,1)S(1)}, bf16[128,128]{1,0:T(8,128)(2,1)}, u32[]{:S(2)}) copy-start(bf16[128,128]{1,0:T(8,128)(2,1)} %w_neigh_ref.1) | copy-start | bytes 98308
  16.9 20.4 %collective-permute-start.2 = (bf16[144,1024]{1,0:T(8,128)(2,1)S(1)}, bf16[144,1024]{1,0:T(8,128)(2,1)S(1)}, u32[]{:S(2)}, u32[]{:S(2)}) collective-permute-start(bf16[144,1024]{1,0:T(8,128)(2,1)S(1)} %get-tuple-element.41), channel_id=1, source_target_pairs={{4,0},{6,2},{8,4},{10,6},{12,8},{14,10},{5,1},{7,3},{9,5},{11,7},{... | collective-permute-start | bytes 884744 | tf_op jit(solution)/shard_map/ppermute | solution.py:25
  18.3 19.1 %collective-permute-start.3 = (bf16[144,1024]{1,0:T(8,128)(2,1)S(1)}, bf16[144,1024]{1,0:T(8,128)(2,1)S(1)}, u32[]{:S(2)}, u32[]{:S(2)}) collective-permute-start(bf16[144,1024]{1,0:T(8,128)(2,1)S(1)} %get-tuple-element.42), channel_id=1, source_target_pairs={{2,0},{4,2},{6,4},{8,6},{10,8},{12,10},{14,12},{3,1},{5,3},{7,5},{... | collective-permute-start | bytes 884744 | tf_op jit(solution)/shard_map/ppermute | solution.py:25
  38.9 2.0 %collective-permute-start.4 = (f32[264,128]{1,0:T(8,128)S(1)}, f32[264,128]{1,0:T(8,128)S(1)}, u32[]{:S(2)}, u32[]{:S(2)}) collective-permute-start(f32[264,128]{1,0:T(8,128)S(1)} %get-tuple-element.52), channel_id=1, source_target_pairs={{0,1},{1,0},{2,3},{3,2},{4,5},{5,4},{6,7},{7,6},{8,9},{9,8},{10,11... | collective-permute-start | bytes 405512 | tf_op jit(solution)/shard_map/ppermute | solution.py:30
  41.0 6.0 %collective-permute-start.7 = (bf16[280,128]{1,0:T(8,128)(2,1)S(1)}, bf16[280,128]{1,0:T(8,128)(2,1)S(1)}, u32[]{:S(2)}, u32[]{:S(2)}) collective-permute-start(bf16[280,128]{1,0:T(8,128)(2,1)S(1)} %get-tuple-element.70), channel_id=1, source_target_pairs={{0,6},{2,4},{4,2},{6,0},{8,14},{10,12},{12,10},{14,8},{1,7},{3,5},... | collective-permute-start | bytes 215048 | tf_op jit(solution)/shard_map/ppermute | solution.py:30
  41.4 6.7 %collective-permute-start.6 = (bf16[280,128]{1,0:T(8,128)(2,1)S(1)}, bf16[280,128]{1,0:T(8,128)(2,1)S(1)}, u32[]{:S(2)}, u32[]{:S(2)}) collective-permute-start(bf16[280,128]{1,0:T(8,128)(2,1)S(1)} %get-tuple-element.70), channel_id=1, source_target_pairs={{0,4},{2,6},{4,0},{6,2},{8,12},{10,14},{12,8},{14,10},{1,5},{3,7},... | collective-permute-start | bytes 215048 | tf_op jit(solution)/shard_map/ppermute | solution.py:30
  42.8 5.3 %collective-permute-start.5 = (bf16[280,128]{1,0:T(8,128)(2,1)S(1)}, bf16[280,128]{1,0:T(8,128)(2,1)S(1)}, u32[]{:S(2)}, u32[]{:S(2)}) collective-permute-start(bf16[280,128]{1,0:T(8,128)(2,1)S(1)} %get-tuple-element.70), channel_id=1, source_target_pairs={{0,2},{2,0},{4,6},{6,4},{8,10},{10,8},{12,14},{14,12},{1,3},{3,1},... | collective-permute-start | bytes 215048 | tf_op jit(solution)/shard_map/ppermute | solution.py:30
  48.3 5.9 %collective-permute-start.8 = (bf16[280,128]{1,0:T(8,128)(2,1)S(1)}, bf16[280,128]{1,0:T(8,128)(2,1)S(1)}, u32[]{:S(2)}, u32[]{:S(2)}) collective-permute-start(bf16[280,128]{1,0:T(8,128)(2,1)S(1)} %get-tuple-element.67), channel_id=1, source_target_pairs={{0,8},{2,10},{4,12},{6,14},{8,0},{10,2},{12,4},{14,6},{1,9},{3,11}... | collective-permute-start | bytes 215048 | tf_op jit(solution)/shard_map/ppermute | solution.py:30

commit v4 on v3

--- a/solution.py
+++ b/solution.py
@@ -52,6 +52,10 @@
     return high, middle, (rest - middle.astype(F32)).astype(BF16)
 
 
+def sigmoid(value):
+    return 0.5 + 0.5 * jnp.tanh(0.5 * value)
+
+
 def iota(dims, dim):
     return lax.broadcasted_iota(jnp.int32, dims, dim)
 
@@ -60,24 +64,68 @@
     return jnp.broadcast_to(row.astype(F32), (count, row.shape[1])).T
 
 
-def prepare_kernel(
+def parcel_kernel(
     local_confs,
     pattern_ref,
     features_ref,
     tiles_ref,
-    w_self_ref,
-    w_neigh_ref,
+    degree_ref,
+    segments_ref,
+    own_ref,
+    high_ref,
+    low_ref,
+    payload_ref,
+    tiles_buffer,
+    sems,
+):
+    copies = [
+        pltpu.make_async_copy(source, target, sems.at[i])
+        for i, (source, target) in enumerate(((tiles_ref, tiles_buffer), (features_ref, own_ref)))
+    ]
+    for copy in copies:
+        copy.start()
+    nodes = own_ref.shape[0]
+    lowest = lax.axis_index("row") - REACH
+    step = nodes // local_confs
+    segment_row = segments_ref[...]
+    notes = jnp.where(iota((8, nodes), 0) == 0, segment_row, degree_ref[...])
+    notes = notes.astype(F32).astype(BF16)
+    payload_ref[nodes + WINDOW * step :] = jnp.concatenate([notes] * local_confs, axis=1)
+    copies[0].wait()
+    for reach in range(WINDOW):
+        total = None
+        for index in range(tiles_buffer.shape[1]):
+            keep = (pattern_ref[0, index] - lowest == reach).astype(F32)
+            term = tiles_buffer[0, index].astype(F32) * keep
+            total = term if total is None else total + term
+        high, low = split_two(total)
+        high_ref[reach] = high
+        low_ref[reach] = low
+        rows = slice(nodes + reach * step, nodes + (reach + 1) * step)
+        for part in range(local_confs):
+            payload_ref[rows, part * nodes : (part + 1) * nodes] = high[
+                part * step : (part + 1) * step
+            ]
+    copies[1].wait()
+    payload_ref[:nodes] = own_ref[...]
+
+
+def prepare_kernel(
+    local_confs,
+    self_w_ref,
+    neigh_w_ref,
+    own_ref,
+    high_ref,
+    low_ref,
     degree_ref,
     segments_ref,
     pairs_ref,
     bias_ref,
     w_out_ref,
-    own_ref,
     self_ref,
     neigh_ref,
     out_ref,
-    high_ref,
-    low_ref,
+    bias_out_ref,
     base_ref,
     summed_ref,
     inverse_ref,
@@ -85,26 +133,18 @@
     mask_ref,
     chosen_ref,
     stub_ref,
-    tiles_buffer,
     sems,
 ):
     copies = [
         pltpu.make_async_copy(source, target, sems.at[i])
-        for i, (source, target) in enumerate(
-            (
-                (tiles_ref, tiles_buffer),
-                (features_ref, own_ref),
-                (w_self_ref, self_ref),
-                (w_neigh_ref, neigh_ref),
-            )
-        )
+        for i, (source, target) in enumerate(((self_w_ref, self_ref), (neigh_w_ref, neigh_ref)))
     ]
     for copy in copies:
         copy.start()
     nodes, hid = own_ref.shape[0], self_ref.shape[0]
     first_conf = lax.axis_index("col") * local_confs
-    lowest = lax.axis_index("row") - REACH
     out_ref[...] = w_out_ref[...]
+    bias_out_ref[...] = bias_ref[...]
     inverse_ref[...] = 1.0 / column_of(degree_ref[...], nodes)
     slots = expand_ref.shape[0]
     for conf in range(local_confs):
@@ -112,9 +152,8 @@
         chosen = iota((slots, hid), 0) // SEGS == first_conf + conf
         expand_ref[:, cols] = chosen.astype(F32).astype(BF16)
     segment_row = segments_ref[...]
-    mask = (column_of(segment_row, slots).astype(jnp.int32) == iota((nodes, slots), 1) % SEGS).astype(
-        F32
-    )
+    segment = column_of(segment_row, slots).astype(jnp.int32)
+    mask = (segment == iota((nodes, slots), 1) % SEGS).astype(F32)
     mask_ref[...] = mask
     slot = iota((slots, pairs_ref.shape[1]), 0)
     segment = pairs_ref[0:1, :]
@@ -126,24 +165,13 @@
     stub_ref[...] = jnp.where(sub == 1, counts, 0.0) + jnp.where(
         sub == 2, segment_row.astype(F32), 0.0
     )
-    copies[0].wait()
-    for reach in range(WINDOW):
-        total = None
-        for index in range(tiles_buffer.shape[1]):
-            keep = (pattern_ref[0, index] - lowest == reach).astype(F32)
-            term = tiles_buffer[0, index].astype(F32) * keep
-            total = term if total is None else total + term
-        high, low = split_two(total)
-        high_ref[reach] = high
-        low_ref[reach] = low
-    copies[1].wait()
     own = own_ref[...]
     summed_ref[...] = mm(high_ref[REACH], own) + mm(low_ref[REACH], own)
-    copies[2].wait()
+    copies[0].wait()
     for conf in range(local_confs):
         cols = slice(conf * hid, (conf + 1) * hid)
         base_ref[:, cols] = mm(own_ref[:, cols], self_ref[...]) + bias_ref[...]
-    copies[3].wait()
+    copies[1].wait()
 
 
 def forward_kernel(
@@ -162,8 +190,6 @@
     slope_ref,
     hidden_ref,
     message_ref,
-    far_back_ref,
-    near_back_ref,
 ):
     nodes, hid = base_ref.shape[0], neigh_ref.shape[0]
     summed = summed_ref[...]
@@ -181,22 +207,13 @@
         mean = (summed[:, cols] * inverse).astype(BF16)
         mean_ref[:, cols] = mean
         pre = base_ref[:, cols] + mm(mean, neigh_ref[...])
-        sigm = 1.0 / (1.0 + jnp.exp(-pre))
+        sigm = sigmoid(pre)
         hidden = pre * sigm
         slope = w_out * (sigm * (1.0 + pre * (1.0 - sigm)))
         slope_ref[:, cols] = slope
-        back = (mm(slope.astype(BF16), neigh_ref[...], ((1,), (1,))) * inverse).astype(BF16)
-        far_back_ref[:nodes, cols] = back
-        near_back_ref[:nodes, cols] = back
         high, low = split_two(hidden)
         start = pl.multiple_of((first_conf + conf) * SEGS, SEGS)
         hidden_ref[pl.ds(start, SEGS), :] = mm(member, high) + mm(member, low)
-    step = nodes // local_confs
-    for part in range(local_confs):
-        rows = slice(part * step, (part + 1) * step)
-        cols = slice(part * nodes, (part + 1) * nodes)
-        far_back_ref[nodes:, cols] = high_ref[0, rows]
-        near_back_ref[nodes:, cols] = high_ref[1, rows]
     scores = mm_exact(jnp.broadcast_to(w_out, (8, hid)), hidden_ref[...], ((1,), (1,)))
     message = stub_ref[...] + jnp.where(iota(scores.shape, 0) == 0, scores, 0.0)
     for peer in range(message_ref.shape[0]):
@@ -255,54 +272,99 @@
     grads_ref[2 * hid :] = jnp.where(sub == 0, d_bias, 0.0) + jnp.where(sub == 1, d_out, 0.0)
 
 
-def spread_kernel(
+def own_kernel(
     local_confs,
-    columns,
-    scale,
     d_pre_ref,
-    d_row_ref,
-    expand_ref,
     self_ref,
     neigh_ref,
     inverse_ref,
     high_ref,
     low_ref,
-    far_back_ref,
-    near_back_ref,
-    received_ref,
-    node_grad_ref,
+    total_ref,
 ):
     hid = self_ref.shape[0]
-    nodes = d_pre_ref.shape[0]
-    slots = expand_ref.shape[0]
     inverse = inverse_ref[...]
-    d_row = d_row_ref[0:1, :]
-    row, column = lax.axis_index("row"), lax.axis_index("col")
-    step = nodes // local_confs
-    others = []
-    for distance, back_ref in ((2, far_back_ref), (1, near_back_ref)):
-        source = jnp.minimum(row + distance, lax.axis_size("row") - 1)
-        segment_row = received_ref[source * columns + column][2:3, :]
-        segment = column_of(segment_row, slots).astype(jnp.int32)
-        mask = (segment == iota((nodes, slots), 1) % SEGS).astype(F32)
-        tile = jnp.concatenate(
-            [back_ref[nodes:, part * nodes : (part + 1) * nodes] for part in range(local_confs)],
-            axis=0,
-        )
-        others.append((back_ref, tile, split_two(mask * d_row)))
     for conf in range(local_confs):
         cols = slice(conf * hid, (conf + 1) * hid)
         d_pre = d_pre_ref[:, cols]
         back = (mm(d_pre, neigh_ref[...], ((1,), (1,))) * inverse).astype(BF16)
         total = mm(d_pre, self_ref[...], ((1,), (1,)))
         total = total + mm(high_ref[REACH], back, ((0,), (0,)))
-        total = total + mm(low_ref[REACH], back, ((0,), (0,)))
+        total_ref[:, cols] = total + mm(low_ref[REACH], back, ((0,), (0,)))
+
+
+def later_kernel(
+    local_confs,
+    distance,
+    scale,
+    d_row_ref,
+    total_ref,
+    first_ref,
+    second_ref,
+    third_ref,
+    expand_ref,
+    self_ref,
+    neigh_ref,
+    out_ref,
+    bias_ref,
+    result_ref,
+):
+    hid = self_ref.shape[0]
+    nodes = total_ref.shape[0]
+    slots = expand_ref.shape[0]
+    step = nodes // local_confs
+    notes = third_ref[nodes + WINDOW * step :, :nodes].astype(F32)
+    segment = column_of(notes[0:1], slots).astype(jnp.int32)
+    inverse = 1.0 / jnp.maximum(column_of(notes[1:2], nodes), 1.0)
+    mask = (segment == iota((nodes, slots), 1) % SEGS).astype(F32)
+    factors = split_two(mask * d_row_ref[0:1, :])
+    tiles = []
+    for reach in range(WINDOW):
+        rows = slice(nodes + reach * step, nodes + (reach + 1) * step)
+        parts = [third_ref[rows, part * nodes : (part + 1) * nodes] for part in range(local_confs)]
+        tiles.append(jnp.concatenate(parts, axis=0))
+    w_out = out_ref[...]
+    for conf in range(local_confs):
+        cols = slice(conf * hid, (conf + 1) * hid)
+        own = third_ref[:nodes, cols]
+        summed = mm(tiles[0], first_ref[:nodes, cols]) + mm(tiles[1], second_ref[:nodes, cols])
+        mean = ((summed + mm(tiles[2], own)) * inverse).astype(BF16)
+        pre = mm(own, self_ref[...]) + mm(mean, neigh_ref[...]) + bias_ref[...]
+        sigm = sigmoid(pre)
+        slope = w_out * (sigm * (1.0 + pre * (1.0 - sigm)))
         expand = expand_ref[:, cols]
-        for back_ref, tile, (high, low) in others:
-            d_node = mm(high, expand) + mm(low, expand)
-            back = (d_node * back_ref[:nodes, cols].astype(F32)).astype(BF16)
-            total = total + mm(tile, back, ((0,), (0,)))
-        node_grad_ref[:, cols] = (total * scale).astype(BF16)
+        d_node = mm(factors[0], expand) + mm(factors[1], expand)
+        d_pre = (d_node * slope).astype(BF16)
+        back = (mm(d_pre, neigh_ref[...], ((1,), (1,))) * inverse).astype(BF16)
+        total = total_ref[:, cols] + mm(tiles[REACH - distance], back, ((0,), (0,)))
+        result_ref[:, cols] = (total * scale).astype(result_ref.dtype)
+
+
+def final_kernel(main, count, *refs):
+    hid = refs[0].shape[1]
+    parts = [ref[...].astype(F32) for ref in refs[:count]]
+    if count == 4:
+        total = (parts[0] + parts[1]) + (parts[2] + parts[3])
+    else:
+        total = parts[0] + parts[1]
+    self_ref, neigh_ref, bias_ref, out_ref = refs[count:]
+    self_ref[...] = total[:hid]
+    neigh_ref[...] = total[hid:main]
+    extra = (total.shape[0] - main) // 3
+    rows = [vectors(part, main, extra) for part in parts]
+    if count == 4:
+        row = (rows[0] + rows[1]) + (rows[2] + rows[3])
+    else:
+        row = rows[0] + rows[1]
+    bias_ref[...] = row[0:1]
+    out_ref[...] = row[1:2]
+
+
+def vectors(message, main, extra):
+    high, middle, last = (
+        message[main + i * extra : main + (i + 1) * extra] for i in range(3)
+    )
+    return high + middle + last
 
 
 def rounded(value):
@@ -324,28 +386,18 @@
     return jnp.concatenate([message[:main], parts[0] + parts[1] + parts[2]], axis=0)
 
 
-def summed_over_devices(total, main):
-    for axis in ("col", "row"):
-        count = lax.axis_size(axis)
-        if count & (count - 1):
-            total = lax.psum(total, axis)
-            continue
-        if axis == "col":
-            for step in range(count.bit_length() - 1):
-                total = total + exchanged(total, axis, 1 << step)
-            continue
-        stride = 1
-        while stride < count:
-            message = packed(total, main)
-            others = [
-                exchanged(message, axis, stride * k) for k in (1, 2, 3) if stride * k < count
-            ]
-            if len(others) == 1:
-                total = unpacked(message, main) + unpacked(others[0], main)
-            else:
-                total = four_summed([unpacked(m, main) for m in [message] + others])
-            stride *= 4
-    return total
+def row_stages(count):
+    stride = 1
+    while stride < count:
+        yield [stride * k for k in (1, 2, 3) if stride * k < count]
+        stride *= 4
+
+
+def finished(parts, main, hid):
+    outs = (shape((hid, hid), F32), shape((hid, hid), F32), shape((1, hid), F32), shape((1, hid), F32))
+    return kernel_call(
+        functools.partial(final_kernel, main, len(parts)), outs, [], "finish", 1 << 20, parts
+    )
 
 
 def four_summed(parts):
@@ -385,62 +437,86 @@
     square = shape((nodes, nodes), F32)
     weight = shape((hid, hid), BF16)
     tile_set = shape((WINDOW, nodes, nodes), BF16)
-    own, self_w, neigh_w, out_w, high, low, base, summed, inverse, expand, mask, chosen, stub = (
-        kernel_call(
-            functools.partial(prepare_kernel, local_confs),
-            (
-                narrow,
-                weight,
-                weight,
-                shape((1, hid), F32),
-                tile_set,
-                tile_set,
-                wide,
-                wide,
-                square,
-                shape((slots, width), BF16),
-                shape((nodes, slots), F32),
-                shape((slots, pairs.shape[0]), BF16),
-                shape((8, slots), F32),
-            ),
-            [pltpu.SMEM] + [pltpu.HBM] * 4,
-            "prepare",
-            3 * product,
-            (
-                pattern,
-                features,
-                tiles,
-                w_self,
-                w_neigh,
-                degrees.reshape(1, nodes),
-                segments.reshape(1, nodes),
-                pairs.T,
-                bias.reshape(1, hid),
-                w_out.reshape(1, hid),
-            ),
-            (pltpu.VMEM(tiles.shape, tiles.dtype), pltpu.SemaphoreType.DMA((4,))),
-        )
-    )
-    back_message = shape((nodes + nodes // local_confs, width), BF16)
-    mean, slope, hidden, message, far_back, near_back = kernel_call(
+    degree_row, segment_row = degrees.reshape(1, nodes), segments.reshape(1, nodes)
+    in_hbm = [
+        pltpu.with_memory_space_constraint(value, pltpu.HBM)
+        for value in (features, tiles, w_self, w_neigh)
+    ]
+    own, high, low, payload = kernel_call(
+        functools.partial(parcel_kernel, local_confs),
+        (
+            narrow,
+            tile_set,
+            tile_set,
+            shape((nodes + WINDOW * (nodes // local_confs) + 8, width), BF16),
+        ),
+        [pltpu.SMEM] + [pltpu.HBM] * 2,
+        "parcel",
+        product,
+        (pattern, in_hbm[0], in_hbm[1], degree_row, segment_row),
+        (pltpu.VMEM(tiles.shape, tiles.dtype), pltpu.SemaphoreType.DMA((2,))),
+    )
+    (
+        self_w,
+        neigh_w,
+        out_w,
+        bias_w,
+        base,
+        summed,
+        inverse,
+        expand,
+        mask,
+        chosen,
+        stub,
+    ) = kernel_call(
+        functools.partial(prepare_kernel, local_confs),
+        (
+            weight,
+            weight,
+            shape((1, hid), F32),
+            shape((1, hid), F32),
+            wide,
+            wide,
+            square,
+            shape((slots, width), BF16),
+            shape((nodes, slots), F32),
+            shape((slots, pairs.shape[0]), BF16),
+            shape((8, slots), F32),
+        ),
+        [pltpu.HBM] * 2,
+        "prepare",
+        3 * product,
+        (
+            in_hbm[2],
+            in_hbm[3],
+            own,
+            high,
+            low,
+            degree_row,
+            segment_row,
+            pairs.T,
+            bias.reshape(1, hid),
+            w_out.reshape(1, hid),
+        ),
+        (pltpu.SemaphoreType.DMA((2,)),),
+    )
+    next_one = shifted(payload, "row", -1)
+    mean, slope, hidden, message = kernel_call(
         functools.partial(forward_kernel, local_confs),
         (
             narrow,
             wide,
             shape((slots, hid), F32),
             shape((rows * columns, 8, slots), F32),
-            back_message,
-            back_message,
         ),
         [],
         "forward",
         6 * product,
         (near, far, neigh_w, out_w, high, low, base, summed, inverse, stub),
     )
-    far_back = shifted(far_back, "row", -2)
-    near_back = shifted(near_back, "row", -1)
+    next_two = shifted(payload, "row", -2)
     received = lax.all_to_all(message, ("row", "col"), 0, 0, tiled=True)
-    received, far_back, near_back = lax.optimization_barrier((received, far_back, near_back))
+    received, next_one, next_two = lax.optimization_barrier((received, next_one, next_two))
     main = 2 * hid
     grads, loss, d_pre, d_row = kernel_call(
         functools.partial(gradient_kernel, local_confs),
@@ -456,33 +532,49 @@
         (received, chosen, mask, expand, own, mean, slope, hidden),
     )
     scale = math.sqrt(nodes * rows / SEGS)
-    (node_grad,) = kernel_call(
-        functools.partial(spread_kernel, local_confs, columns, scale),
-        (narrow,),
+    (node_total,) = kernel_call(
+        functools.partial(own_kernel, local_confs),
+        (wide,),
         [],
-        "spread",
-        10 * product,
-        (
-            d_pre,
-            d_row,
-            expand,
-            self_w,
-            neigh_w,
-            inverse,
-            high,
-            low,
-            far_back,
-            near_back,
-            received,
-        ),
-    )
-    total = summed_over_devices(grads, main)
+        "own",
+        4 * product,
+        (d_pre, self_w, neigh_w, inverse, high, low),
+    )
+
+    def later(distance, d_row, node_total, panels, out, factor):
+        (result,) = kernel_call(
+            functools.partial(later_kernel, local_confs, distance, factor),
+            (out,),
+            [],
+            f"later{distance}",
+            10 * product,
+            (d_row, node_total, *panels, expand, self_w, neigh_w, out_w, bias_w),
+        )
+        return result
+
+    total = grads
+    for step in range(columns.bit_length() - 1):
+        total = total + exchanged(total, "col", 1 << step)
+    total, d_row, node_total = lax.optimization_barrier((total, d_row, node_total))
+    node_total = later(1, d_row, node_total, (near, own, next_one), wide, 1.0)
+    stages = list(row_stages(rows))
+    for index, stage in enumerate(stages):
+        packet = packed(total, main)
+        parts = [packet] + [exchanged(packet, "row", bits) for bits in stage]
+        if index == len(stages) - 1:
+            break
+        total = [unpacked(part, main) for part in parts]
+        total = four_summed(total) if len(total) == 4 else total[0] + total[1]
+        if index == len(stages) - 2:
+            total, d_row, node_total = lax.optimization_barrier((total, d_row, node_total))
+    grad_self, grad_neigh, grad_bias, grad_out = finished(parts, main, hid)
+    node_grad = later(2, d_row, node_total, (own, next_one, next_two), narrow, scale)
     return (
         loss.reshape(1),
-        total[:hid],
-        total[hid:main],
-        total[main],
-        total[main + 1],
+        grad_self,
+        grad_neigh,
+        grad_bias.reshape(hid),
+        grad_out.reshape(hid),
         node_grad,
     )
 

time: 55.9 us -> 51.9 us (0.928)
  blocking collectives: 17.8 us -> 0 us
  Pallas kernels: 7.24 us -> 15.2 us
  starting transfers between devices: 14.9 us -> 22.8 us
  local copies, waits for them, and re-layouts: 4.82 us -> 1.37 us
  waiting for transfers between devices: 9.08 us -> 11.1 us
  other arithmetic: 0.74 us -> 0.17 us
    all_to_all x1 -> x0, blocking collectives: 17.8 us -> none  [body(): received = lax.all_to_all(message, ('row', 'col'), 0, 0, tiled=True)]
    all_to_all x0 -> x1, starting transfers between devices: none -> 8.13 us  [body(): received = lax.all_to_all(message, ('row', 'col'), 0, 0, tiled=True)]
    pallas_call x4 -> x8, Pallas kernels: 7.24 us -> 15.2 us  [kernel_call(): pl.pallas_call(kernel, out_shape=outs, in_specs=[pl.BlockSpec(memory_spac...]
    ppermute x4, waiting for transfers between devices: 0.01 us -> 6.41 us  [shifted(): lax.ppermute(value, axis, [(source, source + steps) for source in range(i...]
    ppermute x5, waiting for transfers between devices: 9.07 us -> 3.1 us  [exchanged(): lax.ppermute(value, axis, [(source, source ^ bit) for source in range(cou...]
    unnamed x20 -> x12, local copies, waits for them, and re-layouts: 4.1 us -> 1.33 us
    all_to_all x0 -> x1, waiting for transfers between devices: none -> 1.57 us  [body(): received = lax.all_to_all(message, ('row', 'col'), 0, 0, tiled=True)]
    slice x1 -> x0, local copies, waits for them, and re-layouts: 0.66 us -> none  [body(): total[hid:main]]
  transfers between devices with their start and end apart: 9 -> 10, of which waited for: 3 -> 6; matrix products, arithmetic and copies ran while one was open for 0% -> 0% of each run, Pallas kernels for 6% -> 25%
where the time goes in v4:
time: 51.9 us; the launch traced here: 51.6 us
  starting transfers between devices  22.8 us (44%)
  Pallas kernels  15.2 us (29%)
  waiting for transfers between devices  11.1 us (21%)
  local copies, waits for them, and re-layouts  1.37 us (3%)
  between operations  0.91 us (2%)
    pallas_call x8, Pallas kernels, kernel_call(): pl.pallas_call(kernel, out_shape=outs, in_specs=[pl.BlockSpec(memory_spac...  15.2 us
    ppermute x4, starting transfers between devices, shifted(): lax.ppermute(value, axis, [(source, source + steps) for source in range(i...  10.9 us
    all_to_all x1, starting transfers between devices, body(): received = lax.all_to_all(message, ('row', 'col'), 0, 0, tiled=True)  8.13 us
    ppermute x4, waiting for transfers between devices, shifted(): lax.ppermute(value, axis, [(source, source + steps) for source in range(i...  6.41 us
    ppermute x5, starting transfers between devices, exchanged(): lax.ppermute(value, axis, [(source, source ^ bit) for source in range(cou...  3.74 us
    ppermute x5, waiting for transfers between devices, exchanged(): lax.ppermute(value, axis, [(source, source ^ bit) for source in range(cou...  3.1 us
    all_to_all x1, waiting for transfers between devices, body(): received = lax.all_to_all(message, ('row', 'col'), 0, 0, tiled=True)  1.57 us
    unnamed x12, local copies, waits for them, and re-layouts  1.33 us
  transfers between devices with their start and end apart: 10, of which 6 were waited for; matrix products, arithmetic and copies ran while one was open for 0% of the time, Pallas kernels for 25%

profile of v4, /device:TPU:0, one launch (start us, length us, event | category | flops | bytes accessed | tf_op | source)
XLA Modules:
  0.0 51.6 jit_solution(6499633731531935364)
XLA Ops:
  0.6 4.9 %collective-permute-start = (bf16[128,1024]{1,0:T(8,128)(2,1)}, bf16[128,1024]{1,0:T(8,128)(2,1)S(1)}, u32[]{:S(2)}, u32[]{:S(2)}) collective-permute-start(bf16[128,1024]{1,0:T(8,128)(2,1)} %features_ref.1), channel_id=1, source_target_pairs={{0,2},{2,4},{4,6},{6,8},{8,10},{10,12},{12,14},{1,3},{3,5},{5,7},{... | collective-permute-start | bytes 786440 | tf_op jit(solution)/shard_map/ppermute | solution.py:25
  5.5 3.5 %collective-permute-start.1 = (bf16[128,1024]{1,0:T(8,128)(2,1)}, bf16[128,1024]{1,0:T(8,128)(2,1)S(1)}, u32[]{:S(2)}, u32[]{:S(2)}) collective-permute-start(bf16[128,1024]{1,0:T(8,128)(2,1)} %features_ref.1), channel_id=1, source_target_pairs={{0,4},{2,6},{4,8},{6,10},{8,12},{10,14},{1,5},{3,7},{5,9},{7,11},{... | collective-permute-start | bytes 786440 | tf_op jit(solution)/shard_map/ppermute | solution.py:25
  9.0 0.0 copy-start.1
  9.0 0.0 copy-start.2
  9.0 0.0 copy-start.3
  9.0 0.6 %copy-done.1 = s32[128]{0:T(128)S(1)} copy-done((s32[128]{0:T(128)S(1)}, s32[128]{0:T(128)}, u32[]{:S(2)}) %copy-start.1) | copy-done | bytes 536
  9.6 0.0 copy-done.2
  9.7 0.0 copy-done.3
  9.7 1.7 %parcel.1 = (bf16[128,1024]{1,0:T(8,128)(2,1)S(1)}, bf16[3,128,128]{2,1,0:T(8,128)(2,1)S(1)}, bf16[3,128,128]{2,1,0:T(8,128)(2,1)S(1)}, bf16[184,1024]{1,0:T(8,128)(2,1)S(1)}) custom-call(s32[1,8]{1,0:T(1,128)S(1)} %copy-done.3, bf16[128,1024]{1,0:T(8,128)(2,1)} %features_ref.1, bf16[1,8,128,128]{3,2,1,0:T(8,128)(2,1)} %tiles_ref.1, s32[1,128]{1,0:T(1,128)S(1)} %bitcast.9, ...), custom_call_target="tpu_custom_call" | custom-call | flops 33554432 | bytes 1360928 | tf_op jit(solution)/shard_map/parcel/pallas_call | solution.py:414
  11.4 1.3 %collective-permute-start.2 = (bf16[184,1024]{1,0:T(8,128)(2,1)S(1)}, bf16[184,1024]{1,0:T(8,128)(2,1)S(1)}, u32[]{:S(2)}, u32[]{:S(2)}) collective-permute-start(bf16[184,1024]{1,0:T(8,128)(2,1)S(1)} %get-tuple-element.52), channel_id=1, source_target_pairs={{2,0},{4,2},{6,4},{8,6},{10,8},{12,10},{14,12},{3,1},{5,3},{7,5},{... | collective-permute-start | bytes 1130504 | tf_op jit(solution)/shard_map/ppermute | solution.py:25
  12.7 1.3 %collective-permute-start.3 = (bf16[184,1024]{1,0:T(8,128)(2,1)S(1)}, bf16[184,1024]{1,0:T(8,128)(2,1)S(1)}, u32[]{:S(2)}, u32[]{:S(2)}) collective-permute-start(bf16[184,1024]{1,0:T(8,128)(2,1)S(1)} %get-tuple-element.52), channel_id=1, source_target_pairs={{4,0},{6,2},{8,4},{10,6},{12,8},{14,10},{5,1},{7,3},{9,5},{11,7},{... | collective-permute-start | bytes 1130504 | tf_op jit(solution)/shard_map/ppermute | solution.py:25
  14.0 0.0 copy-start
  14.0 0.0 copy-start.4
  14.0 0.0 copy-start.5
  14.0 0.6 %copy-done = s32[64,3]{0,1:T(4,128)S(1)} copy-done((s32[64,3]{0,1:T(4,128)S(1)}, s32[64,3]{0,1:T(4,128)}, u32[]{:S(2)}) %copy-start) | copy-done | bytes 792
  14.7 0.0 copy-done.4
  14.7 0.0 copy-done.5
  14.7 1.2 %prepare.1 = (bf16[128,128]{1,0:T(8,128)(2,1)S(1)}, bf16[128,128]{1,0:T(8,128)(2,1)S(1)}, f32[1,128]{1,0:T(1,128)S(1)}, f32[1,128]{1,0:T(1,128)S(1)}, f32[128,10...) custom-call(bf16[128,128]{1,0:T(8,128)(2,1)} %self_w_ref.1, ...), custom_call_target="tpu_custom_call" | custom-call | flops 100663296 | bytes 2055936 | tf_op jit(solution)/shard_map/prepare/pallas_call | solution.py:414
  15.9 0.0 collective-permute-done.near_ref.first_ref
  15.9 0.0 collective-permute-done.1.far_ref
  15.9 2.4 %forward.1 = (bf16[128,1024]{1,0:T(8,128)(2,1)S(1)}, f32[128,1024]{1,0:T(8,128)S(1)}, f32[128,128]{1,0:T(8,128)S(1)}, f32[16,8,128]{2,1,0:T(8,128)}) custom-call(bf16[128,1024]{1,0:T(8,128)(2,1)S(1)} %collective-permute-done.near_ref.first_ref, bf16[128,1024]{1,0:T(8,128)(2,1)S(1)} %collective-permute-done.1.far_ref, ...), custom_call_target="tpu_custom_call" | custom-call | flops 201326592 | bytes 2789888 | tf_op jit(solution)/shard_map/forward/pallas_call | solution.py:414
  18.3 8.1 %all-to-all-start = ((f32[16,8,128]{2,1,0:T(8,128)}), f32[16,8,128]{2,1,0:T(8,128)S(1)}, u32[]{:S(2)}, u32[]{:S(2)}) async-start(f32[16,8,128]{2,1,0:T(8,128)} %get-tuple-element.51), calls=%async_computation | async-start | bytes 131072 | tf_op jit(solution)/shard_map/all_to_all | solution.py:518
  26.4 0.0 collective-permute-done.2.third_ref.second_ref
  26.4 6.4 %collective-permute-done.3.third_ref = bf16[184,1024]{1,0:T(8,128)(2,1)S(1)} collective-permute-done((bf16[184,1024]{1,0:T(8,128)(2,1)S(1)}, bf16[184,1024]{1,0:T(8,128)(2,1)S(1)}, u32[]{:S(2)}, u32[]{:S(2)}) %collective-permute-start.3) | collective-permute-done | bytes 376864 | tf_op jit(solution)/shard_map/ppermute | solution.py:25
  32.8 1.6 %all-to-all-done.received_ref = f32[16,8,128]{2,1,0:T(8,128)S(1)} async-done(((f32[16,8,128]{2,1,0:T(8,128)}), f32[16,8,128]{2,1,0:T(8,128)S(1)}, u32[]{:S(2)}, u32[]{:S(2)}) %all-to-all-start) | async-done | bytes 65568 | tf_op jit(solution)/shard_map/all_to_all | solution.py:518
  34.4 1.5 %gradient.1 = (f32[264,128]{1,0:T(8,128)S(1)}, f32[1,1]{1,0:T(1,128)}, bf16[128,1024]{1,0:T(8,128)(2,1)S(1)}, f32[8,128]{1,0:T(8,128)S(1)}) custom-call(f32[16,8,128]{2,1,0:T(8,128)S(1)} %all-to-all-done.received_ref, bf16[128,64]{1,0:T(8,128)(2,1)S(1)} %get-tuple-element.54.chosen_ref, f32[128,128]{1,0:T(8,128)S(1)} %get-tuple-element.55.mask_ref, ...), custom_call_target="tpu_custom_call" | custom-call | flops 100663296 | bytes 1925124 | tf_op jit(solution)/shard_map/gradient/pallas_call | solution.py:414
  35.9 0.1 collective-permute-start.4
  36.0 1.1 %own.1.total_ref = f32[128,1024]{1,0:T(8,128)S(1)} custom-call(bf16[128,1024]{1,0:T(8,128)(2,1)S(1)} %get-tuple-element.63.d_pre_ref, bf16[128,128]{1,0:T(8,128)(2,1)S(1)} %get-tuple-element.64.self_ref, bf16[128,128]{1,0:T(8,128)(2,1)S(1)} %get-tuple-element.45.neigh_ref, f32[128,128]{1,0:T(8,128)S(1)} %get-tuple-element.49.inverse_ref, ...), custom_call_target="tpu_custom_call" | custom-call | flops 134217728 | bytes 1114112 | tf_op jit(solution)/shard_map/own/pallas_call | solution.py:414
  37.1 0.1 collective-permute-done.4
  37.3 1.7 %collective-permute-start.7 = (bf16[280,128]{1,0:T(8,128)(2,1)S(1)}, bf16[280,128]{1,0:T(8,128)(2,1)S(1)}, u32[]{:S(2)}, u32[]{:S(2)}) collective-permute-start(bf16[280,128]{1,0:T(8,128)(2,1)S(1)} %get-tuple-element.84), channel_id=1, source_target_pairs={{0,6},{2,4},{4,2},{6,0},{8,14},{10,12},{12,10},{14,8},{1,7},{3,5},... | collective-permute-start | bytes 215048 | tf_op jit(solution)/shard_map/ppermute | solution.py:30
  39.0 1.4 %collective-permute-start.6 = (bf16[280,128]{1,0:T(8,128)(2,1)S(1)}, bf16[280,128]{1,0:T(8,128)(2,1)S(1)}, u32[]{:S(2)}, u32[]{:S(2)}) collective-permute-start(bf16[280,128]{1,0:T(8,128)(2,1)S(1)} %get-tuple-element.84), channel_id=1, source_target_pairs={{0,4},{2,6},{4,0},{6,2},{8,12},{10,14},{12,8},{14,10},{1,5},{3,7},... | collective-permute-start | bytes 215048 | tf_op jit(solution)/shard_map/ppermute | solution.py:30
  40.3 0.5 %collective-permute-start.5 = (bf16[280,128]{1,0:T(8,128)(2,1)S(1)}, bf16[280,128]{1,0:T(8,128)(2,1)S(1)}, u32[]{:S(2)}, u32[]{:S(2)}) collective-permute-start(bf16[280,128]{1,0:T(8,128)(2,1)S(1)} %get-tuple-element.84), channel_id=1, source_target_pairs={{0,2},{2,0},{4,6},{6,4},{8,10},{10,8},{12,14},{14,12},{1,3},{3,1},... | collective-permute-start | bytes 215048 | tf_op jit(solution)/shard_map/ppermute | solution.py:30
  40.9 3.0 %later1.1.total_ref = f32[128,1024]{1,0:T(8,128)S(1)} custom-call(f32[8,128]{1,0:T(8,128)S(1)} %get-tuple-element.75.d_row_ref, f32[128,1024]{1,0:T(8,128)S(1)} %own.1.total_ref, bf16[128,1024]{1,0:T(8,128)(2,1)S(1)} %collective-permute-done.near_ref.first_ref, bf16[128,1024]{1,0:T(8,128)(2,1)S(1)} %get-tuple-element.42.own_ref.second_ref.first_ref, ...), custom_call_target="tpu_custom_call" | custom-call | flops 335544320 | bytes 2282496 | tf_op jit(solution)/shard_map/later1/pallas_call | solution.py:414
  43.9 0.0 collective-permute-done.7
  43.9 0.3 collective-permute-done.6
  44.3 0.4 collective-permute-done.5
  44.8 0.1 collective-permute-start.8
  44.9 3.7 %later2.1 = bf16[128,1024]{1,0:T(8,128)(2,1)} custom-call(f32[8,128]{1,0:T(8,128)S(1)} %get-tuple-element.75.d_row_ref, f32[128,1024]{1,0:T(8,128)S(1)} %later1.1.total_ref, bf16[128,1024]{1,0:T(8,128)(2,1)S(1)} %get-tuple-element.42.own_ref.second_ref.first_ref, bf16[184,1024]{1,0:T(8,128)(2,1)S(1)} %collective-permute-done.2.third_ref.second_ref, ...), custom_call_target="tpu_custom_call" | custom-call | flops 335544320 | bytes 2135040 | tf_op jit(solution)/shard_map/later2/pallas_call | solution.py:414
  48.6 2.3 %collective-permute-done.8.refs_1_ = bf16[280,128]{1,0:T(8,128)(2,1)S(1)} collective-permute-done((bf16[280,128]{1,0:T(8,128)(2,1)S(1)}, bf16[280,128]{1,0:T(8,128)(2,1)S(1)}, u32[]{:S(2)}, u32[]{:S(2)}) %collective-permute-start.8) | collective-permute-done | bytes 71712 | tf_op jit(solution)/shard_map/ppermute | solution.py:30
  50.9 0.7 %finish.1 = (f32[128,128]{1,0:T(8,128)}, f32[128,128]{1,0:T(8,128)}, f32[1,128]{1,0:T(1,128)}, f32[1,128]{1,0:T(1,128)}) custom-call(bf16[280,128]{1,0:T(8,128)(2,1)S(1)} %pad_maximum_fusion.1.refs_0_, bf16[280,128]{1,0:T(8,128)(2,1)S(1)} %collective-permute-done.8.refs_1_), custom_call_target="tpu_custom_call" | custom-call | flops 1048576 | bytes 275456 | tf_op jit(solution)/shard_map/finish/pallas_call | solution.py:414
  (19 shorter events, 0.2 us)
Async XLA Ops:
  0.6 15.3 %collective-permute-start = (bf16[128,1024]{1,0:T(8,128)(2,1)}, bf16[128,1024]{1,0:T(8,128)(2,1)S(1)}, u32[]{:S(2)}, u32[]{:S(2)}) collective-permute-start(bf16[128,1024]{1,0:T(8,128)(2,1)} %features_ref.1), channel_id=1, source_target_pairs={{0,2},{2,4},{4,6},{6,8},{8,10},{10,12},{12,14},{1,3},{3,5},{5,7},{... | collective-permute-start | bytes 786440 | tf_op jit(solution)/shard_map/ppermute | solution.py:25
  5.5 10.4 %collective-permute-start.1 = (bf16[128,1024]{1,0:T(8,128)(2,1)}, bf16[128,1024]{1,0:T(8,128)(2,1)S(1)}, u32[]{:S(2)}, u32[]{:S(2)}) collective-permute-start(bf16[128,1024]{1,0:T(8,128)(2,1)} %features_ref.1), channel_id=1, source_target_pairs={{0,4},{2,6},{4,8},{6,10},{8,12},{10,14},{1,5},{3,7},{5,9},{7,11},{... | collective-permute-start | bytes 786440 | tf_op jit(solution)/shard_map/ppermute | solution.py:25
  9.0 0.7 %copy-start.1 = (s32[128]{0:T(128)S(1)}, s32[128]{0:T(128)}, u32[]{:S(2)}) copy-start(s32[128]{0:T(128)} %param.13) | copy-start | bytes 1540
  9.0 0.7 %copy-start.2 = (s32[128]{0:T(128)S(1)}, s32[128]{0:T(128)}, u32[]{:S(2)}) copy-start(s32[128]{0:T(128)} %param.14) | copy-start | bytes 1540
  9.0 0.7 %copy-start.3 = (s32[1,8]{1,0:T(1,128)S(1)}, s32[1,8]{1,0:T(1,128)}, u32[]{:S(2)}) copy-start(s32[1,8]{1,0:T(1,128)} %pattern_ref.1) | copy-start | bytes 100
  11.4 15.0 %collective-permute-start.2 = (bf16[184,1024]{1,0:T(8,128)(2,1)S(1)}, bf16[184,1024]{1,0:T(8,128)(2,1)S(1)}, u32[]{:S(2)}, u32[]{:S(2)}) collective-permute-start(bf16[184,1024]{1,0:T(8,128)(2,1)S(1)} %get-tuple-element.52), channel_id=1, source_target_pairs={{2,0},{4,2},{6,4},{8,6},{10,8},{12,10},{14,12},{3,1},{5,3},{7,5},{... | collective-permute-start | bytes 1130504 | tf_op jit(solution)/shard_map/ppermute | solution.py:25
  12.7 20.1 %collective-permute-start.3 = (bf16[184,1024]{1,0:T(8,128)(2,1)S(1)}, bf16[184,1024]{1,0:T(8,128)(2,1)S(1)}, u32[]{:S(2)}, u32[]{:S(2)}) collective-permute-start(bf16[184,1024]{1,0:T(8,128)(2,1)S(1)} %get-tuple-element.52), channel_id=1, source_target_pairs={{4,0},{6,2},{8,4},{10,6},{12,8},{14,10},{5,1},{7,3},{9,5},{11,7},{... | collective-permute-start | bytes 1130504 | tf_op jit(solution)/shard_map/ppermute | solution.py:25
  14.0 0.7 %copy-start = (s32[64,3]{0,1:T(4,128)S(1)}, s32[64,3]{0,1:T(4,128)}, u32[]{:S(2)}) copy-start(s32[64,3]{0,1:T(4,128)} %param.15) | copy-start | bytes 2308
  14.0 0.7 %copy-start.4 = (f32[128]{0:T(128)S(1)}, f32[128]{0:T(128)}, u32[]{:S(2)}) copy-start(f32[128]{0:T(128)} %param.18) | copy-start | bytes 1540
  14.0 0.7 %copy-start.5 = (f32[128]{0:T(128)S(1)}, f32[128]{0:T(128)}, u32[]{:S(2)}) copy-start(f32[128]{0:T(128)} %param.19) | copy-start | bytes 1540
  18.3 16.1 %all-to-all-start = ((f32[16,8,128]{2,1,0:T(8,128)}), f32[16,8,128]{2,1,0:T(8,128)S(1)}, u32[]{:S(2)}, u32[]{:S(2)}) async-start(f32[16,8,128]{2,1,0:T(8,128)} %get-tuple-element.51), calls=%async_computation | async-start | bytes 131072 | tf_op jit(solution)/shard_map/all_to_all | solution.py:518
  35.9 1.4 %collective-permute-start.4 = (f32[264,128]{1,0:T(8,128)S(1)}, f32[264,128]{1,0:T(8,128)S(1)}, u32[]{:S(2)}, u32[]{:S(2)}) collective-permute-start(f32[264,128]{1,0:T(8,128)S(1)} %get-tuple-element.61), channel_id=1, source_target_pairs={{0,1},{1,0},{2,3},{3,2},{4,5},{5,4},{6,7},{7,6},{8,9},{9,8},{10,11... | collective-permute-start | bytes 405512 | tf_op jit(solution)/shard_map/ppermute | solution.py:30
  37.3 6.6 %collective-permute-start.7 = (bf16[280,128]{1,0:T(8,128)(2,1)S(1)}, bf16[280,128]{1,0:T(8,128)(2,1)S(1)}, u32[]{:S(2)}, u32[]{:S(2)}) collective-permute-start(bf16[280,128]{1,0:T(8,128)(2,1)S(1)} %get-tuple-element.84), channel_id=1, source_target_pairs={{0,6},{2,4},{4,2},{6,0},{8,14},{10,12},{12,10},{14,8},{1,7},{3,5},... | collective-permute-start | bytes 215048 | tf_op jit(solution)/shard_map/ppermute | solution.py:30
  39.0 5.3 %collective-permute-start.6 = (bf16[280,128]{1,0:T(8,128)(2,1)S(1)}, bf16[280,128]{1,0:T(8,128)(2,1)S(1)}, u32[]{:S(2)}, u32[]{:S(2)}) collective-permute-start(bf16[280,128]{1,0:T(8,128)(2,1)S(1)} %get-tuple-element.84), channel_id=1, source_target_pairs={{0,4},{2,6},{4,0},{6,2},{8,12},{10,14},{12,8},{14,10},{1,5},{3,7},... | collective-permute-start | bytes 215048 | tf_op jit(solution)/shard_map/ppermute | solution.py:30
  40.3 4.3 %collective-permute-start.5 = (bf16[280,128]{1,0:T(8,128)(2,1)S(1)}, bf16[280,128]{1,0:T(8,128)(2,1)S(1)}, u32[]{:S(2)}, u32[]{:S(2)}) collective-permute-start(bf16[280,128]{1,0:T(8,128)(2,1)S(1)} %get-tuple-element.84), channel_id=1, source_target_pairs={{0,2},{2,0},{4,6},{6,4},{8,10},{10,8},{12,14},{14,12},{1,3},{3,1},... | collective-permute-start | bytes 215048 | tf_op jit(solution)/shard_map/ppermute | solution.py:30
  44.8 6.1 %collective-permute-start.8 = (bf16[280,128]{1,0:T(8,128)(2,1)S(1)}, bf16[280,128]{1,0:T(8,128)(2,1)S(1)}, u32[]{:S(2)}, u32[]{:S(2)}) collective-permute-start(bf16[280,128]{1,0:T(8,128)(2,1)S(1)} %pad_maximum_fusion.1.refs_0_), channel_id=1, source_target_pairs={{0,8},{2,10},{4,12},{6,14},{8,0},{10,2},{12,4},{14,6},{1,9},{3,11}... | collective-permute-start | bytes 215048 | tf_op jit(solution)/shard_map/ppermute | solution.py:30

commit v5 on v4

--- a/solution.py
+++ b/solution.py
@@ -19,10 +19,35 @@
 LIMIT = 24 << 20
 
 
+def paired(value, steps, phase):
+    rows, groups = lax.axis_size("row"), lax.axis_size("groups")
+    route = []
+    for group in range(groups):
+        for row in range(rows):
+            target = row + steps if row // steps % 2 == phase else row - steps
+            other = group
+            if not 0 <= target < rows:
+                target = row
+                other = group ^ 1 if groups % 2 == 0 else group
+            route.append((group * rows + row, other * rows + target))
+    return lax.ppermute(value, ("groups", "row"), route)
+
+
 def shifted(value, axis, steps):
     count = lax.axis_size(axis)
     initial, last = (max(0, -steps), min(count, count - steps))
     return lax.ppermute(value, axis, [(source, source + steps) for source in range(initial, last)])
+
+
+def around(value):
+    order = ((2, 0), (2, 1), (1, 1), (1, 0))
+    found = {where: paired(value, *where) for where in order}
+    return tuple(found[steps, phase] for steps in (1, 2) for phase in (0, 1))
+
+
+def panels(steps, first, second):
+    even = lax.axis_index("row") // steps % 2 == 0
+    return jnp.where(even, second, first), jnp.where(even, first, second)
 
 
 def exchanged(value, axis, bit):
@@ -90,7 +115,7 @@
     segment_row = segments_ref[...]
     notes = jnp.where(iota((8, nodes), 0) == 0, segment_row, degree_ref[...])
     notes = notes.astype(F32).astype(BF16)
-    payload_ref[nodes + WINDOW * step :] = jnp.concatenate([notes] * local_confs, axis=1)
+    payload_ref[WINDOW * step :] = jnp.concatenate([notes] * local_confs, axis=1)
     copies[0].wait()
     for reach in range(WINDOW):
         total = None
@@ -101,13 +126,12 @@
         high, low = split_two(total)
         high_ref[reach] = high
         low_ref[reach] = low
-        rows = slice(nodes + reach * step, nodes + (reach + 1) * step)
+        rows = slice(reach * step, (reach + 1) * step)
         for part in range(local_confs):
             payload_ref[rows, part * nodes : (part + 1) * nodes] = high[
                 part * step : (part + 1) * step
             ]
     copies[1].wait()
-    payload_ref[:nodes] = own_ref[...]
 
 
 def prepare_kernel(
@@ -176,8 +200,10 @@
 
 def forward_kernel(
     local_confs,
-    near_ref,
-    far_ref,
+    near_a_ref,
+    near_b_ref,
+    far_a_ref,
+    far_b_ref,
     neigh_ref,
     out_ref,
     high_ref,
@@ -193,8 +219,9 @@
 ):
     nodes, hid = base_ref.shape[0], neigh_ref.shape[0]
     summed = summed_ref[...]
-    for reach, panel_ref in enumerate((far_ref, near_ref)):
-        panel = panel_ref[...]
+    far = panels(2, far_a_ref[...], far_b_ref[...])[0]
+    near = panels(1, near_a_ref[...], near_b_ref[...])[0]
+    for reach, panel in enumerate((far, near)):
         summed = summed + (mm(high_ref[reach], panel) + mm(low_ref[reach], panel))
     inverse = inverse_ref[...]
     w_out = out_ref[...]
@@ -299,9 +326,12 @@
     scale,
     d_row_ref,
     total_ref,
-    first_ref,
-    second_ref,
-    third_ref,
+    own_ref,
+    near_a_ref,
+    near_b_ref,
+    far_a_ref,
+    far_b_ref,
+    note_ref,
     expand_ref,
     self_ref,
     neigh_ref,
@@ -313,23 +343,28 @@
     nodes = total_ref.shape[0]
     slots = expand_ref.shape[0]
     step = nodes // local_confs
-    notes = third_ref[nodes + WINDOW * step :, :nodes].astype(F32)
+    note = note_ref[...]
+    notes = note[WINDOW * step :, :nodes].astype(F32)
     segment = column_of(notes[0:1], slots).astype(jnp.int32)
     inverse = 1.0 / jnp.maximum(column_of(notes[1:2], nodes), 1.0)
-    mask = (segment == iota((nodes, slots), 1) % SEGS).astype(F32)
+    present = lax.axis_index("row") + distance < lax.axis_size("row")
+    mask = (segment == iota((nodes, slots), 1) % SEGS).astype(F32) * present.astype(F32)
     factors = split_two(mask * d_row_ref[0:1, :])
     tiles = []
     for reach in range(WINDOW):
-        rows = slice(nodes + reach * step, nodes + (reach + 1) * step)
-        parts = [third_ref[rows, part * nodes : (part + 1) * nodes] for part in range(local_confs)]
+        rows = slice(reach * step, (reach + 1) * step)
+        parts = [note[rows, part * nodes : (part + 1) * nodes] for part in range(local_confs)]
         tiles.append(jnp.concatenate(parts, axis=0))
     w_out = out_ref[...]
     for conf in range(local_confs):
         cols = slice(conf * hid, (conf + 1) * hid)
-        own = third_ref[:nodes, cols]
-        summed = mm(tiles[0], first_ref[:nodes, cols]) + mm(tiles[1], second_ref[:nodes, cols])
-        mean = ((summed + mm(tiles[2], own)) * inverse).astype(BF16)
-        pre = mm(own, self_ref[...]) + mm(mean, neigh_ref[...]) + bias_ref[...]
+        before, after = panels(1, near_a_ref[:, cols], near_b_ref[:, cols])
+        sources = [before, own_ref[:, cols], after]
+        if distance == 2:
+            sources = sources[1:] + [panels(2, far_a_ref[:, cols], far_b_ref[:, cols])[1]]
+        summed = mm(tiles[0], sources[0]) + mm(tiles[1], sources[1]) + mm(tiles[2], sources[2])
+        mean = (summed * inverse).astype(BF16)
+        pre = mm(sources[2], self_ref[...]) + mm(mean, neigh_ref[...]) + bias_ref[...]
         sigm = sigmoid(pre)
         slope = w_out * (sigm * (1.0 + pre * (1.0 - sigm)))
         expand = expand_ref[:, cols]
@@ -430,8 +465,7 @@
     rows, columns = lax.axis_size("row"), lax.axis_size("col")
     product = 2 * nodes * nodes * width
     slots = local_confs * columns * SEGS
-    far = shifted(features, "row", 2)
-    near = shifted(features, "row", 1)
+    near_a, near_b, far_a, far_b = around(features)
     wide = shape((nodes, width), F32)
     narrow = shape((nodes, width), BF16)
     square = shape((nodes, nodes), F32)
@@ -448,7 +482,7 @@
             narrow,
             tile_set,
             tile_set,
-            shape((nodes + WINDOW * (nodes // local_confs) + 8, width), BF16),
+            shape((WINDOW * (nodes // local_confs) + 8, width), BF16),
         ),
         [pltpu.SMEM] + [pltpu.HBM] * 2,
         "parcel",
@@ -500,7 +534,10 @@
         ),
         (pltpu.SemaphoreType.DMA((2,)),),
     )
-    next_one = shifted(payload, "row", -1)
+    base, payload = lax.optimization_barrier((base, payload))
+    one = shifted(payload, "row", -1)
+    two = shifted(payload, "row", -2)
+    notes = (one, two)
     mean, slope, hidden, message = kernel_call(
         functools.partial(forward_kernel, local_confs),
         (
@@ -512,11 +549,11 @@
         [],
         "forward",
         6 * product,
-        (near, far, neigh_w, out_w, high, low, base, summed, inverse, stub),
-    )
-    next_two = shifted(payload, "row", -2)
+        (near_a, near_b, far_a, far_b, neigh_w, out_w, high, low, base, summed, inverse, stub),
+    )
+    message, notes = lax.optimization_barrier((message, notes))
     received = lax.all_to_all(message, ("row", "col"), 0, 0, tiled=True)
-    received, next_one, next_two = lax.optimization_barrier((received, next_one, next_two))
+    received, notes = lax.optimization_barrier((received, notes))
     main = 2 * hid
     grads, loss, d_pre, d_row = kernel_call(
         functools.partial(gradient_kernel, local_confs),
@@ -541,14 +578,28 @@
         (d_pre, self_w, neigh_w, inverse, high, low),
     )
 
-    def later(distance, d_row, node_total, panels, out, factor):
+    def later(distance, d_row, node_total, out, factor):
         (result,) = kernel_call(
             functools.partial(later_kernel, local_confs, distance, factor),
             (out,),
             [],
             f"later{distance}",
             10 * product,
-            (d_row, node_total, *panels, expand, self_w, neigh_w, out_w, bias_w),
+            (
+                d_row,
+                node_total,
+                own,
+                near_a,
+                near_b,
+                far_a,
+                far_b,
+                notes[distance - 1],
+                expand,
+                self_w,
+                neigh_w,
+                out_w,
+                bias_w,
+            ),
         )
         return result
 
@@ -556,7 +607,7 @@
     for step in range(columns.bit_length() - 1):
         total = total + exchanged(total, "col", 1 << step)
     total, d_row, node_total = lax.optimization_barrier((total, d_row, node_total))
-    node_total = later(1, d_row, node_total, (near, own, next_one), wide, 1.0)
+    node_total = later(1, d_row, node_total, wide, 1.0)
     stages = list(row_stages(rows))
     for index, stage in enumerate(stages):
         packet = packed(total, main)
@@ -568,7 +619,7 @@
         if index == len(stages) - 2:
             total, d_row, node_total = lax.optimization_barrier((total, d_row, node_total))
     grad_self, grad_neigh, grad_bias, grad_out = finished(parts, main, hid)
-    node_grad = later(2, d_row, node_total, (own, next_one, next_two), narrow, scale)
+    node_grad = later(2, d_row, node_total, narrow, scale)
     return (
         loss.reshape(1),
         grad_self,

time: 51.9 us -> 49.9 us (0.961)
  blocking collectives: 0 us -> 13.6 us
  starting transfers between devices: 22.8 us -> 13 us
  waiting for transfers between devices: 11.1 us -> 5.94 us
  Pallas kernels: 15.2 us -> 14.6 us
    all_to_all x0 -> x1, blocking collectives: none -> 13.6 us  [body(): received = lax.all_to_all(message, ('row', 'col'), 0, 0, tiled=True)]
    ppermute x4 -> x2, starting transfers between devices: 10.9 us -> 2.58 us  [shifted(): lax.ppermute(value, axis, [(source, source + steps) for source in range(i...]
    all_to_all x1 -> x0, starting transfers between devices: 8.13 us -> none  [body(): received = lax.all_to_all(message, ('row', 'col'), 0, 0, tiled=True)]
    ppermute x0 -> x4, starting transfers between devices: none -> 6.52 us  [paired(): return lax.ppermute(value, ('groups', 'row'), route)]
    ppermute x4 -> x2, waiting for transfers between devices: 6.41 us -> 0.41 us  [shifted(): lax.ppermute(value, axis, [(source, source + steps) for source in range(i...]
    ppermute x0 -> x4, waiting for transfers between devices: none -> 3.26 us  [paired(): return lax.ppermute(value, ('groups', 'row'), route)]
    all_to_all x1 -> x0, waiting for transfers between devices: 1.57 us -> none  [body(): received = lax.all_to_all(message, ('row', 'col'), 0, 0, tiled=True)]
    ppermute x5, waiting for transfers between devices: 3.1 us -> 2.27 us  [exchanged(): lax.ppermute(value, axis, [(source, source ^ bit) for source in range(cou...]
  transfers between devices with their start and end apart: 10 -> 11, of which waited for: 6 -> 6; matrix products, arithmetic and copies ran while one was open for 0% -> 0% of each run, Pallas kernels for 25% -> 25%
where the time goes in v5:
time: 49.9 us; the launch traced here: 49.6 us
  Pallas kernels  14.6 us (29%)
  blocking collectives  13.6 us (27%)
  starting transfers between devices  13 us (26%)
  waiting for transfers between devices  5.94 us (12%)
  local copies, waits for them, and re-layouts  1.39 us (3%)
  between operations  0.86 us (2%)
    pallas_call x8, Pallas kernels, kernel_call(): pl.pallas_call(kernel, out_shape=outs, in_specs=[pl.BlockSpec(memory_spac...  14.6 us
    all_to_all x1, blocking collectives, body(): received = lax.all_to_all(message, ('row', 'col'), 0, 0, tiled=True)  13.6 us
    ppermute x4, starting transfers between devices, paired(): return lax.ppermute(value, ('groups', 'row'), route)  6.52 us
    ppermute x5, starting transfers between devices, exchanged(): lax.ppermute(value, axis, [(source, source ^ bit) for source in range(cou...  3.89 us
    ppermute x4, waiting for transfers between devices, paired(): return lax.ppermute(value, ('groups', 'row'), route)  3.26 us
    ppermute x2, starting transfers between devices, shifted(): lax.ppermute(value, axis, [(source, source + steps) for source in range(i...  2.58 us
    ppermute x5, waiting for transfers between devices, exchanged(): lax.ppermute(value, axis, [(source, source ^ bit) for source in range(cou...  2.27 us
    unnamed x12, local copies, waits for them, and re-layouts  1.35 us
  transfers between devices with their start and end apart: 11, of which 6 were waited for; matrix products, arithmetic and copies ran while one was open for 0% of the time, Pallas kernels for 25%

profile of v5, /device:TPU:0, one launch (start us, length us, event | category | flops | bytes accessed | tf_op | source)
XLA Modules:
  0.0 49.6 jit_solution(7492642143164298604)
XLA Ops:
  0.6 3.1 %collective-permute-start.2 = (bf16[128,1024]{1,0:T(8,128)(2,1)}, bf16[128,1024]{1,0:T(8,128)(2,1)S(1)}, u32[]{:S(2)}, u32[]{:S(2)}) collective-permute-start(bf16[128,1024]{1,0:T(8,128)(2,1)} %features_ref.1), channel_id=1, source_target_pairs={{0,4},{2,6},{4,0},{6,2},{8,12},{10,14},{12,8},{14,10},{16,20},{18,... | collective-permute-start | bytes 786440 | tf_op jit(solution)/shard_map/ppermute | solution.py:33
  3.7 1.5 %collective-permute-start.1 = (bf16[128,1024]{1,0:T(8,128)(2,1)}, bf16[128,1024]{1,0:T(8,128)(2,1)S(1)}, u32[]{:S(2)}, u32[]{:S(2)}) collective-permute-start(bf16[128,1024]{1,0:T(8,128)(2,1)} %features_ref.1), channel_id=1, source_target_pairs={{0,16},{2,4},{4,2},{6,8},{8,6},{10,12},{12,10},{14,30},{16,0},{18,... | collective-permute-start | bytes 786440 | tf_op jit(solution)/shard_map/ppermute | solution.py:33
  5.2 0.0 collective-permute-start
  5.3 1.9 %collective-permute-start.3 = (bf16[128,1024]{1,0:T(8,128)(2,1)}, bf16[128,1024]{1,0:T(8,128)(2,1)S(1)}, u32[]{:S(2)}, u32[]{:S(2)}) collective-permute-start(bf16[128,1024]{1,0:T(8,128)(2,1)} %features_ref.1), channel_id=1, source_target_pairs={{0,16},{2,18},{4,8},{6,10},{8,4},{10,6},{12,28},{14,30},{16,0},{18... | collective-permute-start | bytes 786440 | tf_op jit(solution)/shard_map/ppermute | solution.py:33
  7.2 0.0 copy-start.1
  7.2 0.0 copy-start.2
  7.2 0.0 copy-start.3
  7.2 0.6 %copy-done.1 = s32[128]{0:T(128)S(1)} copy-done((s32[128]{0:T(128)S(1)}, s32[128]{0:T(128)}, u32[]{:S(2)}) %copy-start.1) | copy-done | bytes 536
  7.8 0.0 copy-done.2
  7.8 0.0 copy-done.3
  7.8 1.7 %parcel.1 = (bf16[128,1024]{1,0:T(8,128)(2,1)S(1)}, bf16[3,128,128]{2,1,0:T(8,128)(2,1)S(1)}, bf16[3,128,128]{2,1,0:T(8,128)(2,1)S(1)}, bf16[56,1024]{1,0:T(8,128)(2,1)S(1)}) custom-call(s32[1,8]{1,0:T(1,128)S(1)} %copy-done.3, bf16[128,1024]{1,0:T(8,128)(2,1)} %features_ref.1, bf16[1,8,128,128]{3,2,1,0:T(8,128)(2,1)} %tiles_ref.1, s32[1,128]{1,0:T(1,128)S(1)} %bitcast.9, ...), custom_call_target="tpu_custom_call" | custom-call | flops 33554432 | bytes 1098784 | tf_op jit(solution)/shard_map/parcel/pallas_call | solution.py:449
  9.5 0.0 copy-start
  9.5 0.0 copy-start.4
  9.6 0.0 copy-start.5
  9.6 0.6 %copy-done = s32[64,3]{0,1:T(4,128)S(1)} copy-done((s32[64,3]{0,1:T(4,128)S(1)}, s32[64,3]{0,1:T(4,128)}, u32[]{:S(2)}) %copy-start) | copy-done | bytes 792
  10.2 0.0 copy-done.4
  10.2 0.0 copy-done.5
  10.2 1.2 %prepare.1 = (bf16[128,128]{1,0:T(8,128)(2,1)S(1)}, bf16[128,128]{1,0:T(8,128)(2,1)S(1)}, f32[1,128]{1,0:T(1,128)S(1)}, f32[1,128]{1,0:T(1,128)S(1)}, f32[128,10...) custom-call(bf16[128,128]{1,0:T(8,128)(2,1)} %self_w_ref.1, ...), custom_call_target="tpu_custom_call" | custom-call | flops 100663296 | bytes 2055936 | tf_op jit(solution)/shard_map/prepare/pallas_call | solution.py:449
  11.4 1.3 %collective-permute-start.5 = (bf16[56,1024]{1,0:T(8,128)(2,1)S(1)}, bf16[56,1024]{1,0:T(8,128)(2,1)S(1)}, u32[]{:S(2)}, u32[]{:S(2)}) collective-permute-start(bf16[56,1024]{1,0:T(8,128)(2,1)S(1)} %get-tuple-element.59), channel_id=1, source_target_pairs={{4,0},{6,2},{8,4},{10,6},{12,8},{14,10},{5,1},{7,3},{9,5},{11,7},{... | collective-permute-start | bytes 344072 | tf_op jit(solution)/shard_map/ppermute | solution.py:39
  12.7 0.0 collective-permute-done.2.far_a_ref
  12.7 1.3 %collective-permute-start.4 = (bf16[56,1024]{1,0:T(8,128)(2,1)S(1)}, bf16[56,1024]{1,0:T(8,128)(2,1)S(1)}, u32[]{:S(2)}, u32[]{:S(2)}) collective-permute-start(bf16[56,1024]{1,0:T(8,128)(2,1)S(1)} %get-tuple-element.59), channel_id=1, source_target_pairs={{2,0},{4,2},{6,4},{8,6},{10,8},{12,10},{14,12},{3,1},{5,3},{7,5},{... | collective-permute-start | bytes 344072 | tf_op jit(solution)/shard_map/ppermute | solution.py:39
  14.0 0.0 collective-permute-done.1.near_b_ref
  14.1 2.5 %collective-permute-done.near_a_ref = bf16[128,1024]{1,0:T(8,128)(2,1)S(1)} collective-permute-done((bf16[128,1024]{1,0:T(8,128)(2,1)}, bf16[128,1024]{1,0:T(8,128)(2,1)S(1)}, u32[]{:S(2)}, u32[]{:S(2)}) %collective-permute-start) | collective-permute-done | bytes 262176 | tf_op jit(solution)/shard_map/ppermute | solution.py:33
  16.6 0.7 %collective-permute-done.3.far_b_ref = bf16[128,1024]{1,0:T(8,128)(2,1)S(1)} collective-permute-done((bf16[128,1024]{1,0:T(8,128)(2,1)}, bf16[128,1024]{1,0:T(8,128)(2,1)S(1)}, u32[]{:S(2)}, u32[]{:S(2)}) %collective-permute-start.3) | collective-permute-done | bytes 262176 | tf_op jit(solution)/shard_map/ppermute | solution.py:33
  17.3 1.7 %forward.1 = (bf16[128,1024]{1,0:T(8,128)(2,1)S(1)}, f32[128,1024]{1,0:T(8,128)S(1)}, f32[128,128]{1,0:T(8,128)S(1)}, f32[16,8,128]{2,1,0:T(8,128)S(1)}) custom-call(bf16[128,1024]{1,0:T(8,128)(2,1)S(1)} %collective-permute-done.near_a_ref, bf16[128,1024]{1,0:T(8,128)(2,1)S(1)} %collective-permute-done.1.near_b_ref, ...), custom_call_target="tpu_custom_call" | custom-call | flops 201326592 | bytes 3314176 | tf_op jit(solution)/shard_map/forward/pallas_call | solution.py:449
  19.0 0.4 collective-permute-done.5.note_ref
  19.4 0.0 collective-permute-done.4.note_ref
  19.4 13.6 %all_to_all.5.received_ref = f32[16,8,128]{2,1,0:T(8,128)S(1)} all-to-all(f32[16,8,128]{2,1,0:T(8,128)S(1)} %get-tuple-element.60), channel_id=1, replica_groups=mesh['groups'=2,'row'=8,'col'=2] {'row','col'}, dimensions={0} | all-to-all | bytes 131072 | tf_op jit(solution)/shard_map/all_to_all | solution.py:555
  33.1 1.5 %gradient.1 = (f32[264,128]{1,0:T(8,128)S(1)}, f32[1,1]{1,0:T(1,128)}, bf16[128,1024]{1,0:T(8,128)(2,1)S(1)}, f32[8,128]{1,0:T(8,128)S(1)}) custom-call(f32[16,8,128]{2,1,0:T(8,128)S(1)} %all_to_all.5.received_ref, bf16[128,64]{1,0:T(8,128)(2,1)S(1)} %get-tuple-element.64.chosen_ref, f32[128,128]{1,0:T(8,128)S(1)} %get-tuple-element.65.mask_ref, ...), custom_call_target="tpu_custom_call" | custom-call | flops 100663296 | bytes 1925124 | tf_op jit(solution)/shard_map/gradient/pallas_call | solution.py:449
  34.6 0.0 collective-permute-start.6
  34.6 1.1 %own.1.total_ref = f32[128,1024]{1,0:T(8,128)S(1)} custom-call(bf16[128,1024]{1,0:T(8,128)(2,1)S(1)} %get-tuple-element.73.d_pre_ref, bf16[128,128]{1,0:T(8,128)(2,1)S(1)} %get-tuple-element.74.self_ref, bf16[128,128]{1,0:T(8,128)(2,1)S(1)} %get-tuple-element.50.neigh_ref, f32[128,128]{1,0:T(8,128)S(1)} %get-tuple-element.56.inverse_ref, ...), custom_call_target="tpu_custom_call" | custom-call | flops 134217728 | bytes 1114112 | tf_op jit(solution)/shard_map/own/pallas_call | solution.py:449
  35.7 0.2 collective-permute-done.6
  36.0 0.3 collective-permute-start.9
  36.3 1.4 %collective-permute-start.8 = (bf16[280,128]{1,0:T(8,128)(2,1)S(1)}, bf16[280,128]{1,0:T(8,128)(2,1)S(1)}, u32[]{:S(2)}, u32[]{:S(2)}) collective-permute-start(bf16[280,128]{1,0:T(8,128)(2,1)S(1)} %get-tuple-element.94), channel_id=1, source_target_pairs={{0,4},{2,6},{4,0},{6,2},{8,12},{10,14},{12,8},{14,10},{1,5},{3,7},... | collective-permute-start | bytes 215048 | tf_op jit(solution)/shard_map/ppermute | solution.py:55
  37.7 1.9 %collective-permute-start.7 = (bf16[280,128]{1,0:T(8,128)(2,1)S(1)}, bf16[280,128]{1,0:T(8,128)(2,1)S(1)}, u32[]{:S(2)}, u32[]{:S(2)}) collective-permute-start(bf16[280,128]{1,0:T(8,128)(2,1)S(1)} %get-tuple-element.94), channel_id=1, source_target_pairs={{0,2},{2,0},{4,6},{6,4},{8,10},{10,8},{12,14},{14,12},{1,3},{3,1},... | collective-permute-start | bytes 215048 | tf_op jit(solution)/shard_map/ppermute | solution.py:55
  39.6 3.0 %later1.1.total_ref = f32[128,1024]{1,0:T(8,128)S(1)} custom-call(f32[8,128]{1,0:T(8,128)S(1)} %get-tuple-element.85.d_row_ref, f32[128,1024]{1,0:T(8,128)S(1)} %own.1.total_ref, bf16[128,1024]{1,0:T(8,128)(2,1)S(1)} %get-tuple-element.47.own_ref, bf16[128,1024]{1,0:T(8,128)(2,1)S(1)} %collective-permute-done.near_a_ref, ...), custom_call_target="tpu_custom_call" | custom-call | flops 335544320 | bytes 2806784 | tf_op jit(solution)/shard_map/later1/pallas_call | solution.py:449
  42.7 0.0 collective-permute-done.9
  42.7 0.2 collective-permute-done.7
  42.9 0.0 collective-permute-done.8
  43.1 0.3 collective-permute-start.10
  43.4 3.7 %later2.1 = bf16[128,1024]{1,0:T(8,128)(2,1)} custom-call(f32[8,128]{1,0:T(8,128)S(1)} %get-tuple-element.85.d_row_ref, f32[128,1024]{1,0:T(8,128)S(1)} %later1.1.total_ref, bf16[128,1024]{1,0:T(8,128)(2,1)S(1)} %get-tuple-element.47.own_ref, bf16[128,1024]{1,0:T(8,128)(2,1)S(1)} %collective-permute-done.near_a_ref, ...), custom_call_target="tpu_custom_call" | custom-call | flops 335544320 | bytes 2544640 | tf_op jit(solution)/shard_map/later2/pallas_call | solution.py:449
  47.2 1.8 %collective-permute-done.10.refs_1_ = bf16[280,128]{1,0:T(8,128)(2,1)S(1)} collective-permute-done((bf16[280,128]{1,0:T(8,128)(2,1)S(1)}, bf16[280,128]{1,0:T(8,128)(2,1)S(1)}, u32[]{:S(2)}, u32[]{:S(2)}) %collective-permute-start.10) | collective-permute-done | bytes 71712 | tf_op jit(solution)/shard_map/ppermute | solution.py:55
  49.0 0.7 %finish.1 = (f32[128,128]{1,0:T(8,128)}, f32[128,128]{1,0:T(8,128)}, f32[1,128]{1,0:T(1,128)}, f32[1,128]{1,0:T(1,128)}) custom-call(bf16[280,128]{1,0:T(8,128)(2,1)S(1)} %pad_maximum_fusion.1.refs_0_, bf16[280,128]{1,0:T(8,128)(2,1)S(1)} %collective-permute-done.10.refs_1_), custom_call_target="tpu_custom_call" | custom-call | flops 1048576 | bytes 275456 | tf_op jit(solution)/shard_map/finish/pallas_call | solution.py:449
  (19 shorter events, 0.2 us)
Async XLA Ops:
  0.6 12.1 %collective-permute-start.2 = (bf16[128,1024]{1,0:T(8,128)(2,1)}, bf16[128,1024]{1,0:T(8,128)(2,1)S(1)}, u32[]{:S(2)}, u32[]{:S(2)}) collective-permute-start(bf16[128,1024]{1,0:T(8,128)(2,1)} %features_ref.1), channel_id=1, source_target_pairs={{0,4},{2,6},{4,0},{6,2},{8,12},{10,14},{12,8},{14,10},{16,20},{18,... | collective-permute-start | bytes 786440 | tf_op jit(solution)/shard_map/ppermute | solution.py:33
  3.7 10.3 %collective-permute-start.1 = (bf16[128,1024]{1,0:T(8,128)(2,1)}, bf16[128,1024]{1,0:T(8,128)(2,1)S(1)}, u32[]{:S(2)}, u32[]{:S(2)}) collective-permute-start(bf16[128,1024]{1,0:T(8,128)(2,1)} %features_ref.1), channel_id=1, source_target_pairs={{0,16},{2,4},{4,2},{6,8},{8,6},{10,12},{12,10},{14,30},{16,0},{18,... | collective-permute-start | bytes 786440 | tf_op jit(solution)/shard_map/ppermute | solution.py:33
  5.2 11.4 %collective-permute-start = (bf16[128,1024]{1,0:T(8,128)(2,1)}, bf16[128,1024]{1,0:T(8,128)(2,1)S(1)}, u32[]{:S(2)}, u32[]{:S(2)}) collective-permute-start(bf16[128,1024]{1,0:T(8,128)(2,1)} %features_ref.1), channel_id=1, source_target_pairs={{0,2},{2,0},{4,6},{6,4},{8,10},{10,8},{12,14},{14,12},{16,18},{18,... | collective-permute-start | bytes 786440 | tf_op jit(solution)/shard_map/ppermute | solution.py:33
  5.3 12.1 %collective-permute-start.3 = (bf16[128,1024]{1,0:T(8,128)(2,1)}, bf16[128,1024]{1,0:T(8,128)(2,1)S(1)}, u32[]{:S(2)}, u32[]{:S(2)}) collective-permute-start(bf16[128,1024]{1,0:T(8,128)(2,1)} %features_ref.1), channel_id=1, source_target_pairs={{0,16},{2,18},{4,8},{6,10},{8,4},{10,6},{12,28},{14,30},{16,0},{18... | collective-permute-start | bytes 786440 | tf_op jit(solution)/shard_map/ppermute | solution.py:33
  7.2 0.7 %copy-start.1 = (s32[128]{0:T(128)S(1)}, s32[128]{0:T(128)}, u32[]{:S(2)}) copy-start(s32[128]{0:T(128)} %param.13) | copy-start | bytes 1540
  7.2 0.7 %copy-start.2 = (s32[128]{0:T(128)S(1)}, s32[128]{0:T(128)}, u32[]{:S(2)}) copy-start(s32[128]{0:T(128)} %param.14) | copy-start | bytes 1540
  7.2 0.7 %copy-start.3 = (s32[1,8]{1,0:T(1,128)S(1)}, s32[1,8]{1,0:T(1,128)}, u32[]{:S(2)}) copy-start(s32[1,8]{1,0:T(1,128)} %pattern_ref.1) | copy-start | bytes 100
  9.5 0.7 %copy-start = (s32[64,3]{0,1:T(4,128)S(1)}, s32[64,3]{0,1:T(4,128)}, u32[]{:S(2)}) copy-start(s32[64,3]{0,1:T(4,128)} %param.15) | copy-start | bytes 2308
  9.5 0.7 %copy-start.4 = (f32[128]{0:T(128)S(1)}, f32[128]{0:T(128)}, u32[]{:S(2)}) copy-start(f32[128]{0:T(128)} %param.18) | copy-start | bytes 1540
  9.6 0.7 %copy-start.5 = (f32[128]{0:T(128)S(1)}, f32[128]{0:T(128)}, u32[]{:S(2)}) copy-start(f32[128]{0:T(128)} %param.19) | copy-start | bytes 1540
  11.4 8.0 %collective-permute-start.5 = (bf16[56,1024]{1,0:T(8,128)(2,1)S(1)}, bf16[56,1024]{1,0:T(8,128)(2,1)S(1)}, u32[]{:S(2)}, u32[]{:S(2)}) collective-permute-start(bf16[56,1024]{1,0:T(8,128)(2,1)S(1)} %get-tuple-element.59), channel_id=1, source_target_pairs={{4,0},{6,2},{8,4},{10,6},{12,8},{14,10},{5,1},{7,3},{9,5},{11,7},{... | collective-permute-start | bytes 344072 | tf_op jit(solution)/shard_map/ppermute | solution.py:39
  12.7 6.7 %collective-permute-start.4 = (bf16[56,1024]{1,0:T(8,128)(2,1)S(1)}, bf16[56,1024]{1,0:T(8,128)(2,1)S(1)}, u32[]{:S(2)}, u32[]{:S(2)}) collective-permute-start(bf16[56,1024]{1,0:T(8,128)(2,1)S(1)} %get-tuple-element.59), channel_id=1, source_target_pairs={{2,0},{4,2},{6,4},{8,6},{10,8},{12,10},{14,12},{3,1},{5,3},{7,5},{... | collective-permute-start | bytes 344072 | tf_op jit(solution)/shard_map/ppermute | solution.py:39
  34.6 1.4 %collective-permute-start.6 = (f32[264,128]{1,0:T(8,128)S(1)}, f32[264,128]{1,0:T(8,128)S(1)}, u32[]{:S(2)}, u32[]{:S(2)}) collective-permute-start(f32[264,128]{1,0:T(8,128)S(1)} %get-tuple-element.71), channel_id=1, source_target_pairs={{0,1},{1,0},{2,3},{3,2},{4,5},{5,4},{6,7},{7,6},{8,9},{9,8},{10,11... | collective-permute-start | bytes 405512 | tf_op jit(solution)/shard_map/ppermute | solution.py:55
  36.0 6.7 %collective-permute-start.9 = (bf16[280,128]{1,0:T(8,128)(2,1)S(1)}, bf16[280,128]{1,0:T(8,128)(2,1)S(1)}, u32[]{:S(2)}, u32[]{:S(2)}) collective-permute-start(bf16[280,128]{1,0:T(8,128)(2,1)S(1)} %get-tuple-element.94), channel_id=1, source_target_pairs={{0,6},{2,4},{4,2},{6,0},{8,14},{10,12},{12,10},{14,8},{1,7},{3,5},... | collective-permute-start | bytes 215048 | tf_op jit(solution)/shard_map/ppermute | solution.py:55
  36.3 6.7 %collective-permute-start.8 = (bf16[280,128]{1,0:T(8,128)(2,1)S(1)}, bf16[280,128]{1,0:T(8,128)(2,1)S(1)}, u32[]{:S(2)}, u32[]{:S(2)}) collective-permute-start(bf16[280,128]{1,0:T(8,128)(2,1)S(1)} %get-tuple-element.94), channel_id=1, source_target_pairs={{0,4},{2,6},{4,0},{6,2},{8,12},{10,14},{12,8},{14,10},{1,5},{3,7},... | collective-permute-start | bytes 215048 | tf_op jit(solution)/shard_map/ppermute | solution.py:55
  37.7 5.2 %collective-permute-start.7 = (bf16[280,128]{1,0:T(8,128)(2,1)S(1)}, bf16[280,128]{1,0:T(8,128)(2,1)S(1)}, u32[]{:S(2)}, u32[]{:S(2)}) collective-permute-start(bf16[280,128]{1,0:T(8,128)(2,1)S(1)} %get-tuple-element.94), channel_id=1, source_target_pairs={{0,2},{2,0},{4,6},{6,4},{8,10},{10,8},{12,14},{14,12},{1,3},{3,1},... | collective-permute-start | bytes 215048 | tf_op jit(solution)/shard_map/ppermute | solution.py:55
  43.1 5.8 %collective-permute-start.10 = (bf16[280,128]{1,0:T(8,128)(2,1)S(1)}, bf16[280,128]{1,0:T(8,128)(2,1)S(1)}, u32[]{:S(2)}, u32[]{:S(2)}) collective-permute-start(bf16[280,128]{1,0:T(8,128)(2,1)S(1)} %pad_maximum_fusion.1.refs_0_), channel_id=1, source_target_pairs={{0,8},{2,10},{4,12},{6,14},{8,0},{10,2},{12,4},{14,6},{1,9},{3,11}... | collective-permute-start | bytes 215048 | tf_op jit(solution)/shard_map/ppermute | solution.py:55

commit v6 on v5

--- a/solution.py
+++ b/solution.py
@@ -100,6 +100,7 @@
     high_ref,
     low_ref,
     payload_ref,
+    full_ref,
     tiles_buffer,
     sems,
 ):
@@ -115,7 +116,7 @@
     segment_row = segments_ref[...]
     notes = jnp.where(iota((8, nodes), 0) == 0, segment_row, degree_ref[...])
     notes = notes.astype(F32).astype(BF16)
-    payload_ref[WINDOW * step :] = jnp.concatenate([notes] * local_confs, axis=1)
+    full_ref[WINDOW * step :] = jnp.concatenate([notes] * local_confs, axis=1)
     copies[0].wait()
     for reach in range(WINDOW):
         total = None
@@ -128,9 +129,12 @@
         low_ref[reach] = low
         rows = slice(reach * step, (reach + 1) * step)
         for part in range(local_confs):
-            payload_ref[rows, part * nodes : (part + 1) * nodes] = high[
+            full_ref[rows, part * nodes : (part + 1) * nodes] = high[
                 part * step : (part + 1) * step
             ]
+    share = payload_ref.shape[0]
+    start = lax.axis_index("col") * (full_ref.shape[0] - share)
+    payload_ref[...] = full_ref[pl.ds(pl.multiple_of(start, 8), share), :]
     copies[1].wait()
 
 
@@ -221,13 +225,16 @@
     summed = summed_ref[...]
     far = panels(2, far_a_ref[...], far_b_ref[...])[0]
     near = panels(1, near_a_ref[...], near_b_ref[...])[0]
-    for reach, panel in enumerate((far, near)):
-        summed = summed + (mm(high_ref[reach], panel) + mm(low_ref[reach], panel))
+    weights = [ref[reach] for reach in (0, 1) for ref in (high_ref, low_ref)]
+    summed = summed + mm(
+        jnp.concatenate(weights, axis=1), jnp.concatenate([far, far, near, near], axis=0)
+    )
     inverse = inverse_ref[...]
     w_out = out_ref[...]
     segment_row = stub_ref[2:3, :].astype(jnp.int32)
     member = (segment_row == iota((SEGS, nodes), 0)).astype(F32).astype(BF16)
     first_conf = lax.axis_index("col") * local_confs
+    member = jnp.concatenate([member, member], axis=1)
     hidden_ref[...] = jnp.zeros_like(hidden_ref)
     for conf in range(local_confs):
         cols = slice(conf * hid, (conf + 1) * hid)
@@ -238,9 +245,9 @@
         hidden = pre * sigm
         slope = w_out * (sigm * (1.0 + pre * (1.0 - sigm)))
         slope_ref[:, cols] = slope
-        high, low = split_two(hidden)
+        pair = jnp.concatenate(split_two(hidden), axis=0)
         start = pl.multiple_of((first_conf + conf) * SEGS, SEGS)
-        hidden_ref[pl.ds(start, SEGS), :] = mm(member, high) + mm(member, low)
+        hidden_ref[pl.ds(start, SEGS), :] = mm(member, pair)
     scores = mm_exact(jnp.broadcast_to(w_out, (8, hid)), hidden_ref[...], ((1,), (1,)))
     message = stub_ref[...] + jnp.where(iota(scores.shape, 0) == 0, scores, 0.0)
     for peer in range(message_ref.shape[0]):
@@ -289,10 +296,10 @@
         d_pre_b = d_pre.astype(BF16)
         d_pre_ref[:, cols] = d_pre_b
         rows = jnp.concatenate([own_ref[:, cols], mean_ref[:, cols]], axis=1)
-        term = mm(d_pre_b, rows, ((0,), (0,)))
+        term = mm(rows, d_pre_b, ((0,), (0,)))
         grads = term if grads is None else grads + term
         d_bias = d_pre if d_bias is None else d_bias + d_pre
-    grads_ref[: 2 * hid] = grads.T
+    grads_ref[: 2 * hid] = grads
     d_out = mm_exact(d_rows, hidden_ref[...], ((1,), (0,)))
     d_bias = jnp.sum(d_bias, axis=0, keepdims=True)
     sub = iota((8, hid), 0)
@@ -332,6 +339,7 @@
     far_a_ref,
     far_b_ref,
     note_ref,
+    note_other_ref,
     expand_ref,
     self_ref,
     neigh_ref,
@@ -343,7 +351,11 @@
     nodes = total_ref.shape[0]
     slots = expand_ref.shape[0]
     step = nodes // local_confs
-    note = note_ref[...]
+    first_core = lax.axis_index("col") == 0
+    upper = jnp.where(first_core, note_ref[...], note_other_ref[...])
+    lower = jnp.where(first_core, note_other_ref[...], note_ref[...])
+    share = upper.shape[0]
+    note = jnp.concatenate([upper, lower[2 * share - WINDOW * step - 8 :]], axis=0)
     notes = note[WINDOW * step :, :nodes].astype(F32)
     segment = column_of(notes[0:1], slots).astype(jnp.int32)
     inverse = 1.0 / jnp.maximum(column_of(notes[1:2], nodes), 1.0)
@@ -355,6 +367,7 @@
         rows = slice(reach * step, (reach + 1) * step)
         parts = [note[rows, part * nodes : (part + 1) * nodes] for part in range(local_confs)]
         tiles.append(jnp.concatenate(parts, axis=0))
+    weights = jnp.concatenate([self_ref[...], neigh_ref[...]], axis=0)
     w_out = out_ref[...]
     for conf in range(local_confs):
         cols = slice(conf * hid, (conf + 1) * hid)
@@ -364,7 +377,7 @@
             sources = sources[1:] + [panels(2, far_a_ref[:, cols], far_b_ref[:, cols])[1]]
         summed = mm(tiles[0], sources[0]) + mm(tiles[1], sources[1]) + mm(tiles[2], sources[2])
         mean = (summed * inverse).astype(BF16)
-        pre = mm(sources[2], self_ref[...]) + mm(mean, neigh_ref[...]) + bias_ref[...]
+        pre = mm(jnp.concatenate([sources[2], mean], axis=1), weights) + bias_ref[...]
         sigm = sigmoid(pre)
         slope = w_out * (sigm * (1.0 + pre * (1.0 - sigm)))
         expand = expand_ref[:, cols]
@@ -476,19 +489,25 @@
         pltpu.with_memory_space_constraint(value, pltpu.HBM)
         for value in (features, tiles, w_self, w_neigh)
     ]
+    note_rows = WINDOW * (nodes // local_confs) + 8
+    share = -(-note_rows // 16) * 8 if columns == 2 else note_rows
     own, high, low, payload = kernel_call(
         functools.partial(parcel_kernel, local_confs),
         (
             narrow,
             tile_set,
             tile_set,
-            shape((WINDOW * (nodes // local_confs) + 8, width), BF16),
+            shape((share, width), BF16),
         ),
         [pltpu.SMEM] + [pltpu.HBM] * 2,
         "parcel",
         product,
         (pattern, in_hbm[0], in_hbm[1], degree_row, segment_row),
-        (pltpu.VMEM(tiles.shape, tiles.dtype), pltpu.SemaphoreType.DMA((2,))),
+        (
+            pltpu.VMEM((note_rows, width), BF16),
+            pltpu.VMEM(tiles.shape, tiles.dtype),
+            pltpu.SemaphoreType.DMA((2,)),
+        ),
     )
     (
         self_w,
@@ -554,6 +573,11 @@
     message, notes = lax.optimization_barrier((message, notes))
     received = lax.all_to_all(message, ("row", "col"), 0, 0, tiled=True)
     received, notes = lax.optimization_barrier((received, notes))
+    if columns == 2:
+        received, notes = lax.optimization_barrier((received, notes))
+        notes = tuple((note, exchanged(note, "col", 1)) for note in notes)
+    else:
+        notes = tuple((note, note) for note in notes)
     main = 2 * hid
     grads, loss, d_pre, d_row = kernel_call(
         functools.partial(gradient_kernel, local_confs),
@@ -593,7 +617,7 @@
                 near_b,
                 far_a,
                 far_b,
-                notes[distance - 1],
+                *notes[distance - 1],
                 expand,
                 self_w,
                 neigh_w,

time: 49.9 us -> 49 us (0.982)
  Pallas kernels: 14.6 us -> 13.5 us
  blocking collectives: 13.6 us -> 12.9 us
  starting transfers between devices: 13 us -> 13.6 us
    pallas_call x8, Pallas kernels: 14.6 us -> 13.5 us  [kernel_call(): pl.pallas_call(kernel, out_shape=outs, in_specs=[pl.BlockSpec(memory_spac...]
    all_to_all x1, blocking collectives: 13.6 us -> 12.9 us  [body(): received = lax.all_to_all(message, ('row', 'col'), 0, 0, tiled=True)]
    ppermute x5 -> x7, starting transfers between devices: 3.89 us -> 4.52 us  [exchanged(): lax.ppermute(value, axis, [(source, source ^ bit) for source in range(cou...]
    ppermute x5 -> x7, waiting for transfers between devices: 2.27 us -> 2.34 us  [exchanged(): lax.ppermute(value, axis, [(source, source ^ bit) for source in range(cou...]
  transfers between devices with their start and end apart: 11 -> 13, of which waited for: 6 -> 5; matrix products, arithmetic and copies ran while one was open for 0% -> 0% of each run, Pallas kernels for 25% -> 24%
where the time goes in v6:
time: 49 us; the launch traced here: 48.7 us
  starting transfers between devices  13.6 us (28%)
  Pallas kernels  13.5 us (28%)
  blocking collectives  12.9 us (26%)
  waiting for transfers between devices  6.15 us (13%)
  local copies, waits for them, and re-layouts  1.39 us (3%)
  between operations  0.91 us (2%)
    pallas_call x8, Pallas kernels, kernel_call(): pl.pallas_call(kernel, out_shape=outs, in_specs=[pl.BlockSpec(memory_spac...  13.5 us
    all_to_all x1, blocking collectives, body(): received = lax.all_to_all(message, ('row', 'col'), 0, 0, tiled=True)  12.9 us
    ppermute x4, starting transfers between devices, paired(): return lax.ppermute(value, ('groups', 'row'), route)  6.52 us
    ppermute x7, starting transfers between devices, exchanged(): lax.ppermute(value, axis, [(source, source ^ bit) for source in range(cou...  4.52 us
    ppermute x4, waiting for transfers between devices, paired(): return lax.ppermute(value, ('groups', 'row'), route)  3.26 us
    ppermute x2, starting transfers between devices, shifted(): lax.ppermute(value, axis, [(source, source + steps) for source in range(i...  2.58 us
    ppermute x7, waiting for transfers between devices, exchanged(): lax.ppermute(value, axis, [(source, source ^ bit) for source in range(cou...  2.34 us
    unnamed x12, local copies, waits for them, and re-layouts  1.35 us
  transfers between devices with their start and end apart: 13, of which 5 were waited for; matrix products, arithmetic and copies ran while one was open for 0% of the time, Pallas kernels for 24%

profile of v6, /device:TPU:0, one launch (start us, length us, event | category | flops | bytes accessed | tf_op | source)
XLA Modules:
  0.0 48.7 jit_solution(7380689657091008437)
XLA Ops:
  0.6 3.1 %collective-permute-start.2 = (bf16[128,1024]{1,0:T(8,128)(2,1)}, bf16[128,1024]{1,0:T(8,128)(2,1)S(1)}, u32[]{:S(2)}, u32[]{:S(2)}) collective-permute-start(bf16[128,1024]{1,0:T(8,128)(2,1)} %features_ref.1), channel_id=1, source_target_pairs={{0,4},{2,6},{4,0},{6,2},{8,12},{10,14},{12,8},{14,10},{16,20},{18,... | collective-permute-start | bytes 786440 | tf_op jit(solution)/shard_map/ppermute | solution.py:33
  3.7 1.5 %collective-permute-start.1 = (bf16[128,1024]{1,0:T(8,128)(2,1)}, bf16[128,1024]{1,0:T(8,128)(2,1)S(1)}, u32[]{:S(2)}, u32[]{:S(2)}) collective-permute-start(bf16[128,1024]{1,0:T(8,128)(2,1)} %features_ref.1), channel_id=1, source_target_pairs={{0,16},{2,4},{4,2},{6,8},{8,6},{10,12},{12,10},{14,30},{16,0},{18,... | collective-permute-start | bytes 786440 | tf_op jit(solution)/shard_map/ppermute | solution.py:33
  5.2 0.0 collective-permute-start
  5.3 1.9 %collective-permute-start.3 = (bf16[128,1024]{1,0:T(8,128)(2,1)}, bf16[128,1024]{1,0:T(8,128)(2,1)S(1)}, u32[]{:S(2)}, u32[]{:S(2)}) collective-permute-start(bf16[128,1024]{1,0:T(8,128)(2,1)} %features_ref.1), channel_id=1, source_target_pairs={{0,16},{2,18},{4,8},{6,10},{8,4},{10,6},{12,28},{14,30},{16,0},{18... | collective-permute-start | bytes 786440 | tf_op jit(solution)/shard_map/ppermute | solution.py:33
  7.2 0.0 copy-start.1
  7.2 0.0 copy-start.2
  7.2 0.0 copy-start.3
  7.2 0.6 %copy-done.1 = s32[128]{0:T(128)S(1)} copy-done((s32[128]{0:T(128)S(1)}, s32[128]{0:T(128)}, u32[]{:S(2)}) %copy-start.1) | copy-done | bytes 536
  7.8 0.0 copy-done.2
  7.8 0.0 copy-done.3
  7.8 1.7 %parcel.1 = (bf16[128,1024]{1,0:T(8,128)(2,1)S(1)}, bf16[3,128,128]{2,1,0:T(8,128)(2,1)S(1)}, bf16[3,128,128]{2,1,0:T(8,128)(2,1)S(1)}, bf16[32,1024]{1,0:T(8,128)(2,1)S(1)}) custom-call(s32[1,8]{1,0:T(1,128)S(1)} %copy-done.3, bf16[128,1024]{1,0:T(8,128)(2,1)} %features_ref.1, bf16[1,8,128,128]{3,2,1,0:T(8,128)(2,1)} %tiles_ref.1, s32[1,128]{1,0:T(1,128)S(1)} %bitcast.9, ...), custom_call_target="tpu_custom_call" | custom-call | flops 33554432 | bytes 1049632 | tf_op jit(solution)/shard_map/parcel/pallas_call | solution.py:462
  9.5 0.0 copy-start
  9.6 0.0 copy-start.4
  9.6 0.0 copy-start.5
  9.6 0.6 %copy-done = s32[64,3]{0,1:T(4,128)S(1)} copy-done((s32[64,3]{0,1:T(4,128)S(1)}, s32[64,3]{0,1:T(4,128)}, u32[]{:S(2)}) %copy-start) | copy-done | bytes 792
  10.2 0.0 copy-done.4
  10.2 0.0 copy-done.5
  10.2 1.2 %prepare.1 = (bf16[128,128]{1,0:T(8,128)(2,1)S(1)}, bf16[128,128]{1,0:T(8,128)(2,1)S(1)}, f32[1,128]{1,0:T(1,128)S(1)}, f32[1,128]{1,0:T(1,128)S(1)}, f32[128,10...) custom-call(bf16[128,128]{1,0:T(8,128)(2,1)} %self_w_ref.1, ...), custom_call_target="tpu_custom_call" | custom-call | flops 100663296 | bytes 2055936 | tf_op jit(solution)/shard_map/prepare/pallas_call | solution.py:462
  11.4 1.3 %collective-permute-start.5 = (bf16[32,1024]{1,0:T(8,128)(2,1)S(1)}, bf16[32,1024]{1,0:T(8,128)(2,1)S(1)}, u32[]{:S(2)}, u32[]{:S(2)}) collective-permute-start(bf16[32,1024]{1,0:T(8,128)(2,1)S(1)} %get-tuple-element.59), channel_id=1, source_target_pairs={{4,0},{6,2},{8,4},{10,6},{12,8},{14,10},{5,1},{7,3},{9,5},{11,7},{... | collective-permute-start | bytes 196616 | tf_op jit(solution)/shard_map/ppermute | solution.py:39
  12.7 0.0 collective-permute-done.2.far_a_ref
  12.8 1.3 %collective-permute-start.4 = (bf16[32,1024]{1,0:T(8,128)(2,1)S(1)}, bf16[32,1024]{1,0:T(8,128)(2,1)S(1)}, u32[]{:S(2)}, u32[]{:S(2)}) collective-permute-start(bf16[32,1024]{1,0:T(8,128)(2,1)S(1)} %get-tuple-element.59), channel_id=1, source_target_pairs={{2,0},{4,2},{6,4},{8,6},{10,8},{12,10},{14,12},{3,1},{5,3},{7,5},{... | collective-permute-start | bytes 196616 | tf_op jit(solution)/shard_map/ppermute | solution.py:39
  14.1 0.0 collective-permute-done.1.near_b_ref
  14.1 3.2 %collective-permute-done.near_a_ref = bf16[128,1024]{1,0:T(8,128)(2,1)S(1)} collective-permute-done((bf16[128,1024]{1,0:T(8,128)(2,1)}, bf16[128,1024]{1,0:T(8,128)(2,1)S(1)}, u32[]{:S(2)}, u32[]{:S(2)}) %collective-permute-start) | collective-permute-done | bytes 262176 | tf_op jit(solution)/shard_map/ppermute | solution.py:33
  17.2 0.1 collective-permute-done.3.far_b_ref
  17.3 1.0 %forward.1 = (bf16[128,1024]{1,0:T(8,128)(2,1)S(1)}, f32[128,1024]{1,0:T(8,128)S(1)}, f32[128,128]{1,0:T(8,128)S(1)}, f32[16,8,128]{2,1,0:T(8,128)S(1)}) custom-call(bf16[128,1024]{1,0:T(8,128)(2,1)S(1)} %collective-permute-done.near_a_ref, bf16[128,1024]{1,0:T(8,128)(2,1)S(1)} %collective-permute-done.1.near_b_ref, ...), custom_call_target="tpu_custom_call" | custom-call | flops 201326592 | bytes 3314176 | tf_op jit(solution)/shard_map/forward/pallas_call | solution.py:462
  18.3 0.0 collective-permute-done.5.note_ref
  18.4 0.6 %collective-permute-done.4.note_ref = bf16[32,1024]{1,0:T(8,128)(2,1)S(1)} collective-permute-done((bf16[32,1024]{1,0:T(8,128)(2,1)S(1)}, bf16[32,1024]{1,0:T(8,128)(2,1)S(1)}, u32[]{:S(2)}, u32[]{:S(2)}) %collective-permute-start.4) | collective-permute-done | bytes 65568 | tf_op jit(solution)/shard_map/ppermute | solution.py:39
  18.9 12.9 %all_to_all.5.received_ref = f32[16,8,128]{2,1,0:T(8,128)S(1)} all-to-all(f32[16,8,128]{2,1,0:T(8,128)S(1)} %get-tuple-element.60), channel_id=1, replica_groups=mesh['groups'=2,'row'=8,'col'=2] {'row','col'}, dimensions={0} | all-to-all | bytes 131072 | tf_op jit(solution)/shard_map/all_to_all | solution.py:574
  31.9 1.1 %gradient.1 = (f32[264,128]{1,0:T(8,128)S(1)}, f32[1,1]{1,0:T(1,128)}, bf16[128,1024]{1,0:T(8,128)(2,1)S(1)}, f32[8,128]{1,0:T(8,128)S(1)}) custom-call(f32[16,8,128]{2,1,0:T(8,128)S(1)} %all_to_all.5.received_ref, bf16[128,64]{1,0:T(8,128)(2,1)S(1)} %get-tuple-element.64.chosen_ref, f32[128,128]{1,0:T(8,128)S(1)} %get-tuple-element.65.mask_ref, ...), custom_call_target="tpu_custom_call" | custom-call | flops 100663296 | bytes 1925124 | tf_op jit(solution)/shard_map/gradient/pallas_call | solution.py:462
  32.9 0.1 collective-permute-start.6
  33.0 0.5 %collective-permute-start.10 = (bf16[32,1024]{1,0:T(8,128)(2,1)S(1)}, bf16[32,1024]{1,0:T(8,128)(2,1)S(1)}, u32[]{:S(2)}, u32[]{:S(2)}) collective-permute-start(bf16[32,1024]{1,0:T(8,128)(2,1)S(1)} %collective-permute-done.4.note_ref), channel_id=1, source_target_pairs={{0,1},{1,0},{2,3},{3,2},{4,5},{5,4},{6,7},{7,6},{8,9},{9,8},{10,11... | collective-permute-start | bytes 196616 | tf_op jit(solution)/shard_map/ppermute | solution.py:55
  33.5 0.1 collective-permute-start.12
  33.6 1.1 %own.1.total_ref = f32[128,1024]{1,0:T(8,128)S(1)} custom-call(bf16[128,1024]{1,0:T(8,128)(2,1)S(1)} %get-tuple-element.73.d_pre_ref, bf16[128,128]{1,0:T(8,128)(2,1)S(1)} %get-tuple-element.74.self_ref, bf16[128,128]{1,0:T(8,128)(2,1)S(1)} %get-tuple-element.50.neigh_ref, f32[128,128]{1,0:T(8,128)S(1)} %get-tuple-element.56.inverse_ref, ...), custom_call_target="tpu_custom_call" | custom-call | flops 134217728 | bytes 1114112 | tf_op jit(solution)/shard_map/own/pallas_call | solution.py:462
  34.7 0.0 collective-permute-done.6
  34.8 0.3 collective-permute-start.9
  35.1 1.4 %collective-permute-start.8 = (bf16[280,128]{1,0:T(8,128)(2,1)S(1)}, bf16[280,128]{1,0:T(8,128)(2,1)S(1)}, u32[]{:S(2)}, u32[]{:S(2)}) collective-permute-start(bf16[280,128]{1,0:T(8,128)(2,1)S(1)} %get-tuple-element.94), channel_id=1, source_target_pairs={{0,4},{2,6},{4,0},{6,2},{8,12},{10,14},{12,8},{14,10},{1,5},{3,7},... | collective-permute-start | bytes 215048 | tf_op jit(solution)/shard_map/ppermute | solution.py:55
  36.6 1.9 %collective-permute-start.7 = (bf16[280,128]{1,0:T(8,128)(2,1)S(1)}, bf16[280,128]{1,0:T(8,128)(2,1)S(1)}, u32[]{:S(2)}, u32[]{:S(2)}) collective-permute-start(bf16[280,128]{1,0:T(8,128)(2,1)S(1)} %get-tuple-element.94), channel_id=1, source_target_pairs={{0,2},{2,0},{4,6},{6,4},{8,10},{10,8},{12,14},{14,12},{1,3},{3,1},... | collective-permute-start | bytes 215048 | tf_op jit(solution)/shard_map/ppermute | solution.py:55
  38.4 0.0 collective-permute-done.10.note_other_ref
  38.4 3.0 %later1.1.total_ref = f32[128,1024]{1,0:T(8,128)S(1)} custom-call(f32[8,128]{1,0:T(8,128)S(1)} %get-tuple-element.85.d_row_ref, f32[128,1024]{1,0:T(8,128)S(1)} %own.1.total_ref, bf16[128,1024]{1,0:T(8,128)(2,1)S(1)} %get-tuple-element.47.own_ref, bf16[128,1024]{1,0:T(8,128)(2,1)S(1)} %collective-permute-done.near_a_ref, ...), custom_call_target="tpu_custom_call" | custom-call | flops 335544320 | bytes 2823168 | tf_op jit(solution)/shard_map/later1/pallas_call | solution.py:462
  41.5 0.0 collective-permute-done.9
  41.5 0.4 collective-permute-done.7
  41.9 0.0 collective-permute-done.8
  42.1 0.3 collective-permute-start.11
  42.3 0.0 collective-permute-done.12.note_other_ref
  42.4 3.7 %later2.1 = bf16[128,1024]{1,0:T(8,128)(2,1)} custom-call(f32[8,128]{1,0:T(8,128)S(1)} %get-tuple-element.85.d_row_ref, f32[128,1024]{1,0:T(8,128)S(1)} %later1.1.total_ref, bf16[128,1024]{1,0:T(8,128)(2,1)S(1)} %get-tuple-element.47.own_ref, bf16[128,1024]{1,0:T(8,128)(2,1)S(1)} %collective-permute-done.near_a_ref, ...), custom_call_target="tpu_custom_call" | custom-call | flops 335544320 | bytes 2561024 | tf_op jit(solution)/shard_map/later2/pallas_call | solution.py:462
  46.1 1.9 %collective-permute-done.11.refs_1_ = bf16[280,128]{1,0:T(8,128)(2,1)S(1)} collective-permute-done((bf16[280,128]{1,0:T(8,128)(2,1)S(1)}, bf16[280,128]{1,0:T(8,128)(2,1)S(1)}, u32[]{:S(2)}, u32[]{:S(2)}) %collective-permute-start.11) | collective-permute-done | bytes 71712 | tf_op jit(solution)/shard_map/ppermute | solution.py:55
  48.0 0.7 %finish.1 = (f32[128,128]{1,0:T(8,128)}, f32[128,128]{1,0:T(8,128)}, f32[1,128]{1,0:T(1,128)}, f32[1,128]{1,0:T(1,128)}) custom-call(bf16[280,128]{1,0:T(8,128)(2,1)S(1)} %pad_maximum_fusion.1.refs_0_, bf16[280,128]{1,0:T(8,128)(2,1)S(1)} %collective-permute-done.11.refs_1_), custom_call_target="tpu_custom_call" | custom-call | flops 1048576 | bytes 275456 | tf_op jit(solution)/shard_map/finish/pallas_call | solution.py:462
  (19 shorter events, 0.2 us)
Async XLA Ops:
  0.6 12.1 %collective-permute-start.2 = (bf16[128,1024]{1,0:T(8,128)(2,1)}, bf16[128,1024]{1,0:T(8,128)(2,1)S(1)}, u32[]{:S(2)}, u32[]{:S(2)}) collective-permute-start(bf16[128,1024]{1,0:T(8,128)(2,1)} %features_ref.1), channel_id=1, source_target_pairs={{0,4},{2,6},{4,0},{6,2},{8,12},{10,14},{12,8},{14,10},{16,20},{18,... | collective-permute-start | bytes 786440 | tf_op jit(solution)/shard_map/ppermute | solution.py:33
  3.7 10.3 %collective-permute-start.1 = (bf16[128,1024]{1,0:T(8,128)(2,1)}, bf16[128,1024]{1,0:T(8,128)(2,1)S(1)}, u32[]{:S(2)}, u32[]{:S(2)}) collective-permute-start(bf16[128,1024]{1,0:T(8,128)(2,1)} %features_ref.1), channel_id=1, source_target_pairs={{0,16},{2,4},{4,2},{6,8},{8,6},{10,12},{12,10},{14,30},{16,0},{18,... | collective-permute-start | bytes 786440 | tf_op jit(solution)/shard_map/ppermute | solution.py:33
  5.2 12.0 %collective-permute-start = (bf16[128,1024]{1,0:T(8,128)(2,1)}, bf16[128,1024]{1,0:T(8,128)(2,1)S(1)}, u32[]{:S(2)}, u32[]{:S(2)}) collective-permute-start(bf16[128,1024]{1,0:T(8,128)(2,1)} %features_ref.1), channel_id=1, source_target_pairs={{0,2},{2,0},{4,6},{6,4},{8,10},{10,8},{12,14},{14,12},{16,18},{18,... | collective-permute-start | bytes 786440 | tf_op jit(solution)/shard_map/ppermute | solution.py:33
  5.3 12.1 %collective-permute-start.3 = (bf16[128,1024]{1,0:T(8,128)(2,1)}, bf16[128,1024]{1,0:T(8,128)(2,1)S(1)}, u32[]{:S(2)}, u32[]{:S(2)}) collective-permute-start(bf16[128,1024]{1,0:T(8,128)(2,1)} %features_ref.1), channel_id=1, source_target_pairs={{0,16},{2,18},{4,8},{6,10},{8,4},{10,6},{12,28},{14,30},{16,0},{18... | collective-permute-start | bytes 786440 | tf_op jit(solution)/shard_map/ppermute | solution.py:33
  7.2 0.7 %copy-start.1 = (s32[128]{0:T(128)S(1)}, s32[128]{0:T(128)}, u32[]{:S(2)}) copy-start(s32[128]{0:T(128)} %param.13) | copy-start | bytes 1540
  7.2 0.7 %copy-start.2 = (s32[128]{0:T(128)S(1)}, s32[128]{0:T(128)}, u32[]{:S(2)}) copy-start(s32[128]{0:T(128)} %param.14) | copy-start | bytes 1540
  7.2 0.7 %copy-start.3 = (s32[1,8]{1,0:T(1,128)S(1)}, s32[1,8]{1,0:T(1,128)}, u32[]{:S(2)}) copy-start(s32[1,8]{1,0:T(1,128)} %pattern_ref.1) | copy-start | bytes 100
  9.5 0.7 %copy-start = (s32[64,3]{0,1:T(4,128)S(1)}, s32[64,3]{0,1:T(4,128)}, u32[]{:S(2)}) copy-start(s32[64,3]{0,1:T(4,128)} %param.15) | copy-start | bytes 2308
  9.6 0.7 %copy-start.4 = (f32[128]{0:T(128)S(1)}, f32[128]{0:T(128)}, u32[]{:S(2)}) copy-start(f32[128]{0:T(128)} %param.18) | copy-start | bytes 1540
  9.6 0.7 %copy-start.5 = (f32[128]{0:T(128)S(1)}, f32[128]{0:T(128)}, u32[]{:S(2)}) copy-start(f32[128]{0:T(128)} %param.19) | copy-start | bytes 1540
  11.4 6.9 %collective-permute-start.5 = (bf16[32,1024]{1,0:T(8,128)(2,1)S(1)}, bf16[32,1024]{1,0:T(8,128)(2,1)S(1)}, u32[]{:S(2)}, u32[]{:S(2)}) collective-permute-start(bf16[32,1024]{1,0:T(8,128)(2,1)S(1)} %get-tuple-element.59), channel_id=1, source_target_pairs={{4,0},{6,2},{8,4},{10,6},{12,8},{14,10},{5,1},{7,3},{9,5},{11,7},{... | collective-permute-start | bytes 196616 | tf_op jit(solution)/shard_map/ppermute | solution.py:39
  12.8 6.2 %collective-permute-start.4 = (bf16[32,1024]{1,0:T(8,128)(2,1)S(1)}, bf16[32,1024]{1,0:T(8,128)(2,1)S(1)}, u32[]{:S(2)}, u32[]{:S(2)}) collective-permute-start(bf16[32,1024]{1,0:T(8,128)(2,1)S(1)} %get-tuple-element.59), channel_id=1, source_target_pairs={{2,0},{4,2},{6,4},{8,6},{10,8},{12,10},{14,12},{3,1},{5,3},{7,5},{... | collective-permute-start | bytes 196616 | tf_op jit(solution)/shard_map/ppermute | solution.py:39
  32.9 1.8 %collective-permute-start.6 = (f32[264,128]{1,0:T(8,128)S(1)}, f32[264,128]{1,0:T(8,128)S(1)}, u32[]{:S(2)}, u32[]{:S(2)}) collective-permute-start(f32[264,128]{1,0:T(8,128)S(1)} %get-tuple-element.71), channel_id=1, source_target_pairs={{0,1},{1,0},{2,3},{3,2},{4,5},{5,4},{6,7},{7,6},{8,9},{9,8},{10,11... | collective-permute-start | bytes 405512 | tf_op jit(solution)/shard_map/ppermute | solution.py:55
  33.0 5.4 %collective-permute-start.10 = (bf16[32,1024]{1,0:T(8,128)(2,1)S(1)}, bf16[32,1024]{1,0:T(8,128)(2,1)S(1)}, u32[]{:S(2)}, u32[]{:S(2)}) collective-permute-start(bf16[32,1024]{1,0:T(8,128)(2,1)S(1)} %collective-permute-done.4.note_ref), channel_id=1, source_target_pairs={{0,1},{1,0},{2,3},{3,2},{4,5},{5,4},{6,7},{7,6},{8,9},{9,8},{10,11... | collective-permute-start | bytes 196616 | tf_op jit(solution)/shard_map/ppermute | solution.py:55
  33.5 8.8 %collective-permute-start.12 = (bf16[32,1024]{1,0:T(8,128)(2,1)S(1)}, bf16[32,1024]{1,0:T(8,128)(2,1)S(1)}, u32[]{:S(2)}, u32[]{:S(2)}) collective-permute-start(bf16[32,1024]{1,0:T(8,128)(2,1)S(1)} %collective-permute-done.5.note_ref), channel_id=1, source_target_pairs={{0,1},{1,0},{2,3},{3,2},{4,5},{5,4},{6,7},{7,6},{8,9},{9,8},{10,11... | collective-permute-start | bytes 196616 | tf_op jit(solution)/shard_map/ppermute | solution.py:55
  34.8 6.7 %collective-permute-start.9 = (bf16[280,128]{1,0:T(8,128)(2,1)S(1)}, bf16[280,128]{1,0:T(8,128)(2,1)S(1)}, u32[]{:S(2)}, u32[]{:S(2)}) collective-permute-start(bf16[280,128]{1,0:T(8,128)(2,1)S(1)} %get-tuple-element.94), channel_id=1, source_target_pairs={{0,6},{2,4},{4,2},{6,0},{8,14},{10,12},{12,10},{14,8},{1,7},{3,5},... | collective-permute-start | bytes 215048 | tf_op jit(solution)/shard_map/ppermute | solution.py:55
  35.1 6.8 %collective-permute-start.8 = (bf16[280,128]{1,0:T(8,128)(2,1)S(1)}, bf16[280,128]{1,0:T(8,128)(2,1)S(1)}, u32[]{:S(2)}, u32[]{:S(2)}) collective-permute-start(bf16[280,128]{1,0:T(8,128)(2,1)S(1)} %get-tuple-element.94), channel_id=1, source_target_pairs={{0,4},{2,6},{4,0},{6,2},{8,12},{10,14},{12,8},{14,10},{1,5},{3,7},... | collective-permute-start | bytes 215048 | tf_op jit(solution)/shard_map/ppermute | solution.py:55
  36.6 5.3 %collective-permute-start.7 = (bf16[280,128]{1,0:T(8,128)(2,1)S(1)}, bf16[280,128]{1,0:T(8,128)(2,1)S(1)}, u32[]{:S(2)}, u32[]{:S(2)}) collective-permute-start(bf16[280,128]{1,0:T(8,128)(2,1)S(1)} %get-tuple-element.94), channel_id=1, source_target_pairs={{0,2},{2,0},{4,6},{6,4},{8,10},{10,8},{12,14},{14,12},{1,3},{3,1},... | collective-permute-start | bytes 215048 | tf_op jit(solution)/shard_map/ppermute | solution.py:55
  42.1 6.0 %collective-permute-start.11 = (bf16[280,128]{1,0:T(8,128)(2,1)S(1)}, bf16[280,128]{1,0:T(8,128)(2,1)S(1)}, u32[]{:S(2)}, u32[]{:S(2)}) collective-permute-start(bf16[280,128]{1,0:T(8,128)(2,1)S(1)} %pad_maximum_fusion.1.refs_0_), channel_id=1, source_target_pairs={{0,8},{2,10},{4,12},{6,14},{8,0},{10,2},{12,4},{14,6},{1,9},{3,11}... | collective-permute-start | bytes 215048 | tf_op jit(solution)/shard_map/ppermute | solution.py:55

commit v7 on v6

--- a/solution.py
+++ b/solution.py
@@ -575,7 +575,9 @@
     received, notes = lax.optimization_barrier((received, notes))
     if columns == 2:
         received, notes = lax.optimization_barrier((received, notes))
-        notes = tuple((note, exchanged(note, "col", 1)) for note in notes)
+        both = jnp.concatenate(notes, axis=0)
+        swapped = exchanged(both, "col", 1)
+        notes = ((notes[0], swapped[:share]), (notes[1], swapped[share:]))
     else:
         notes = tuple((note, note) for note in notes)
     main = 2 * hid

time: 49 us -> 48.6 us (level)
    ppermute x7 -> x6, waiting for transfers between devices: 2.34 us -> 1.86 us  [exchanged(): lax.ppermute(value, axis, [(source, source ^ bit) for source in range(cou...]
    ppermute x7 -> x6, starting transfers between devices: 4.52 us -> 4.53 us  [exchanged(): lax.ppermute(value, axis, [(source, source ^ bit) for source in range(cou...]
  transfers between devices with their start and end apart: 13 -> 12, of which waited for: 5 -> 5; matrix products, arithmetic and copies ran while one was open for 0% -> 0% of each run, Pallas kernels for 24% -> 27%
where the time goes in v7:
time: 48.6 us; the launch traced here: 48.3 us
  starting transfers between devices  13.6 us (28%)
  Pallas kernels  13.5 us (28%)
  blocking collectives  12.9 us (27%)
  waiting for transfers between devices  5.67 us (12%)
  local copies, waits for them, and re-layouts  1.4 us (3%)
  between operations  0.93 us (2%)
    pallas_call x8, Pallas kernels, kernel_call(): pl.pallas_call(kernel, out_shape=outs, in_specs=[pl.BlockSpec(memory_spac...  13.5 us
    all_to_all x1, blocking collectives, body(): received = lax.all_to_all(message, ('row', 'col'), 0, 0, tiled=True)  12.9 us
    ppermute x4, starting transfers between devices, paired(): return lax.ppermute(value, ('groups', 'row'), route)  6.52 us
    ppermute x6, starting transfers between devices, exchanged(): lax.ppermute(value, axis, [(source, source ^ bit) for source in range(cou...  4.53 us
    ppermute x4, waiting for transfers between devices, paired(): return lax.ppermute(value, ('groups', 'row'), route)  3.26 us
    ppermute x2, starting transfers between devices, shifted(): lax.ppermute(value, axis, [(source, source + steps) for source in range(i...  2.58 us
    ppermute x6, waiting for transfers between devices, exchanged(): lax.ppermute(value, axis, [(source, source ^ bit) for source in range(cou...  1.86 us
    unnamed x12, local copies, waits for them, and re-layouts  1.35 us
  transfers between devices with their start and end apart: 12, of which 5 were waited for; matrix products, arithmetic and copies ran while one was open for 0% of the time, Pallas kernels for 27%

profile of v7, /device:TPU:0, one launch (start us, length us, event | category | flops | bytes accessed | tf_op | source)
XLA Modules:
  0.0 48.3 jit_solution(17117096276921539178)
XLA Ops:
  0.6 3.1 %collective-permute-start.2 = (bf16[128,1024]{1,0:T(8,128)(2,1)}, bf16[128,1024]{1,0:T(8,128)(2,1)S(1)}, u32[]{:S(2)}, u32[]{:S(2)}) collective-permute-start(bf16[128,1024]{1,0:T(8,128)(2,1)} %features_ref.1), channel_id=1, source_target_pairs={{0,4},{2,6},{4,0},{6,2},{8,12},{10,14},{12,8},{14,10},{16,20},{18,... | collective-permute-start | bytes 786440 | tf_op jit(solution)/shard_map/ppermute | solution.py:33
  3.7 1.5 %collective-permute-start.1 = (bf16[128,1024]{1,0:T(8,128)(2,1)}, bf16[128,1024]{1,0:T(8,128)(2,1)S(1)}, u32[]{:S(2)}, u32[]{:S(2)}) collective-permute-start(bf16[128,1024]{1,0:T(8,128)(2,1)} %features_ref.1), channel_id=1, source_target_pairs={{0,16},{2,4},{4,2},{6,8},{8,6},{10,12},{12,10},{14,30},{16,0},{18,... | collective-permute-start | bytes 786440 | tf_op jit(solution)/shard_map/ppermute | solution.py:33
  5.2 0.0 collective-permute-start
  5.3 1.9 %collective-permute-start.3 = (bf16[128,1024]{1,0:T(8,128)(2,1)}, bf16[128,1024]{1,0:T(8,128)(2,1)S(1)}, u32[]{:S(2)}, u32[]{:S(2)}) collective-permute-start(bf16[128,1024]{1,0:T(8,128)(2,1)} %features_ref.1), channel_id=1, source_target_pairs={{0,16},{2,18},{4,8},{6,10},{8,4},{10,6},{12,28},{14,30},{16,0},{18... | collective-permute-start | bytes 786440 | tf_op jit(solution)/shard_map/ppermute | solution.py:33
  7.2 0.0 copy-start.1
  7.2 0.0 copy-start.2
  7.2 0.0 copy-start.3
  7.2 0.6 %copy-done.1 = s32[128]{0:T(128)S(1)} copy-done((s32[128]{0:T(128)S(1)}, s32[128]{0:T(128)}, u32[]{:S(2)}) %copy-start.1) | copy-done | bytes 536
  7.8 0.0 copy-done.2
  7.8 0.0 copy-done.3
  7.8 1.7 %parcel.1 = (bf16[128,1024]{1,0:T(8,128)(2,1)S(1)}, bf16[3,128,128]{2,1,0:T(8,128)(2,1)S(1)}, bf16[3,128,128]{2,1,0:T(8,128)(2,1)S(1)}, bf16[32,1024]{1,0:T(8,128)(2,1)S(1)}) custom-call(s32[1,8]{1,0:T(1,128)S(1)} %copy-done.3, bf16[128,1024]{1,0:T(8,128)(2,1)} %features_ref.1, bf16[1,8,128,128]{3,2,1,0:T(8,128)(2,1)} %tiles_ref.1, s32[1,128]{1,0:T(1,128)S(1)} %bitcast.9, ...), custom_call_target="tpu_custom_call" | custom-call | flops 33554432 | bytes 1049632 | tf_op jit(solution)/shard_map/parcel/pallas_call | solution.py:462
  9.5 0.0 copy-start
  9.6 0.0 copy-start.4
  9.6 0.0 copy-start.5
  9.6 0.6 %copy-done = s32[64,3]{0,1:T(4,128)S(1)} copy-done((s32[64,3]{0,1:T(4,128)S(1)}, s32[64,3]{0,1:T(4,128)}, u32[]{:S(2)}) %copy-start) | copy-done | bytes 792
  10.2 0.0 copy-done.4
  10.2 0.0 copy-done.5
  10.2 1.2 %prepare.1 = (bf16[128,128]{1,0:T(8,128)(2,1)S(1)}, bf16[128,128]{1,0:T(8,128)(2,1)S(1)}, f32[1,128]{1,0:T(1,128)S(1)}, f32[1,128]{1,0:T(1,128)S(1)}, f32[128,10...) custom-call(bf16[128,128]{1,0:T(8,128)(2,1)} %self_w_ref.1, ...), custom_call_target="tpu_custom_call" | custom-call | flops 100663296 | bytes 2055936 | tf_op jit(solution)/shard_map/prepare/pallas_call | solution.py:462
  11.4 1.3 %collective-permute-start.5 = (bf16[32,1024]{1,0:T(8,128)(2,1)S(1)}, bf16[32,1024]{1,0:T(8,128)(2,1)S(1)}, u32[]{:S(2)}, u32[]{:S(2)}) collective-permute-start(bf16[32,1024]{1,0:T(8,128)(2,1)S(1)} %get-tuple-element.59), channel_id=1, source_target_pairs={{4,0},{6,2},{8,4},{10,6},{12,8},{14,10},{5,1},{7,3},{9,5},{11,7},{... | collective-permute-start | bytes 196616 | tf_op jit(solution)/shard_map/ppermute | solution.py:39
  12.7 0.0 collective-permute-done.2.far_a_ref
  12.8 1.3 %collective-permute-start.4 = (bf16[32,1024]{1,0:T(8,128)(2,1)S(1)}, bf16[32,1024]{1,0:T(8,128)(2,1)S(1)}, u32[]{:S(2)}, u32[]{:S(2)}) collective-permute-start(bf16[32,1024]{1,0:T(8,128)(2,1)S(1)} %get-tuple-element.59), channel_id=1, source_target_pairs={{2,0},{4,2},{6,4},{8,6},{10,8},{12,10},{14,12},{3,1},{5,3},{7,5},{... | collective-permute-start | bytes 196616 | tf_op jit(solution)/shard_map/ppermute | solution.py:39
  14.1 0.0 collective-permute-done.1.near_b_ref
  14.1 3.2 %collective-permute-done.near_a_ref = bf16[128,1024]{1,0:T(8,128)(2,1)S(1)} collective-permute-done((bf16[128,1024]{1,0:T(8,128)(2,1)}, bf16[128,1024]{1,0:T(8,128)(2,1)S(1)}, u32[]{:S(2)}, u32[]{:S(2)}) %collective-permute-start) | collective-permute-done | bytes 262176 | tf_op jit(solution)/shard_map/ppermute | solution.py:33
  17.2 0.1 collective-permute-done.3.far_b_ref
  17.3 1.0 %forward.1 = (bf16[128,1024]{1,0:T(8,128)(2,1)S(1)}, f32[128,1024]{1,0:T(8,128)S(1)}, f32[128,128]{1,0:T(8,128)S(1)}, f32[16,8,128]{2,1,0:T(8,128)S(1)}) custom-call(bf16[128,1024]{1,0:T(8,128)(2,1)S(1)} %collective-permute-done.near_a_ref, bf16[128,1024]{1,0:T(8,128)(2,1)S(1)} %collective-permute-done.1.near_b_ref, ...), custom_call_target="tpu_custom_call" | custom-call | flops 201326592 | bytes 3314176 | tf_op jit(solution)/shard_map/forward/pallas_call | solution.py:462
  18.3 0.0 collective-permute-done.5.note_ref
  18.4 0.6 %collective-permute-done.4.note_ref = bf16[32,1024]{1,0:T(8,128)(2,1)S(1)} collective-permute-done((bf16[32,1024]{1,0:T(8,128)(2,1)S(1)}, bf16[32,1024]{1,0:T(8,128)(2,1)S(1)}, u32[]{:S(2)}, u32[]{:S(2)}) %collective-permute-start.4) | collective-permute-done | bytes 65568 | tf_op jit(solution)/shard_map/ppermute | solution.py:39
  18.9 12.9 %all_to_all.5.received_ref = f32[16,8,128]{2,1,0:T(8,128)S(1)} all-to-all(f32[16,8,128]{2,1,0:T(8,128)S(1)} %get-tuple-element.60), channel_id=1, replica_groups=mesh['groups'=2,'row'=8,'col'=2] {'row','col'}, dimensions={0} | all-to-all | bytes 131072 | tf_op jit(solution)/shard_map/all_to_all | solution.py:574
  31.9 0.1 collective-permute-start.10
  31.9 1.1 %gradient.1 = (f32[264,128]{1,0:T(8,128)S(1)}, f32[1,1]{1,0:T(1,128)}, bf16[128,1024]{1,0:T(8,128)(2,1)S(1)}, f32[8,128]{1,0:T(8,128)S(1)}) custom-call(f32[16,8,128]{2,1,0:T(8,128)S(1)} %all_to_all.5.received_ref, bf16[128,64]{1,0:T(8,128)(2,1)S(1)} %get-tuple-element.64.chosen_ref, f32[128,128]{1,0:T(8,128)S(1)} %get-tuple-element.65.mask_ref, ...), custom_call_target="tpu_custom_call" | custom-call | flops 100663296 | bytes 1925124 | tf_op jit(solution)/shard_map/gradient/pallas_call | solution.py:462
  33.0 0.6 %collective-permute-start.6 = (f32[264,128]{1,0:T(8,128)S(1)}, f32[264,128]{1,0:T(8,128)S(1)}, u32[]{:S(2)}, u32[]{:S(2)}) collective-permute-start(f32[264,128]{1,0:T(8,128)S(1)} %get-tuple-element.71), channel_id=1, source_target_pairs={{0,1},{1,0},{2,3},{3,2},{4,5},{5,4},{6,7},{7,6},{8,9},{9,8},{10,11... | collective-permute-start | bytes 405512 | tf_op jit(solution)/shard_map/ppermute | solution.py:55
  33.6 1.1 %own.1.total_ref = f32[128,1024]{1,0:T(8,128)S(1)} custom-call(bf16[128,1024]{1,0:T(8,128)(2,1)S(1)} %get-tuple-element.73.d_pre_ref, bf16[128,128]{1,0:T(8,128)(2,1)S(1)} %get-tuple-element.74.self_ref, bf16[128,128]{1,0:T(8,128)(2,1)S(1)} %get-tuple-element.50.neigh_ref, f32[128,128]{1,0:T(8,128)S(1)} %get-tuple-element.56.inverse_ref, ...), custom_call_target="tpu_custom_call" | custom-call | flops 134217728 | bytes 1114112 | tf_op jit(solution)/shard_map/own/pallas_call | solution.py:462
  34.7 0.0 collective-permute-done.10
  34.7 0.0 collective-permute-done.6
  34.8 0.3 collective-permute-start.9
  35.1 1.4 %collective-permute-start.8 = (bf16[280,128]{1,0:T(8,128)(2,1)S(1)}, bf16[280,128]{1,0:T(8,128)(2,1)S(1)}, u32[]{:S(2)}, u32[]{:S(2)}) collective-permute-start(bf16[280,128]{1,0:T(8,128)(2,1)S(1)} %get-tuple-element.96), channel_id=1, source_target_pairs={{0,4},{2,6},{4,0},{6,2},{8,12},{10,14},{12,8},{14,10},{1,5},{3,7},... | collective-permute-start | bytes 215048 | tf_op jit(solution)/shard_map/ppermute | solution.py:55
  36.6 1.9 %collective-permute-start.7 = (bf16[280,128]{1,0:T(8,128)(2,1)S(1)}, bf16[280,128]{1,0:T(8,128)(2,1)S(1)}, u32[]{:S(2)}, u32[]{:S(2)}) collective-permute-start(bf16[280,128]{1,0:T(8,128)(2,1)S(1)} %get-tuple-element.96), channel_id=1, source_target_pairs={{0,2},{2,0},{4,6},{6,4},{8,10},{10,8},{12,14},{14,12},{1,3},{3,1},... | collective-permute-start | bytes 215048 | tf_op jit(solution)/shard_map/ppermute | solution.py:55
  38.5 3.0 %later1.1.total_ref = f32[128,1024]{1,0:T(8,128)S(1)} custom-call(f32[8,128]{1,0:T(8,128)S(1)} %get-tuple-element.86.d_row_ref, f32[128,1024]{1,0:T(8,128)S(1)} %own.1.total_ref, bf16[128,1024]{1,0:T(8,128)(2,1)S(1)} %get-tuple-element.47.own_ref, bf16[128,1024]{1,0:T(8,128)(2,1)S(1)} %collective-permute-done.near_a_ref, ...), custom_call_target="tpu_custom_call" | custom-call | flops 335544320 | bytes 2823168 | tf_op jit(solution)/shard_map/later1/pallas_call | solution.py:462
  41.5 0.0 collective-permute-done.9
  41.5 0.1 collective-permute-done.7
  41.7 0.0 collective-permute-done.8
  41.9 0.3 collective-permute-start.11
  42.1 3.7 %later2.1 = bf16[128,1024]{1,0:T(8,128)(2,1)} custom-call(f32[8,128]{1,0:T(8,128)S(1)} %get-tuple-element.86.d_row_ref, f32[128,1024]{1,0:T(8,128)S(1)} %later1.1.total_ref, bf16[128,1024]{1,0:T(8,128)(2,1)S(1)} %get-tuple-element.47.own_ref, bf16[128,1024]{1,0:T(8,128)(2,1)S(1)} %collective-permute-done.near_a_ref, ...), custom_call_target="tpu_custom_call" | custom-call | flops 335544320 | bytes 2561024 | tf_op jit(solution)/shard_map/later2/pallas_call | solution.py:462
  45.9 1.7 %collective-permute-done.11.refs_1_ = bf16[280,128]{1,0:T(8,128)(2,1)S(1)} collective-permute-done((bf16[280,128]{1,0:T(8,128)(2,1)S(1)}, bf16[280,128]{1,0:T(8,128)(2,1)S(1)}, u32[]{:S(2)}, u32[]{:S(2)}) %collective-permute-start.11) | collective-permute-done | bytes 71712 | tf_op jit(solution)/shard_map/ppermute | solution.py:55
  47.6 0.7 %finish.1 = (f32[128,128]{1,0:T(8,128)}, f32[128,128]{1,0:T(8,128)}, f32[1,128]{1,0:T(1,128)}, f32[1,128]{1,0:T(1,128)}) custom-call(bf16[280,128]{1,0:T(8,128)(2,1)S(1)} %pad_maximum_fusion.2.refs_0_, bf16[280,128]{1,0:T(8,128)(2,1)S(1)} %collective-permute-done.11.refs_1_), custom_call_target="tpu_custom_call" | custom-call | flops 1048576 | bytes 275456 | tf_op jit(solution)/shard_map/finish/pallas_call | solution.py:462
  (21 shorter events, 0.2 us)
Async XLA Ops:
  0.6 12.1 %collective-permute-start.2 = (bf16[128,1024]{1,0:T(8,128)(2,1)}, bf16[128,1024]{1,0:T(8,128)(2,1)S(1)}, u32[]{:S(2)}, u32[]{:S(2)}) collective-permute-start(bf16[128,1024]{1,0:T(8,128)(2,1)} %features_ref.1), channel_id=1, source_target_pairs={{0,4},{2,6},{4,0},{6,2},{8,12},{10,14},{12,8},{14,10},{16,20},{18,... | collective-permute-start | bytes 786440 | tf_op jit(solution)/shard_map/ppermute | solution.py:33
  3.7 10.3 %collective-permute-start.1 = (bf16[128,1024]{1,0:T(8,128)(2,1)}, bf16[128,1024]{1,0:T(8,128)(2,1)S(1)}, u32[]{:S(2)}, u32[]{:S(2)}) collective-permute-start(bf16[128,1024]{1,0:T(8,128)(2,1)} %features_ref.1), channel_id=1, source_target_pairs={{0,16},{2,4},{4,2},{6,8},{8,6},{10,12},{12,10},{14,30},{16,0},{18,... | collective-permute-start | bytes 786440 | tf_op jit(solution)/shard_map/ppermute | solution.py:33
  5.2 12.0 %collective-permute-start = (bf16[128,1024]{1,0:T(8,128)(2,1)}, bf16[128,1024]{1,0:T(8,128)(2,1)S(1)}, u32[]{:S(2)}, u32[]{:S(2)}) collective-permute-start(bf16[128,1024]{1,0:T(8,128)(2,1)} %features_ref.1), channel_id=1, source_target_pairs={{0,2},{2,0},{4,6},{6,4},{8,10},{10,8},{12,14},{14,12},{16,18},{18,... | collective-permute-start | bytes 786440 | tf_op jit(solution)/shard_map/ppermute | solution.py:33
  5.3 12.1 %collective-permute-start.3 = (bf16[128,1024]{1,0:T(8,128)(2,1)}, bf16[128,1024]{1,0:T(8,128)(2,1)S(1)}, u32[]{:S(2)}, u32[]{:S(2)}) collective-permute-start(bf16[128,1024]{1,0:T(8,128)(2,1)} %features_ref.1), channel_id=1, source_target_pairs={{0,16},{2,18},{4,8},{6,10},{8,4},{10,6},{12,28},{14,30},{16,0},{18... | collective-permute-start | bytes 786440 | tf_op jit(solution)/shard_map/ppermute | solution.py:33
  7.2 0.7 %copy-start.1 = (s32[128]{0:T(128)S(1)}, s32[128]{0:T(128)}, u32[]{:S(2)}) copy-start(s32[128]{0:T(128)} %param.13) | copy-start | bytes 1540
  7.2 0.7 %copy-start.2 = (s32[128]{0:T(128)S(1)}, s32[128]{0:T(128)}, u32[]{:S(2)}) copy-start(s32[128]{0:T(128)} %param.14) | copy-start | bytes 1540
  7.2 0.7 %copy-start.3 = (s32[1,8]{1,0:T(1,128)S(1)}, s32[1,8]{1,0:T(1,128)}, u32[]{:S(2)}) copy-start(s32[1,8]{1,0:T(1,128)} %pattern_ref.1) | copy-start | bytes 100
  9.5 0.7 %copy-start = (s32[64,3]{0,1:T(4,128)S(1)}, s32[64,3]{0,1:T(4,128)}, u32[]{:S(2)}) copy-start(s32[64,3]{0,1:T(4,128)} %param.15) | copy-start | bytes 2308
  9.6 0.7 %copy-start.4 = (f32[128]{0:T(128)S(1)}, f32[128]{0:T(128)}, u32[]{:S(2)}) copy-start(f32[128]{0:T(128)} %param.18) | copy-start | bytes 1540
  9.6 0.7 %copy-start.5 = (f32[128]{0:T(128)S(1)}, f32[128]{0:T(128)}, u32[]{:S(2)}) copy-start(f32[128]{0:T(128)} %param.19) | copy-start | bytes 1540
  11.4 6.9 %collective-permute-start.5 = (bf16[32,1024]{1,0:T(8,128)(2,1)S(1)}, bf16[32,1024]{1,0:T(8,128)(2,1)S(1)}, u32[]{:S(2)}, u32[]{:S(2)}) collective-permute-start(bf16[32,1024]{1,0:T(8,128)(2,1)S(1)} %get-tuple-element.59), channel_id=1, source_target_pairs={{4,0},{6,2},{8,4},{10,6},{12,8},{14,10},{5,1},{7,3},{9,5},{11,7},{... | collective-permute-start | bytes 196616 | tf_op jit(solution)/shard_map/ppermute | solution.py:39
  12.8 6.2 %collective-permute-start.4 = (bf16[32,1024]{1,0:T(8,128)(2,1)S(1)}, bf16[32,1024]{1,0:T(8,128)(2,1)S(1)}, u32[]{:S(2)}, u32[]{:S(2)}) collective-permute-start(bf16[32,1024]{1,0:T(8,128)(2,1)S(1)} %get-tuple-element.59), channel_id=1, source_target_pairs={{2,0},{4,2},{6,4},{8,6},{10,8},{12,10},{14,12},{3,1},{5,3},{7,5},{... | collective-permute-start | bytes 196616 | tf_op jit(solution)/shard_map/ppermute | solution.py:39
  31.9 2.8 %collective-permute-start.10 = (bf16[64,1024]{1,0:T(8,128)(2,1)S(1)}, bf16[64,1024]{1,0:T(8,128)(2,1)S(1)}, u32[]{:S(2)}, u32[]{:S(2)}) collective-permute-start(bf16[64,1024]{1,0:T(8,128)(2,1)S(1)} %pad_maximum_fusion), channel_id=1, source_target_pairs={{0,1},{1,0},{2,3},{3,2},{4,5},{5,4},{6,7},{7,6},{8,9},{9,8},{10,11... | collective-permute-start | bytes 393224 | tf_op jit(solution)/shard_map/ppermute | solution.py:55
  33.0 1.7 %collective-permute-start.6 = (f32[264,128]{1,0:T(8,128)S(1)}, f32[264,128]{1,0:T(8,128)S(1)}, u32[]{:S(2)}, u32[]{:S(2)}) collective-permute-start(f32[264,128]{1,0:T(8,128)S(1)} %get-tuple-element.71), channel_id=1, source_target_pairs={{0,1},{1,0},{2,3},{3,2},{4,5},{5,4},{6,7},{7,6},{8,9},{9,8},{10,11... | collective-permute-start | bytes 405512 | tf_op jit(solution)/shard_map/ppermute | solution.py:55
  34.8 6.7 %collective-permute-start.9 = (bf16[280,128]{1,0:T(8,128)(2,1)S(1)}, bf16[280,128]{1,0:T(8,128)(2,1)S(1)}, u32[]{:S(2)}, u32[]{:S(2)}) collective-permute-start(bf16[280,128]{1,0:T(8,128)(2,1)S(1)} %get-tuple-element.96), channel_id=1, source_target_pairs={{0,6},{2,4},{4,2},{6,0},{8,14},{10,12},{12,10},{14,8},{1,7},{3,5},... | collective-permute-start | bytes 215048 | tf_op jit(solution)/shard_map/ppermute | solution.py:55
  35.1 6.6 %collective-permute-start.8 = (bf16[280,128]{1,0:T(8,128)(2,1)S(1)}, bf16[280,128]{1,0:T(8,128)(2,1)S(1)}, u32[]{:S(2)}, u32[]{:S(2)}) collective-permute-start(bf16[280,128]{1,0:T(8,128)(2,1)S(1)} %get-tuple-element.96), channel_id=1, source_target_pairs={{0,4},{2,6},{4,0},{6,2},{8,12},{10,14},{12,8},{14,10},{1,5},{3,7},... | collective-permute-start | bytes 215048 | tf_op jit(solution)/shard_map/ppermute | solution.py:55
  36.6 5.1 %collective-permute-start.7 = (bf16[280,128]{1,0:T(8,128)(2,1)S(1)}, bf16[280,128]{1,0:T(8,128)(2,1)S(1)}, u32[]{:S(2)}, u32[]{:S(2)}) collective-permute-start(bf16[280,128]{1,0:T(8,128)(2,1)S(1)} %get-tuple-element.96), channel_id=1, source_target_pairs={{0,2},{2,0},{4,6},{6,4},{8,10},{10,8},{12,14},{14,12},{1,3},{3,1},... | collective-permute-start | bytes 215048 | tf_op jit(solution)/shard_map/ppermute | solution.py:55
  41.9 5.7 %collective-permute-start.11 = (bf16[280,128]{1,0:T(8,128)(2,1)S(1)}, bf16[280,128]{1,0:T(8,128)(2,1)S(1)}, u32[]{:S(2)}, u32[]{:S(2)}) collective-permute-start(bf16[280,128]{1,0:T(8,128)(2,1)S(1)} %pad_maximum_fusion.2.refs_0_), channel_id=1, source_target_pairs={{0,8},{2,10},{4,12},{6,14},{8,0},{10,2},{12,4},{14,6},{1,9},{3,11}... | collective-permute-start | bytes 215048 | tf_op jit(solution)/shard_map/ppermute | solution.py:55

commit v8 on v7

--- a/solution.py
+++ b/solution.py
@@ -96,10 +96,18 @@
     tiles_ref,
     degree_ref,
     segments_ref,
+    pairs_ref,
+    bias_ref,
+    w_out_ref,
     own_ref,
     high_ref,
     low_ref,
     payload_ref,
+    degree_copy_ref,
+    segments_copy_ref,
+    pairs_copy_ref,
+    bias_copy_ref,
+    w_out_copy_ref,
     full_ref,
     tiles_buffer,
     sems,
@@ -110,6 +118,11 @@
     ]
     for copy in copies:
         copy.start()
+    degree_copy_ref[...] = degree_ref[...]
+    segments_copy_ref[...] = segments_ref[...]
+    pairs_copy_ref[...] = pairs_ref[...]
+    bias_copy_ref[...] = bias_ref[...]
+    w_out_copy_ref[...] = w_out_ref[...]
     nodes = own_ref.shape[0]
     lowest = lax.axis_index("row") - REACH
     step = nodes // local_confs
@@ -249,7 +262,7 @@
         start = pl.multiple_of((first_conf + conf) * SEGS, SEGS)
         hidden_ref[pl.ds(start, SEGS), :] = mm(member, pair)
     scores = mm_exact(jnp.broadcast_to(w_out, (8, hid)), hidden_ref[...], ((1,), (1,)))
-    message = stub_ref[...] + jnp.where(iota(scores.shape, 0) == 0, scores, 0.0)
+    message = jnp.concatenate([scores[0:1], stub_ref[1:2, :]], axis=0)
     for peer in range(message_ref.shape[0]):
         message_ref[peer] = message
 
@@ -369,15 +382,15 @@
         tiles.append(jnp.concatenate(parts, axis=0))
     weights = jnp.concatenate([self_ref[...], neigh_ref[...]], axis=0)
     w_out = out_ref[...]
+    before, after = panels(1, near_a_ref[...], near_b_ref[...])
+    sources = [before, own_ref[...], after]
+    if distance == 2:
+        sources = sources[1:] + [panels(2, far_a_ref[...], far_b_ref[...])[1]]
+    summed = mm(jnp.concatenate(tiles, axis=1), jnp.concatenate(sources, axis=0))
     for conf in range(local_confs):
         cols = slice(conf * hid, (conf + 1) * hid)
-        before, after = panels(1, near_a_ref[:, cols], near_b_ref[:, cols])
-        sources = [before, own_ref[:, cols], after]
-        if distance == 2:
-            sources = sources[1:] + [panels(2, far_a_ref[:, cols], far_b_ref[:, cols])[1]]
-        summed = mm(tiles[0], sources[0]) + mm(tiles[1], sources[1]) + mm(tiles[2], sources[2])
-        mean = (summed * inverse).astype(BF16)
-        pre = mm(jnp.concatenate([sources[2], mean], axis=1), weights) + bias_ref[...]
+        mean = (summed[:, cols] * inverse).astype(BF16)
+        pre = mm(jnp.concatenate([sources[2][:, cols], mean], axis=1), weights) + bias_ref[...]
         sigm = sigmoid(pre)
         slope = w_out * (sigm * (1.0 + pre * (1.0 - sigm)))
         expand = expand_ref[:, cols]
@@ -484,25 +497,38 @@
     square = shape((nodes, nodes), F32)
     weight = shape((hid, hid), BF16)
     tile_set = shape((WINDOW, nodes, nodes), BF16)
-    degree_row, segment_row = degrees.reshape(1, nodes), segments.reshape(1, nodes)
     in_hbm = [
         pltpu.with_memory_space_constraint(value, pltpu.HBM)
         for value in (features, tiles, w_self, w_neigh)
     ]
     note_rows = WINDOW * (nodes // local_confs) + 8
     share = -(-note_rows // 16) * 8 if columns == 2 else note_rows
-    own, high, low, payload = kernel_call(
+    own, high, low, payload, degree_row, segment_row, pair_rows, bias_row, out_row = kernel_call(
         functools.partial(parcel_kernel, local_confs),
         (
             narrow,
             tile_set,
             tile_set,
             shape((share, width), BF16),
+            shape((1, nodes), jnp.int32),
+            shape((1, nodes), jnp.int32),
+            shape((3, pairs.shape[0]), jnp.int32),
+            shape((1, hid), F32),
+            shape((1, hid), F32),
         ),
         [pltpu.SMEM] + [pltpu.HBM] * 2,
         "parcel",
         product,
-        (pattern, in_hbm[0], in_hbm[1], degree_row, segment_row),
+        (
+            pattern,
+            in_hbm[0],
+            in_hbm[1],
+            degrees.reshape(1, nodes),
+            segments.reshape(1, nodes),
+            pairs.T,
+            bias.reshape(1, hid),
+            w_out.reshape(1, hid),
+        ),
         (
             pltpu.VMEM((note_rows, width), BF16),
             pltpu.VMEM(tiles.shape, tiles.dtype),
@@ -547,9 +573,9 @@
             low,
             degree_row,
             segment_row,
-            pairs.T,
-            bias.reshape(1, hid),
-            w_out.reshape(1, hid),
+            pair_rows,
+            bias_row,
+            out_row,
         ),
         (pltpu.SemaphoreType.DMA((2,)),),
     )
@@ -563,7 +589,7 @@
             narrow,
             wide,
             shape((slots, hid), F32),
-            shape((rows * columns, 8, slots), F32),
+            shape((rows * columns, 2, slots), F32),
         ),
         [],
         "forward",

time: 48.6 us -> 48.6 us (level)
  waiting for transfers between devices: 5.67 us -> 6.59 us
  Pallas kernels: 13.5 us -> 12.8 us
  local copies, waits for them, and re-layouts: 1.4 us -> 0.77 us
    ppermute x6, waiting for transfers between devices: 1.86 us -> 2.67 us  [exchanged(): lax.ppermute(value, axis, [(source, source ^ bit) for source in range(cou...]
    pallas_call x8, Pallas kernels: 13.5 us -> 12.8 us  [kernel_call(): pl.pallas_call(kernel, out_shape=outs, in_specs=[pl.BlockSpec(memory_spac...]
    unnamed x12, local copies, waits for them, and re-layouts: 1.35 us -> 0.71 us
    ppermute x4, waiting for transfers between devices: 3.26 us -> 3.89 us  [paired(): return lax.ppermute(value, ('groups', 'row'), route)]
    ppermute x2, waiting for transfers between devices: 0.56 us -> 0.03 us  [shifted(): lax.ppermute(value, axis, [(source, source + steps) for source in range(i...]
  transfers between devices with their start and end apart: 12 -> 12, of which waited for: 5 -> 4; matrix products, arithmetic and copies ran while one was open for 0% -> 0% of each run, Pallas kernels for 27% -> 25%
where the time goes in v8:
time: 48.6 us; the launch traced here: 48.3 us
  starting transfers between devices  13.9 us (29%)
  blocking collectives  13.1 us (27%)
  Pallas kernels  12.8 us (26%)
  waiting for transfers between devices  6.59 us (14%)
  between operations  0.92 us (2%)
  local copies, waits for them, and re-layouts  0.77 us (2%)
    all_to_all x1, blocking collectives, body(): received = lax.all_to_all(message, ('row', 'col'), 0, 0, tiled=True)  13.1 us
    pallas_call x8, Pallas kernels, kernel_call(): pl.pallas_call(kernel, out_shape=outs, in_specs=[pl.BlockSpec(memory_spac...  12.8 us
    ppermute x4, starting transfers between devices, paired(): return lax.ppermute(value, ('groups', 'row'), route)  6.52 us
    ppermute x6, starting transfers between devices, exchanged(): lax.ppermute(value, axis, [(source, source ^ bit) for source in range(cou...  4.79 us
    ppermute x4, waiting for transfers between devices, paired(): return lax.ppermute(value, ('groups', 'row'), route)  3.89 us
    ppermute x6, waiting for transfers between devices, exchanged(): lax.ppermute(value, axis, [(source, source ^ bit) for source in range(cou...  2.67 us
    ppermute x2, starting transfers between devices, shifted(): lax.ppermute(value, axis, [(source, source + steps) for source in range(i...  2.58 us
  transfers between devices with their start and end apart: 12, of which 4 were waited for; matrix products, arithmetic and copies ran while one was open for 0% of the time, Pallas kernels for 25%

profile of v8, /device:TPU:0, one launch (start us, length us, event | category | flops | bytes accessed | tf_op | source)
XLA Modules:
  0.0 48.3 jit_solution(5117809595349653853)
XLA Ops:
  0.6 3.1 %collective-permute-start.2 = (bf16[128,1024]{1,0:T(8,128)(2,1)}, bf16[128,1024]{1,0:T(8,128)(2,1)S(1)}, u32[]{:S(2)}, u32[]{:S(2)}) collective-permute-start(bf16[128,1024]{1,0:T(8,128)(2,1)} %features_ref.1), channel_id=1, source_target_pairs={{0,4},{2,6},{4,0},{6,2},{8,12},{10,14},{12,8},{14,10},{16,20},{18,... | collective-permute-start | bytes 786440 | tf_op jit(solution)/shard_map/ppermute | solution.py:33
  3.7 1.5 %collective-permute-start.1 = (bf16[128,1024]{1,0:T(8,128)(2,1)}, bf16[128,1024]{1,0:T(8,128)(2,1)S(1)}, u32[]{:S(2)}, u32[]{:S(2)}) collective-permute-start(bf16[128,1024]{1,0:T(8,128)(2,1)} %features_ref.1), channel_id=1, source_target_pairs={{0,16},{2,4},{4,2},{6,8},{8,6},{10,12},{12,10},{14,30},{16,0},{18,... | collective-permute-start | bytes 786440 | tf_op jit(solution)/shard_map/ppermute | solution.py:33
  5.2 0.0 collective-permute-start
  5.3 1.9 %collective-permute-start.3 = (bf16[128,1024]{1,0:T(8,128)(2,1)}, bf16[128,1024]{1,0:T(8,128)(2,1)S(1)}, u32[]{:S(2)}, u32[]{:S(2)}) collective-permute-start(bf16[128,1024]{1,0:T(8,128)(2,1)} %features_ref.1), channel_id=1, source_target_pairs={{0,16},{2,18},{4,8},{6,10},{8,4},{10,6},{12,28},{14,30},{16,0},{18... | collective-permute-start | bytes 786440 | tf_op jit(solution)/shard_map/ppermute | solution.py:33
  7.2 0.0 copy-start.4
  7.2 0.0 copy-start.5
  7.2 0.0 copy-start
  7.2 0.0 copy-start.1
  7.2 0.0 copy-start.2
  7.2 0.0 copy-start.3
  7.2 0.6 %copy-done.4 = f32[128]{0:T(128)S(1)} copy-done((f32[128]{0:T(128)S(1)}, f32[128]{0:T(128)}, u32[]{:S(2)}) %copy-start.4) | copy-done | bytes 536
  7.8 0.0 copy-done.5
  7.8 0.0 copy-done
  7.9 0.0 copy-done.1
  7.9 0.0 copy-done.2
  7.9 0.0 copy-done.3
  7.9 1.7 %parcel.1 = (bf16[128,1024]{1,0:T(8,128)(2,1)S(1)}, bf16[3,128,128]{2,1,0:T(8,128)(2,1)S(1)}, bf16[3,128,128]{2,1,0:T(8,128)(2,1)S(1)}, bf16[32,1024]{1,0:T(8,12...) custom-call(s32[1,8]{1,0:T(1,128)S(1)} %copy-done.1, ...), custom_call_target="tpu_custom_call" | custom-call | flops 33554432 | bytes 1054240 | tf_op jit(solution)/shard_map/parcel/pallas_call | solution.py:475
  9.6 1.2 %prepare.1 = (bf16[128,128]{1,0:T(8,128)(2,1)S(1)}, bf16[128,128]{1,0:T(8,128)(2,1)S(1)}, f32[1,128]{1,0:T(1,128)S(1)}, f32[1,128]{1,0:T(1,128)S(1)}, f32[128,10...) custom-call(bf16[128,128]{1,0:T(8,128)(2,1)} %self_w_ref.1, ...), custom_call_target="tpu_custom_call" | custom-call | flops 100663296 | bytes 2055936 | tf_op jit(solution)/shard_map/prepare/pallas_call | solution.py:475
  10.8 1.3 %collective-permute-start.5 = (bf16[32,1024]{1,0:T(8,128)(2,1)S(1)}, bf16[32,1024]{1,0:T(8,128)(2,1)S(1)}, u32[]{:S(2)}, u32[]{:S(2)}) collective-permute-start(bf16[32,1024]{1,0:T(8,128)(2,1)S(1)} %get-tuple-element.69), channel_id=1, source_target_pairs={{4,0},{6,2},{8,4},{10,6},{12,8},{14,10},{5,1},{7,3},{9,5},{11,7},{... | collective-permute-start | bytes 196616 | tf_op jit(solution)/shard_map/ppermute | solution.py:39
  12.1 0.0 collective-permute-done.2.far_a_ref
  12.1 1.3 %collective-permute-start.4 = (bf16[32,1024]{1,0:T(8,128)(2,1)S(1)}, bf16[32,1024]{1,0:T(8,128)(2,1)S(1)}, u32[]{:S(2)}, u32[]{:S(2)}) collective-permute-start(bf16[32,1024]{1,0:T(8,128)(2,1)S(1)} %get-tuple-element.69), channel_id=1, source_target_pairs={{2,0},{4,2},{6,4},{8,6},{10,8},{12,10},{14,12},{3,1},{5,3},{7,5},{... | collective-permute-start | bytes 196616 | tf_op jit(solution)/shard_map/ppermute | solution.py:39
  13.4 0.0 collective-permute-done.1.near_b_ref
  13.4 3.8 %collective-permute-done.near_a_ref = bf16[128,1024]{1,0:T(8,128)(2,1)S(1)} collective-permute-done((bf16[128,1024]{1,0:T(8,128)(2,1)}, bf16[128,1024]{1,0:T(8,128)(2,1)S(1)}, u32[]{:S(2)}, u32[]{:S(2)}) %collective-permute-start) | collective-permute-done | bytes 262176 | tf_op jit(solution)/shard_map/ppermute | solution.py:33
  17.2 0.1 collective-permute-done.3.far_b_ref
  17.3 1.0 %forward.1 = (bf16[128,1024]{1,0:T(8,128)(2,1)S(1)}, f32[128,1024]{1,0:T(8,128)S(1)}, f32[128,128]{1,0:T(8,128)S(1)}, f32[16,2,128]{2,1,0:T(2,128)S(1)}) custom-call(bf16[128,1024]{1,0:T(8,128)(2,1)S(1)} %collective-permute-done.near_a_ref, bf16[128,1024]{1,0:T(8,128)(2,1)S(1)} %collective-permute-done.1.near_b_ref, ...), custom_call_target="tpu_custom_call" | custom-call | flops 201326592 | bytes 3265024 | tf_op jit(solution)/shard_map/forward/pallas_call | solution.py:475
  18.3 0.0 collective-permute-done.5.note_ref
  18.3 0.0 collective-permute-done.4.note_ref
  18.4 13.1 %all_to_all.5.received_ref = f32[16,2,128]{2,1,0:T(2,128)S(1)} all-to-all(f32[16,2,128]{2,1,0:T(2,128)S(1)} %get-tuple-element.70), channel_id=1, replica_groups=mesh['groups'=2,'row'=8,'col'=2] {'row','col'}, dimensions={0} | all-to-all | bytes 32768 | tf_op jit(solution)/shard_map/all_to_all | solution.py:600
  31.5 0.1 collective-permute-start.10
  31.5 1.1 %gradient.1 = (f32[264,128]{1,0:T(8,128)S(1)}, f32[1,1]{1,0:T(1,128)}, bf16[128,1024]{1,0:T(8,128)(2,1)S(1)}, f32[8,128]{1,0:T(8,128)S(1)}) custom-call(f32[16,2,128]{2,1,0:T(2,128)S(1)} %all_to_all.5.received_ref, bf16[128,64]{1,0:T(8,128)(2,1)S(1)} %get-tuple-element.74.chosen_ref, f32[128,128]{1,0:T(8,128)S(1)} %get-tuple-element.75.mask_ref, ...), custom_call_target="tpu_custom_call" | custom-call | flops 100663296 | bytes 1875972 | tf_op jit(solution)/shard_map/gradient/pallas_call | solution.py:475
  32.6 0.6 %collective-permute-start.6 = (f32[264,128]{1,0:T(8,128)S(1)}, f32[264,128]{1,0:T(8,128)S(1)}, u32[]{:S(2)}, u32[]{:S(2)}) collective-permute-start(f32[264,128]{1,0:T(8,128)S(1)} %get-tuple-element.81), channel_id=1, source_target_pairs={{0,1},{1,0},{2,3},{3,2},{4,5},{5,4},{6,7},{7,6},{8,9},{9,8},{10,11... | collective-permute-start | bytes 405512 | tf_op jit(solution)/shard_map/ppermute | solution.py:55
  33.2 1.1 %own.1.total_ref = f32[128,1024]{1,0:T(8,128)S(1)} custom-call(bf16[128,1024]{1,0:T(8,128)(2,1)S(1)} %get-tuple-element.83.d_pre_ref, bf16[128,128]{1,0:T(8,128)(2,1)S(1)} %get-tuple-element.84.self_ref, bf16[128,128]{1,0:T(8,128)(2,1)S(1)} %get-tuple-element.60.neigh_ref, f32[128,128]{1,0:T(8,128)S(1)} %get-tuple-element.66.inverse_ref, ...), custom_call_target="tpu_custom_call" | custom-call | flops 134217728 | bytes 1114112 | tf_op jit(solution)/shard_map/own/pallas_call | solution.py:475
  34.3 0.0 collective-permute-done.10
  34.3 0.0 collective-permute-done.6
  34.4 0.5 %collective-permute-start.9 = (bf16[280,128]{1,0:T(8,128)(2,1)S(1)}, bf16[280,128]{1,0:T(8,128)(2,1)S(1)}, u32[]{:S(2)}, u32[]{:S(2)}) collective-permute-start(bf16[280,128]{1,0:T(8,128)(2,1)S(1)} %get-tuple-element.106), channel_id=1, source_target_pairs={{0,6},{2,4},{4,2},{6,0},{8,14},{10,12},{12,10},{14,8},{1,7},{3,5},... | collective-permute-start | bytes 215048 | tf_op jit(solution)/shard_map/ppermute | solution.py:55
  35.0 1.5 %collective-permute-start.8 = (bf16[280,128]{1,0:T(8,128)(2,1)S(1)}, bf16[280,128]{1,0:T(8,128)(2,1)S(1)}, u32[]{:S(2)}, u32[]{:S(2)}) collective-permute-start(bf16[280,128]{1,0:T(8,128)(2,1)S(1)} %get-tuple-element.106), channel_id=1, source_target_pairs={{0,4},{2,6},{4,0},{6,2},{8,12},{10,14},{12,8},{14,10},{1,5},{3,7},... | collective-permute-start | bytes 215048 | tf_op jit(solution)/shard_map/ppermute | solution.py:55
  36.5 1.6 %collective-permute-start.7 = (bf16[280,128]{1,0:T(8,128)(2,1)S(1)}, bf16[280,128]{1,0:T(8,128)(2,1)S(1)}, u32[]{:S(2)}, u32[]{:S(2)}) collective-permute-start(bf16[280,128]{1,0:T(8,128)(2,1)S(1)} %get-tuple-element.106), channel_id=1, source_target_pairs={{0,2},{2,0},{4,6},{6,4},{8,10},{10,8},{12,14},{14,12},{1,3},{3,1},... | collective-permute-start | bytes 215048 | tf_op jit(solution)/shard_map/ppermute | solution.py:55
  38.1 2.7 %later1.1.total_ref = f32[128,1024]{1,0:T(8,128)S(1)} custom-call(f32[8,128]{1,0:T(8,128)S(1)} %get-tuple-element.96.d_row_ref, f32[128,1024]{1,0:T(8,128)S(1)} %own.1.total_ref, bf16[128,1024]{1,0:T(8,128)(2,1)S(1)} %get-tuple-element.52.own_ref, bf16[128,1024]{1,0:T(8,128)(2,1)S(1)} %collective-permute-done.near_a_ref, ...), custom_call_target="tpu_custom_call" | custom-call | flops 335544320 | bytes 2823168 | tf_op jit(solution)/shard_map/later1/pallas_call | solution.py:475
  40.8 0.0 collective-permute-done.9
  40.8 0.4 collective-permute-done.7
  41.3 0.0 collective-permute-done.8
  41.5 0.5 %collective-permute-start.11 = (bf16[280,128]{1,0:T(8,128)(2,1)S(1)}, bf16[280,128]{1,0:T(8,128)(2,1)S(1)}, u32[]{:S(2)}, u32[]{:S(2)}) collective-permute-start(bf16[280,128]{1,0:T(8,128)(2,1)S(1)} %pad_maximum_fusion.2.refs_0_), channel_id=1, source_target_pairs={{0,8},{2,10},{4,12},{6,14},{8,0},{10,2},{12,4},{14,6},{1,9},{3,11}... | collective-permute-start | bytes 215048 | tf_op jit(solution)/shard_map/ppermute | solution.py:55
  42.0 3.4 %later2.1 = bf16[128,1024]{1,0:T(8,128)(2,1)} custom-call(f32[8,128]{1,0:T(8,128)S(1)} %get-tuple-element.96.d_row_ref, f32[128,1024]{1,0:T(8,128)S(1)} %later1.1.total_ref, bf16[128,1024]{1,0:T(8,128)(2,1)S(1)} %get-tuple-element.52.own_ref, bf16[128,1024]{1,0:T(8,128)(2,1)S(1)} %collective-permute-done.near_a_ref, ...), custom_call_target="tpu_custom_call" | custom-call | flops 335544320 | bytes 2561024 | tf_op jit(solution)/shard_map/later2/pallas_call | solution.py:475
  45.4 2.2 %collective-permute-done.11.refs_1_ = bf16[280,128]{1,0:T(8,128)(2,1)S(1)} collective-permute-done((bf16[280,128]{1,0:T(8,128)(2,1)S(1)}, bf16[280,128]{1,0:T(8,128)(2,1)S(1)}, u32[]{:S(2)}, u32[]{:S(2)}) %collective-permute-start.11) | collective-permute-done | bytes 71712 | tf_op jit(solution)/shard_map/ppermute | solution.py:55
  47.6 0.7 %finish.1 = (f32[128,128]{1,0:T(8,128)}, f32[128,128]{1,0:T(8,128)}, f32[1,128]{1,0:T(1,128)}, f32[1,128]{1,0:T(1,128)}) custom-call(bf16[280,128]{1,0:T(8,128)(2,1)S(1)} %pad_maximum_fusion.2.refs_0_, bf16[280,128]{1,0:T(8,128)(2,1)S(1)} %collective-permute-done.11.refs_1_), custom_call_target="tpu_custom_call" | custom-call | flops 1048576 | bytes 275456 | tf_op jit(solution)/shard_map/finish/pallas_call | solution.py:475
  (21 shorter events, 0.2 us)
Async XLA Ops:
  0.6 11.5 %collective-permute-start.2 = (bf16[128,1024]{1,0:T(8,128)(2,1)}, bf16[128,1024]{1,0:T(8,128)(2,1)S(1)}, u32[]{:S(2)}, u32[]{:S(2)}) collective-permute-start(bf16[128,1024]{1,0:T(8,128)(2,1)} %features_ref.1), channel_id=1, source_target_pairs={{0,4},{2,6},{4,0},{6,2},{8,12},{10,14},{12,8},{14,10},{16,20},{18,... | collective-permute-start | bytes 786440 | tf_op jit(solution)/shard_map/ppermute | solution.py:33
  3.7 9.7 %collective-permute-start.1 = (bf16[128,1024]{1,0:T(8,128)(2,1)}, bf16[128,1024]{1,0:T(8,128)(2,1)S(1)}, u32[]{:S(2)}, u32[]{:S(2)}) collective-permute-start(bf16[128,1024]{1,0:T(8,128)(2,1)} %features_ref.1), channel_id=1, source_target_pairs={{0,16},{2,4},{4,2},{6,8},{8,6},{10,12},{12,10},{14,30},{16,0},{18,... | collective-permute-start | bytes 786440 | tf_op jit(solution)/shard_map/ppermute | solution.py:33
  5.2 12.0 %collective-permute-start = (bf16[128,1024]{1,0:T(8,128)(2,1)}, bf16[128,1024]{1,0:T(8,128)(2,1)S(1)}, u32[]{:S(2)}, u32[]{:S(2)}) collective-permute-start(bf16[128,1024]{1,0:T(8,128)(2,1)} %features_ref.1), channel_id=1, source_target_pairs={{0,2},{2,0},{4,6},{6,4},{8,10},{10,8},{12,14},{14,12},{16,18},{18,... | collective-permute-start | bytes 786440 | tf_op jit(solution)/shard_map/ppermute | solution.py:33
  5.3 12.1 %collective-permute-start.3 = (bf16[128,1024]{1,0:T(8,128)(2,1)}, bf16[128,1024]{1,0:T(8,128)(2,1)S(1)}, u32[]{:S(2)}, u32[]{:S(2)}) collective-permute-start(bf16[128,1024]{1,0:T(8,128)(2,1)} %features_ref.1), channel_id=1, source_target_pairs={{0,16},{2,18},{4,8},{6,10},{8,4},{10,6},{12,28},{14,30},{16,0},{18... | collective-permute-start | bytes 786440 | tf_op jit(solution)/shard_map/ppermute | solution.py:33
  7.2 0.7 %copy-start.4 = (f32[128]{0:T(128)S(1)}, f32[128]{0:T(128)}, u32[]{:S(2)}) copy-start(f32[128]{0:T(128)} %param.18) | copy-start | bytes 1540
  7.2 0.7 %copy-start.5 = (f32[128]{0:T(128)S(1)}, f32[128]{0:T(128)}, u32[]{:S(2)}) copy-start(f32[128]{0:T(128)} %param.19) | copy-start | bytes 1540
  7.2 0.7 %copy-start = (s32[64,3]{0,1:T(4,128)S(1)}, s32[64,3]{0,1:T(4,128)}, u32[]{:S(2)}) copy-start(s32[64,3]{0,1:T(4,128)} %param.15) | copy-start | bytes 2308
  7.2 0.7 %copy-start.1 = (s32[1,8]{1,0:T(1,128)S(1)}, s32[1,8]{1,0:T(1,128)}, u32[]{:S(2)}) copy-start(s32[1,8]{1,0:T(1,128)} %pattern_ref.1) | copy-start | bytes 100
  7.2 0.7 %copy-start.2 = (s32[128]{0:T(128)S(1)}, s32[128]{0:T(128)}, u32[]{:S(2)}) copy-start(s32[128]{0:T(128)} %param.13) | copy-start | bytes 1540
  7.2 0.7 %copy-start.3 = (s32[128]{0:T(128)S(1)}, s32[128]{0:T(128)}, u32[]{:S(2)}) copy-start(s32[128]{0:T(128)} %param.14) | copy-start | bytes 1540
  10.8 7.5 %collective-permute-start.5 = (bf16[32,1024]{1,0:T(8,128)(2,1)S(1)}, bf16[32,1024]{1,0:T(8,128)(2,1)S(1)}, u32[]{:S(2)}, u32[]{:S(2)}) collective-permute-start(bf16[32,1024]{1,0:T(8,128)(2,1)S(1)} %get-tuple-element.69), channel_id=1, source_target_pairs={{4,0},{6,2},{8,4},{10,6},{12,8},{14,10},{5,1},{7,3},{9,5},{11,7},{... | collective-permute-start | bytes 196616 | tf_op jit(solution)/shard_map/ppermute | solution.py:39
  12.1 6.2 %collective-permute-start.4 = (bf16[32,1024]{1,0:T(8,128)(2,1)S(1)}, bf16[32,1024]{1,0:T(8,128)(2,1)S(1)}, u32[]{:S(2)}, u32[]{:S(2)}) collective-permute-start(bf16[32,1024]{1,0:T(8,128)(2,1)S(1)} %get-tuple-element.69), channel_id=1, source_target_pairs={{2,0},{4,2},{6,4},{8,6},{10,8},{12,10},{14,12},{3,1},{5,3},{7,5},{... | collective-permute-start | bytes 196616 | tf_op jit(solution)/shard_map/ppermute | solution.py:39
  31.5 2.8 %collective-permute-start.10 = (bf16[64,1024]{1,0:T(8,128)(2,1)S(1)}, bf16[64,1024]{1,0:T(8,128)(2,1)S(1)}, u32[]{:S(2)}, u32[]{:S(2)}) collective-permute-start(bf16[64,1024]{1,0:T(8,128)(2,1)S(1)} %pad_maximum_fusion), channel_id=1, source_target_pairs={{0,1},{1,0},{2,3},{3,2},{4,5},{5,4},{6,7},{7,6},{8,9},{9,8},{10,11... | collective-permute-start | bytes 393224 | tf_op jit(solution)/shard_map/ppermute | solution.py:55
  32.6 1.7 %collective-permute-start.6 = (f32[264,128]{1,0:T(8,128)S(1)}, f32[264,128]{1,0:T(8,128)S(1)}, u32[]{:S(2)}, u32[]{:S(2)}) collective-permute-start(f32[264,128]{1,0:T(8,128)S(1)} %get-tuple-element.81), channel_id=1, source_target_pairs={{0,1},{1,0},{2,3},{3,2},{4,5},{5,4},{6,7},{7,6},{8,9},{9,8},{10,11... | collective-permute-start | bytes 405512 | tf_op jit(solution)/shard_map/ppermute | solution.py:55
  34.4 6.3 %collective-permute-start.9 = (bf16[280,128]{1,0:T(8,128)(2,1)S(1)}, bf16[280,128]{1,0:T(8,128)(2,1)S(1)}, u32[]{:S(2)}, u32[]{:S(2)}) collective-permute-start(bf16[280,128]{1,0:T(8,128)(2,1)S(1)} %get-tuple-element.106), channel_id=1, source_target_pairs={{0,6},{2,4},{4,2},{6,0},{8,14},{10,12},{12,10},{14,8},{1,7},{3,5},... | collective-permute-start | bytes 215048 | tf_op jit(solution)/shard_map/ppermute | solution.py:55
  35.0 6.3 %collective-permute-start.8 = (bf16[280,128]{1,0:T(8,128)(2,1)S(1)}, bf16[280,128]{1,0:T(8,128)(2,1)S(1)}, u32[]{:S(2)}, u32[]{:S(2)}) collective-permute-start(bf16[280,128]{1,0:T(8,128)(2,1)S(1)} %get-tuple-element.106), channel_id=1, source_target_pairs={{0,4},{2,6},{4,0},{6,2},{8,12},{10,14},{12,8},{14,10},{1,5},{3,7},... | collective-permute-start | bytes 215048 | tf_op jit(solution)/shard_map/ppermute | solution.py:55
  36.5 4.8 %collective-permute-start.7 = (bf16[280,128]{1,0:T(8,128)(2,1)S(1)}, bf16[280,128]{1,0:T(8,128)(2,1)S(1)}, u32[]{:S(2)}, u32[]{:S(2)}) collective-permute-start(bf16[280,128]{1,0:T(8,128)(2,1)S(1)} %get-tuple-element.106), channel_id=1, source_target_pairs={{0,2},{2,0},{4,6},{6,4},{8,10},{10,8},{12,14},{14,12},{1,3},{3,1},... | collective-permute-start | bytes 215048 | tf_op jit(solution)/shard_map/ppermute | solution.py:55
  41.5 6.1 %collective-permute-start.11 = (bf16[280,128]{1,0:T(8,128)(2,1)S(1)}, bf16[280,128]{1,0:T(8,128)(2,1)S(1)}, u32[]{:S(2)}, u32[]{:S(2)}) collective-permute-start(bf16[280,128]{1,0:T(8,128)(2,1)S(1)} %pad_maximum_fusion.2.refs_0_), channel_id=1, source_target_pairs={{0,8},{2,10},{4,12},{6,14},{8,0},{10,2},{12,4},{14,6},{1,9},{3,11}... | collective-permute-start | bytes 215048 | tf_op jit(solution)/shard_map/ppermute | solution.py:55

commit v9 on v8

--- a/solution.py
+++ b/solution.py
@@ -299,13 +299,13 @@
     d_rows = jnp.broadcast_to(d_row, d_row_ref.shape)
     d_row_ref[...] = d_rows
     factors = split_three(mask_ref[...] * d_row)
+    expand = expand_ref[...]
+    d_node = mm(factors[0], expand) + mm(factors[1], expand) + mm(factors[2], expand)
     grads = None
     d_bias = None
     for conf in range(local_confs):
         cols = slice(conf * hid, (conf + 1) * hid)
-        expand = expand_ref[:, cols]
-        d_node = mm(factors[0], expand) + mm(factors[1], expand) + mm(factors[2], expand)
-        d_pre = d_node * slope_ref[:, cols]
+        d_pre = d_node[:, cols] * slope_ref[:, cols]
         d_pre_b = d_pre.astype(BF16)
         d_pre_ref[:, cols] = d_pre_b
         rows = jnp.concatenate([own_ref[:, cols], mean_ref[:, cols]], axis=1)

time: 48.6 us -> 48.5 us (level)
  no operation moved by 1% of the time
where the time goes in v9:
time: 48.5 us; the launch traced here: 48.2 us
  starting transfers between devices  13.9 us (29%)
  blocking collectives  13.1 us (27%)
  Pallas kernels  12.8 us (26%)
  waiting for transfers between devices  6.59 us (14%)
  between operations  0.92 us (2%)
  local copies, waits for them, and re-layouts  0.77 us (2%)
    all_to_all x1, blocking collectives, body(): received = lax.all_to_all(message, ('row', 'col'), 0, 0, tiled=True)  13.1 us
    pallas_call x8, Pallas kernels, kernel_call(): pl.pallas_call(kernel, out_shape=outs, in_specs=[pl.BlockSpec(memory_spac...  12.8 us
    ppermute x4, starting transfers between devices, paired(): return lax.ppermute(value, ('groups', 'row'), route)  6.52 us
    ppermute x6, starting transfers between devices, exchanged(): lax.ppermute(value, axis, [(source, source ^ bit) for source in range(cou...  4.79 us
    ppermute x4, waiting for transfers between devices, paired(): return lax.ppermute(value, ('groups', 'row'), route)  3.89 us
    ppermute x6, waiting for transfers between devices, exchanged(): lax.ppermute(value, axis, [(source, source ^ bit) for source in range(cou...  2.67 us
    ppermute x2, starting transfers between devices, shifted(): lax.ppermute(value, axis, [(source, source + steps) for source in range(i...  2.58 us
  transfers between devices with their start and end apart: 12, of which 4 were waited for; matrix products, arithmetic and copies ran while one was open for 0% of the time, Pallas kernels for 25%

profile of v9, /device:TPU:0, one launch (start us, length us, event | category | flops | bytes accessed | tf_op | source)
XLA Modules:
  0.0 48.2 jit_solution(4356673129148690430)
XLA Ops:
  0.6 3.1 %collective-permute-start.2 = (bf16[128,1024]{1,0:T(8,128)(2,1)}, bf16[128,1024]{1,0:T(8,128)(2,1)S(1)}, u32[]{:S(2)}, u32[]{:S(2)}) collective-permute-start(bf16[128,1024]{1,0:T(8,128)(2,1)} %features_ref.1), channel_id=1, source_target_pairs={{0,4},{2,6},{4,0},{6,2},{8,12},{10,14},{12,8},{14,10},{16,20},{18,... | collective-permute-start | bytes 786440 | tf_op jit(solution)/shard_map/ppermute | solution.py:33
  3.7 1.5 %collective-permute-start.1 = (bf16[128,1024]{1,0:T(8,128)(2,1)}, bf16[128,1024]{1,0:T(8,128)(2,1)S(1)}, u32[]{:S(2)}, u32[]{:S(2)}) collective-permute-start(bf16[128,1024]{1,0:T(8,128)(2,1)} %features_ref.1), channel_id=1, source_target_pairs={{0,16},{2,4},{4,2},{6,8},{8,6},{10,12},{12,10},{14,30},{16,0},{18,... | collective-permute-start | bytes 786440 | tf_op jit(solution)/shard_map/ppermute | solution.py:33
  5.2 0.0 collective-permute-start
  5.3 1.9 %collective-permute-start.3 = (bf16[128,1024]{1,0:T(8,128)(2,1)}, bf16[128,1024]{1,0:T(8,128)(2,1)S(1)}, u32[]{:S(2)}, u32[]{:S(2)}) collective-permute-start(bf16[128,1024]{1,0:T(8,128)(2,1)} %features_ref.1), channel_id=1, source_target_pairs={{0,16},{2,18},{4,8},{6,10},{8,4},{10,6},{12,28},{14,30},{16,0},{18... | collective-permute-start | bytes 786440 | tf_op jit(solution)/shard_map/ppermute | solution.py:33
  7.2 0.0 copy-start.4
  7.2 0.0 copy-start.5
  7.2 0.0 copy-start
  7.2 0.0 copy-start.1
  7.2 0.0 copy-start.2
  7.2 0.0 copy-start.3
  7.2 0.6 %copy-done.4 = f32[128]{0:T(128)S(1)} copy-done((f32[128]{0:T(128)S(1)}, f32[128]{0:T(128)}, u32[]{:S(2)}) %copy-start.4) | copy-done | bytes 536
  7.8 0.0 copy-done.5
  7.8 0.0 copy-done
  7.9 0.0 copy-done.1
  7.9 0.0 copy-done.2
  7.9 0.0 copy-done.3
  7.9 1.7 %parcel.1 = (bf16[128,1024]{1,0:T(8,128)(2,1)S(1)}, bf16[3,128,128]{2,1,0:T(8,128)(2,1)S(1)}, bf16[3,128,128]{2,1,0:T(8,128)(2,1)S(1)}, bf16[32,1024]{1,0:T(8,12...) custom-call(s32[1,8]{1,0:T(1,128)S(1)} %copy-done.1, ...), custom_call_target="tpu_custom_call" | custom-call | flops 33554432 | bytes 1054240 | tf_op jit(solution)/shard_map/parcel/pallas_call | solution.py:475
  9.6 1.2 %prepare.1 = (bf16[128,128]{1,0:T(8,128)(2,1)S(1)}, bf16[128,128]{1,0:T(8,128)(2,1)S(1)}, f32[1,128]{1,0:T(1,128)S(1)}, f32[1,128]{1,0:T(1,128)S(1)}, f32[128,10...) custom-call(bf16[128,128]{1,0:T(8,128)(2,1)} %self_w_ref.1, ...), custom_call_target="tpu_custom_call" | custom-call | flops 100663296 | bytes 2055936 | tf_op jit(solution)/shard_map/prepare/pallas_call | solution.py:475
  10.8 1.3 %collective-permute-start.5 = (bf16[32,1024]{1,0:T(8,128)(2,1)S(1)}, bf16[32,1024]{1,0:T(8,128)(2,1)S(1)}, u32[]{:S(2)}, u32[]{:S(2)}) collective-permute-start(bf16[32,1024]{1,0:T(8,128)(2,1)S(1)} %get-tuple-element.69), channel_id=1, source_target_pairs={{4,0},{6,2},{8,4},{10,6},{12,8},{14,10},{5,1},{7,3},{9,5},{11,7},{... | collective-permute-start | bytes 196616 | tf_op jit(solution)/shard_map/ppermute | solution.py:39
  12.1 0.0 collective-permute-done.2.far_a_ref
  12.1 1.3 %collective-permute-start.4 = (bf16[32,1024]{1,0:T(8,128)(2,1)S(1)}, bf16[32,1024]{1,0:T(8,128)(2,1)S(1)}, u32[]{:S(2)}, u32[]{:S(2)}) collective-permute-start(bf16[32,1024]{1,0:T(8,128)(2,1)S(1)} %get-tuple-element.69), channel_id=1, source_target_pairs={{2,0},{4,2},{6,4},{8,6},{10,8},{12,10},{14,12},{3,1},{5,3},{7,5},{... | collective-permute-start | bytes 196616 | tf_op jit(solution)/shard_map/ppermute | solution.py:39
  13.4 0.0 collective-permute-done.1.near_b_ref
  13.4 3.8 %collective-permute-done.near_a_ref = bf16[128,1024]{1,0:T(8,128)(2,1)S(1)} collective-permute-done((bf16[128,1024]{1,0:T(8,128)(2,1)}, bf16[128,1024]{1,0:T(8,128)(2,1)S(1)}, u32[]{:S(2)}, u32[]{:S(2)}) %collective-permute-start) | collective-permute-done | bytes 262176 | tf_op jit(solution)/shard_map/ppermute | solution.py:33
  17.2 0.1 collective-permute-done.3.far_b_ref
  17.3 1.0 %forward.1 = (bf16[128,1024]{1,0:T(8,128)(2,1)S(1)}, f32[128,1024]{1,0:T(8,128)S(1)}, f32[128,128]{1,0:T(8,128)S(1)}, f32[16,2,128]{2,1,0:T(2,128)S(1)}) custom-call(bf16[128,1024]{1,0:T(8,128)(2,1)S(1)} %collective-permute-done.near_a_ref, bf16[128,1024]{1,0:T(8,128)(2,1)S(1)} %collective-permute-done.1.near_b_ref, ...), custom_call_target="tpu_custom_call" | custom-call | flops 201326592 | bytes 3265024 | tf_op jit(solution)/shard_map/forward/pallas_call | solution.py:475
  18.3 0.0 collective-permute-done.5.note_ref
  18.3 0.0 collective-permute-done.4.note_ref
  18.4 13.1 %all_to_all.5.received_ref = f32[16,2,128]{2,1,0:T(2,128)S(1)} all-to-all(f32[16,2,128]{2,1,0:T(2,128)S(1)} %get-tuple-element.70), channel_id=1, replica_groups=mesh['groups'=2,'row'=8,'col'=2] {'row','col'}, dimensions={0} | all-to-all | bytes 32768 | tf_op jit(solution)/shard_map/all_to_all | solution.py:600
  31.5 0.1 collective-permute-start.10
  31.5 1.0 %gradient.1 = (f32[264,128]{1,0:T(8,128)S(1)}, f32[1,1]{1,0:T(1,128)}, bf16[128,1024]{1,0:T(8,128)(2,1)S(1)}, f32[8,128]{1,0:T(8,128)S(1)}) custom-call(f32[16,2,128]{2,1,0:T(2,128)S(1)} %all_to_all.5.received_ref, bf16[128,64]{1,0:T(8,128)(2,1)S(1)} %get-tuple-element.74.chosen_ref, f32[128,128]{1,0:T(8,128)S(1)} %get-tuple-element.75.mask_ref, ...), custom_call_target="tpu_custom_call" | custom-call | flops 100663296 | bytes 1875972 | tf_op jit(solution)/shard_map/gradient/pallas_call | solution.py:475
  32.6 0.6 %collective-permute-start.6 = (f32[264,128]{1,0:T(8,128)S(1)}, f32[264,128]{1,0:T(8,128)S(1)}, u32[]{:S(2)}, u32[]{:S(2)}) collective-permute-start(f32[264,128]{1,0:T(8,128)S(1)} %get-tuple-element.81), channel_id=1, source_target_pairs={{0,1},{1,0},{2,3},{3,2},{4,5},{5,4},{6,7},{7,6},{8,9},{9,8},{10,11... | collective-permute-start | bytes 405512 | tf_op jit(solution)/shard_map/ppermute | solution.py:55
  33.1 1.1 %own.1.total_ref = f32[128,1024]{1,0:T(8,128)S(1)} custom-call(bf16[128,1024]{1,0:T(8,128)(2,1)S(1)} %get-tuple-element.83.d_pre_ref, bf16[128,128]{1,0:T(8,128)(2,1)S(1)} %get-tuple-element.84.self_ref, bf16[128,128]{1,0:T(8,128)(2,1)S(1)} %get-tuple-element.60.neigh_ref, f32[128,128]{1,0:T(8,128)S(1)} %get-tuple-element.66.inverse_ref, ...), custom_call_target="tpu_custom_call" | custom-call | flops 134217728 | bytes 1114112 | tf_op jit(solution)/shard_map/own/pallas_call | solution.py:475
  34.2 0.0 collective-permute-done.10
  34.3 0.0 collective-permute-done.6
  34.4 0.5 %collective-permute-start.9 = (bf16[280,128]{1,0:T(8,128)(2,1)S(1)}, bf16[280,128]{1,0:T(8,128)(2,1)S(1)}, u32[]{:S(2)}, u32[]{:S(2)}) collective-permute-start(bf16[280,128]{1,0:T(8,128)(2,1)S(1)} %get-tuple-element.106), channel_id=1, source_target_pairs={{0,6},{2,4},{4,2},{6,0},{8,14},{10,12},{12,10},{14,8},{1,7},{3,5},... | collective-permute-start | bytes 215048 | tf_op jit(solution)/shard_map/ppermute | solution.py:55
  34.9 1.5 %collective-permute-start.8 = (bf16[280,128]{1,0:T(8,128)(2,1)S(1)}, bf16[280,128]{1,0:T(8,128)(2,1)S(1)}, u32[]{:S(2)}, u32[]{:S(2)}) collective-permute-start(bf16[280,128]{1,0:T(8,128)(2,1)S(1)} %get-tuple-element.106), channel_id=1, source_target_pairs={{0,4},{2,6},{4,0},{6,2},{8,12},{10,14},{12,8},{14,10},{1,5},{3,7},... | collective-permute-start | bytes 215048 | tf_op jit(solution)/shard_map/ppermute | solution.py:55
  36.4 1.6 %collective-permute-start.7 = (bf16[280,128]{1,0:T(8,128)(2,1)S(1)}, bf16[280,128]{1,0:T(8,128)(2,1)S(1)}, u32[]{:S(2)}, u32[]{:S(2)}) collective-permute-start(bf16[280,128]{1,0:T(8,128)(2,1)S(1)} %get-tuple-element.106), channel_id=1, source_target_pairs={{0,2},{2,0},{4,6},{6,4},{8,10},{10,8},{12,14},{14,12},{1,3},{3,1},... | collective-permute-start | bytes 215048 | tf_op jit(solution)/shard_map/ppermute | solution.py:55
  38.0 2.7 %later1.1.total_ref = f32[128,1024]{1,0:T(8,128)S(1)} custom-call(f32[8,128]{1,0:T(8,128)S(1)} %get-tuple-element.96.d_row_ref, f32[128,1024]{1,0:T(8,128)S(1)} %own.1.total_ref, bf16[128,1024]{1,0:T(8,128)(2,1)S(1)} %get-tuple-element.52.own_ref, bf16[128,1024]{1,0:T(8,128)(2,1)S(1)} %collective-permute-done.near_a_ref, ...), custom_call_target="tpu_custom_call" | custom-call | flops 335544320 | bytes 2823168 | tf_op jit(solution)/shard_map/later1/pallas_call | solution.py:475
  40.7 0.0 collective-permute-done.9
  40.7 0.4 collective-permute-done.7
  41.2 0.0 collective-permute-done.8
  41.4 0.5 %collective-permute-start.11 = (bf16[280,128]{1,0:T(8,128)(2,1)S(1)}, bf16[280,128]{1,0:T(8,128)(2,1)S(1)}, u32[]{:S(2)}, u32[]{:S(2)}) collective-permute-start(bf16[280,128]{1,0:T(8,128)(2,1)S(1)} %pad_maximum_fusion.2.refs_0_), channel_id=1, source_target_pairs={{0,8},{2,10},{4,12},{6,14},{8,0},{10,2},{12,4},{14,6},{1,9},{3,11}... | collective-permute-start | bytes 215048 | tf_op jit(solution)/shard_map/ppermute | solution.py:55
  41.9 3.4 %later2.1 = bf16[128,1024]{1,0:T(8,128)(2,1)} custom-call(f32[8,128]{1,0:T(8,128)S(1)} %get-tuple-element.96.d_row_ref, f32[128,1024]{1,0:T(8,128)S(1)} %later1.1.total_ref, bf16[128,1024]{1,0:T(8,128)(2,1)S(1)} %get-tuple-element.52.own_ref, bf16[128,1024]{1,0:T(8,128)(2,1)S(1)} %collective-permute-done.near_a_ref, ...), custom_call_target="tpu_custom_call" | custom-call | flops 335544320 | bytes 2561024 | tf_op jit(solution)/shard_map/later2/pallas_call | solution.py:475
  45.3 2.2 %collective-permute-done.11.refs_1_ = bf16[280,128]{1,0:T(8,128)(2,1)S(1)} collective-permute-done((bf16[280,128]{1,0:T(8,128)(2,1)S(1)}, bf16[280,128]{1,0:T(8,128)(2,1)S(1)}, u32[]{:S(2)}, u32[]{:S(2)}) %collective-permute-start.11) | collective-permute-done | bytes 71712 | tf_op jit(solution)/shard_map/ppermute | solution.py:55
  47.5 0.7 %finish.1 = (f32[128,128]{1,0:T(8,128)}, f32[128,128]{1,0:T(8,128)}, f32[1,128]{1,0:T(1,128)}, f32[1,128]{1,0:T(1,128)}) custom-call(bf16[280,128]{1,0:T(8,128)(2,1)S(1)} %pad_maximum_fusion.2.refs_0_, bf16[280,128]{1,0:T(8,128)(2,1)S(1)} %collective-permute-done.11.refs_1_), custom_call_target="tpu_custom_call" | custom-call | flops 1048576 | bytes 275456 | tf_op jit(solution)/shard_map/finish/pallas_call | solution.py:475
  (21 shorter events, 0.2 us)
Async XLA Ops:
  0.6 11.5 %collective-permute-start.2 = (bf16[128,1024]{1,0:T(8,128)(2,1)}, bf16[128,1024]{1,0:T(8,128)(2,1)S(1)}, u32[]{:S(2)}, u32[]{:S(2)}) collective-permute-start(bf16[128,1024]{1,0:T(8,128)(2,1)} %features_ref.1), channel_id=1, source_target_pairs={{0,4},{2,6},{4,0},{6,2},{8,12},{10,14},{12,8},{14,10},{16,20},{18,... | collective-permute-start | bytes 786440 | tf_op jit(solution)/shard_map/ppermute | solution.py:33
  3.7 9.7 %collective-permute-start.1 = (bf16[128,1024]{1,0:T(8,128)(2,1)}, bf16[128,1024]{1,0:T(8,128)(2,1)S(1)}, u32[]{:S(2)}, u32[]{:S(2)}) collective-permute-start(bf16[128,1024]{1,0:T(8,128)(2,1)} %features_ref.1), channel_id=1, source_target_pairs={{0,16},{2,4},{4,2},{6,8},{8,6},{10,12},{12,10},{14,30},{16,0},{18,... | collective-permute-start | bytes 786440 | tf_op jit(solution)/shard_map/ppermute | solution.py:33
  5.2 12.0 %collective-permute-start = (bf16[128,1024]{1,0:T(8,128)(2,1)}, bf16[128,1024]{1,0:T(8,128)(2,1)S(1)}, u32[]{:S(2)}, u32[]{:S(2)}) collective-permute-start(bf16[128,1024]{1,0:T(8,128)(2,1)} %features_ref.1), channel_id=1, source_target_pairs={{0,2},{2,0},{4,6},{6,4},{8,10},{10,8},{12,14},{14,12},{16,18},{18,... | collective-permute-start | bytes 786440 | tf_op jit(solution)/shard_map/ppermute | solution.py:33
  5.3 12.1 %collective-permute-start.3 = (bf16[128,1024]{1,0:T(8,128)(2,1)}, bf16[128,1024]{1,0:T(8,128)(2,1)S(1)}, u32[]{:S(2)}, u32[]{:S(2)}) collective-permute-start(bf16[128,1024]{1,0:T(8,128)(2,1)} %features_ref.1), channel_id=1, source_target_pairs={{0,16},{2,18},{4,8},{6,10},{8,4},{10,6},{12,28},{14,30},{16,0},{18... | collective-permute-start | bytes 786440 | tf_op jit(solution)/shard_map/ppermute | solution.py:33
  7.2 0.7 %copy-start.4 = (f32[128]{0:T(128)S(1)}, f32[128]{0:T(128)}, u32[]{:S(2)}) copy-start(f32[128]{0:T(128)} %param.18) | copy-start | bytes 1540
  7.2 0.7 %copy-start.5 = (f32[128]{0:T(128)S(1)}, f32[128]{0:T(128)}, u32[]{:S(2)}) copy-start(f32[128]{0:T(128)} %param.19) | copy-start | bytes 1540
  7.2 0.7 %copy-start = (s32[64,3]{0,1:T(4,128)S(1)}, s32[64,3]{0,1:T(4,128)}, u32[]{:S(2)}) copy-start(s32[64,3]{0,1:T(4,128)} %param.15) | copy-start | bytes 2308
  7.2 0.7 %copy-start.1 = (s32[1,8]{1,0:T(1,128)S(1)}, s32[1,8]{1,0:T(1,128)}, u32[]{:S(2)}) copy-start(s32[1,8]{1,0:T(1,128)} %pattern_ref.1) | copy-start | bytes 100
  7.2 0.7 %copy-start.2 = (s32[128]{0:T(128)S(1)}, s32[128]{0:T(128)}, u32[]{:S(2)}) copy-start(s32[128]{0:T(128)} %param.13) | copy-start | bytes 1540
  7.2 0.7 %copy-start.3 = (s32[128]{0:T(128)S(1)}, s32[128]{0:T(128)}, u32[]{:S(2)}) copy-start(s32[128]{0:T(128)} %param.14) | copy-start | bytes 1540
  10.8 7.5 %collective-permute-start.5 = (bf16[32,1024]{1,0:T(8,128)(2,1)S(1)}, bf16[32,1024]{1,0:T(8,128)(2,1)S(1)}, u32[]{:S(2)}, u32[]{:S(2)}) collective-permute-start(bf16[32,1024]{1,0:T(8,128)(2,1)S(1)} %get-tuple-element.69), channel_id=1, source_target_pairs={{4,0},{6,2},{8,4},{10,6},{12,8},{14,10},{5,1},{7,3},{9,5},{11,7},{... | collective-permute-start | bytes 196616 | tf_op jit(solution)/shard_map/ppermute | solution.py:39
  12.1 6.2 %collective-permute-start.4 = (bf16[32,1024]{1,0:T(8,128)(2,1)S(1)}, bf16[32,1024]{1,0:T(8,128)(2,1)S(1)}, u32[]{:S(2)}, u32[]{:S(2)}) collective-permute-start(bf16[32,1024]{1,0:T(8,128)(2,1)S(1)} %get-tuple-element.69), channel_id=1, source_target_pairs={{2,0},{4,2},{6,4},{8,6},{10,8},{12,10},{14,12},{3,1},{5,3},{7,5},{... | collective-permute-start | bytes 196616 | tf_op jit(solution)/shard_map/ppermute | solution.py:39
  31.5 2.8 %collective-permute-start.10 = (bf16[64,1024]{1,0:T(8,128)(2,1)S(1)}, bf16[64,1024]{1,0:T(8,128)(2,1)S(1)}, u32[]{:S(2)}, u32[]{:S(2)}) collective-permute-start(bf16[64,1024]{1,0:T(8,128)(2,1)S(1)} %pad_maximum_fusion), channel_id=1, source_target_pairs={{0,1},{1,0},{2,3},{3,2},{4,5},{5,4},{6,7},{7,6},{8,9},{9,8},{10,11... | collective-permute-start | bytes 393224 | tf_op jit(solution)/shard_map/ppermute | solution.py:55
  32.6 1.7 %collective-permute-start.6 = (f32[264,128]{1,0:T(8,128)S(1)}, f32[264,128]{1,0:T(8,128)S(1)}, u32[]{:S(2)}, u32[]{:S(2)}) collective-permute-start(f32[264,128]{1,0:T(8,128)S(1)} %get-tuple-element.81), channel_id=1, source_target_pairs={{0,1},{1,0},{2,3},{3,2},{4,5},{5,4},{6,7},{7,6},{8,9},{9,8},{10,11... | collective-permute-start | bytes 405512 | tf_op jit(solution)/shard_map/ppermute | solution.py:55
  34.4 6.3 %collective-permute-start.9 = (bf16[280,128]{1,0:T(8,128)(2,1)S(1)}, bf16[280,128]{1,0:T(8,128)(2,1)S(1)}, u32[]{:S(2)}, u32[]{:S(2)}) collective-permute-start(bf16[280,128]{1,0:T(8,128)(2,1)S(1)} %get-tuple-element.106), channel_id=1, source_target_pairs={{0,6},{2,4},{4,2},{6,0},{8,14},{10,12},{12,10},{14,8},{1,7},{3,5},... | collective-permute-start | bytes 215048 | tf_op jit(solution)/shard_map/ppermute | solution.py:55
  34.9 6.3 %collective-permute-start.8 = (bf16[280,128]{1,0:T(8,128)(2,1)S(1)}, bf16[280,128]{1,0:T(8,128)(2,1)S(1)}, u32[]{:S(2)}, u32[]{:S(2)}) collective-permute-start(bf16[280,128]{1,0:T(8,128)(2,1)S(1)} %get-tuple-element.106), channel_id=1, source_target_pairs={{0,4},{2,6},{4,0},{6,2},{8,12},{10,14},{12,8},{14,10},{1,5},{3,7},... | collective-permute-start | bytes 215048 | tf_op jit(solution)/shard_map/ppermute | solution.py:55
  36.4 4.8 %collective-permute-start.7 = (bf16[280,128]{1,0:T(8,128)(2,1)S(1)}, bf16[280,128]{1,0:T(8,128)(2,1)S(1)}, u32[]{:S(2)}, u32[]{:S(2)}) collective-permute-start(bf16[280,128]{1,0:T(8,128)(2,1)S(1)} %get-tuple-element.106), channel_id=1, source_target_pairs={{0,2},{2,0},{4,6},{6,4},{8,10},{10,8},{12,14},{14,12},{1,3},{3,1},... | collective-permute-start | bytes 215048 | tf_op jit(solution)/shard_map/ppermute | solution.py:55
  41.4 6.1 %collective-permute-start.11 = (bf16[280,128]{1,0:T(8,128)(2,1)S(1)}, bf16[280,128]{1,0:T(8,128)(2,1)S(1)}, u32[]{:S(2)}, u32[]{:S(2)}) collective-permute-start(bf16[280,128]{1,0:T(8,128)(2,1)S(1)} %pad_maximum_fusion.2.refs_0_), channel_id=1, source_target_pairs={{0,8},{2,10},{4,12},{6,14},{8,0},{10,2},{12,4},{14,6},{1,9},{3,11}... | collective-permute-start | bytes 215048 | tf_op jit(solution)/shard_map/ppermute | solution.py:55
